TPU v7x, 32 devices: a whole 2x2x4 slice. The times are simulated.
32 devices in a mesh: seq: 8 (over z, y), dp: 4 (over x, core).
Axes of the slice: x: 2, y: 2, z: 4, core: 2. Of those that a mesh axis runs over, the one named last changes fastest.
Arguments:
- src: bfloat16 [4, 1024, 768], P('dp', 'seq'), may hold values from -6 to 6
- tgt: bfloat16 [4, 1024, 768], P('dp', 'seq'), may hold values from -6 to 6
- src_seg: int32 [4, 1024], P('dp', 'seq'), may hold values from 0 to 2, never falling along the last dimension, each value on 1 to 682 neighbouring positions
- tgt_seg: int32 [4, 1024], P('dp', 'seq'), may hold values from 0 to 2, never falling along the last dimension, each value on 1 to 682 neighbouring positions
- enc_qkv: bfloat16 [3, 768, 768], P(None, ('seq', 'dp')), may hold values from -0.21875 to 0.21875
- enc_out_w: bfloat16 [768, 768], P(('seq', 'dp')), may hold values from -1.5 to 1.5
- enc_attn_bias: bfloat16 [3, 768], P(None, ('seq', 'dp')), may hold values from -1 to 1
- enc_up: bfloat16 [768, 3072], P(('seq', 'dp')), may hold values from -0.21875 to 0.21875
- enc_up_bias: bfloat16 [3072], P(('seq', 'dp')), may hold values from -1 to 1
- enc_down: bfloat16 [3072, 768], P(('seq', 'dp')), may hold values from -0.109375 to 0.109375
- enc_down_bias: bfloat16 [768], P(('seq', 'dp')), may hold values from -1 to 1
- enc_gains: bfloat16 [2, 768], P(None, ('seq', 'dp')), may hold values from 0.5 to 1.5
- enc_shifts: bfloat16 [2, 768], P(None, ('seq', 'dp')), may hold values from -1 to 1
- dec_self_qkv: bfloat16 [3, 768, 768], P(None, ('seq', 'dp')), may hold values from -0.21875 to 0.21875
- dec_self_out: bfloat16 [768, 768], P(('seq', 'dp')), may hold values from -1.5 to 1.5
- dec_self_bias: bfloat16 [3, 768], P(None, ('seq', 'dp')), may hold values from -1 to 1
- dec_cross_qkv: bfloat16 [3, 768, 768], P(None, ('seq', 'dp')), may hold values from -0.21875 to 0.21875
- dec_cross_out: bfloat16 [768, 768], P(('seq', 'dp')), may hold values from -1.5 to 1.5
- dec_cross_bias: bfloat16 [3, 768], P(None, ('seq', 'dp')), may hold values from -1 to 1
- dec_up: bfloat16 [768, 3072], P(('seq', 'dp')), may hold values from -0.21875 to 0.21875
- dec_up_bias: bfloat16 [3072], P(('seq', 'dp')), may hold values from -1 to 1
- dec_down: bfloat16 [3072, 768], P(('seq', 'dp')), may hold values from -0.109375 to 0.109375
- dec_down_bias: bfloat16 [768], P(('seq', 'dp')), may hold values from -1 to 1
- dec_gains: bfloat16 [3, 768], P(None, ('seq', 'dp')), may hold values from 0.5 to 1.5
- dec_shifts: bfloat16 [3, 768], P(None, ('seq', 'dp')), may hold values from -1 to 1
- out_grad: bfloat16 [4, 1024, 768], P('dp', 'seq'), may hold values from -6 to 6
Outputs:
- dec_out: bfloat16 [4, 1024, 768], P('dp', 'seq')
- src_grad: float32 [4, 1024, 768], P('dp', 'seq')
- tgt_grad: float32 [4, 1024, 768], P('dp', 'seq')
- g_enc_qkv: float32 [3, 768, 768], P(None, ('seq', 'dp'))
- g_enc_out_w: float32 [768, 768], P(('seq', 'dp'))
- g_enc_attn_bias: float32 [3, 768], P(None, ('seq', 'dp'))
- g_enc_up: float32 [768, 3072], P(('seq', 'dp'))
- g_enc_up_bias: float32 [3072], P(('seq', 'dp'))
- g_enc_down: float32 [3072, 768], P(('seq', 'dp'))
- g_enc_down_bias: float32 [768], P(('seq', 'dp'))
- g_enc_gains: float32 [2, 768], P(None, ('seq', 'dp'))
- g_enc_shifts: float32 [2, 768], P(None, ('seq', 'dp'))
- g_dec_self_qkv: float32 [3, 768, 768], P(None, ('seq', 'dp'))
- g_dec_self_out: float32 [768, 768], P(('seq', 'dp'))
- g_dec_self_bias: float32 [3, 768], P(None, ('seq', 'dp'))
- g_dec_cross_qkv: float32 [3, 768, 768], P(None, ('seq', 'dp'))
- g_dec_cross_out: float32 [768, 768], P(('seq', 'dp'))
- g_dec_cross_bias: float32 [3, 768], P(None, ('seq', 'dp'))
- g_dec_up: float32 [768, 3072], P(('seq', 'dp'))
- g_dec_up_bias: float32 [3072], P(('seq', 'dp'))
- g_dec_down: float32 [3072, 768], P(('seq', 'dp'))
- g_dec_down_bias: float32 [768], P(('seq', 'dp'))
- g_dec_gains: float32 [3, 768], P(None, ('seq', 'dp'))
- g_dec_shifts: float32 [3, 768], P(None, ('seq', 'dp'))
Inputs may be any that keep to these rules, and one draw needn't show every extreme that they name: `src_seg`: in every row the ids never fall along the row, all 3 ids occur, no document has more than 682 tokens and one has exactly 682. `tgt_seg`: in every row the ids never fall along the row, all 3 ids occur, no document has more than 682 tokens and one has exactly 682.
All inputs are finite; a program needn't handle non-finite values.
Results may differ from a plain program's by a relative error of at most 0.024.
Values may be sent and summed in bfloat16 or wider, within the bound.
No kernel may reach another device: no remote copies, remote signals or barrier semaphores. Data moves between devices by JAX's collectives and lax.ppermute only.
A program may use at most 256 MiB of HBM per device.

v0:
```python
import jax
import jax.numpy as jnp
from jax import lax
from jax.sharding import PartitionSpec as P

HEADS = 12


EPSILON = 1e-05
MASKED = -1e30
CONTRACT_ROWS = (((0,), (0,)), ((), ()))
CONTRACT_COLS = (((1,), (1,)), ((), ()))


def matmul(left, right):
    return jnp.dot(left, right, preferred_element_type=jnp.float32)


def outer_sum(left, right):
    return lax.dot_general(left, right, CONTRACT_ROWS, preferred_element_type=jnp.float32)


def back_matmul(left, right):
    return lax.dot_general(left, right, CONTRACT_COLS, preferred_element_type=jnp.float32)


def layer_norm(resid, gain, shift):
    center = resid - jnp.mean(resid, axis=-1, keepdims=True)
    second = jnp.mean(center * center, axis=-1, keepdims=True)
    return center * lax.rsqrt(second + EPSILON) * gain + shift


def norm_back(resid, gain, shift, grad_out):
    pullback = jax.vjp(layer_norm, resid, gain, shift)[1]
    return pullback(grad_out)


def gelu_exact(values):
    return jax.nn.gelu(values, approximate=False)


def to_heads(values):
    return values.reshape(values.shape[0], HEADS, -1)


def attend(queries, keys_in, values, query_seg, key_seg, causal):
    row_count, model_width = queries.shape
    scaling = (model_width // HEADS) ** (-0.5)
    query_heads = to_heads(queries)
    query_place = lax.axis_index("seq") * row_count + jnp.arange(row_count, dtype=jnp.int32)

    def block_scores(key_block, seg_block):
        key_place = jnp.arange(key_block.shape[0], dtype=jnp.int32)
        scores = (
            jnp.einsum(
                "qhd,khd->hqk", query_heads, to_heads(key_block), preferred_element_type=jnp.float32
            )
            * scaling
        )
        allowed = query_seg[:, None] == seg_block[None, :]
        if causal:
            allowed = allowed & (key_place[None, :] <= query_place[:, None])
        return (jnp.where(allowed[None], scores, MASKED), allowed)

    row_peak = jnp.full((HEADS, row_count), MASKED, jnp.float32)
    key_block = lax.all_gather(keys_in, "seq", axis=0, tiled=True)
    seg_block = lax.all_gather(key_seg, "seq", axis=0, tiled=True)
    scores, allowed = block_scores(key_block, seg_block)
    new_peak = jnp.maximum(row_peak, jnp.max(scores, axis=2))
    weights = jnp.where(allowed[None], jnp.exp(scores - new_peak[:, :, None]), 0.0)
    row_totals = jnp.sum(weights, axis=2)
    row_peak, row_totals = (new_peak, row_totals)
    log_heads = row_peak + jnp.log(row_totals)
    key_block = lax.all_gather(keys_in, "seq", axis=0, tiled=True)
    value_block = lax.all_gather(values, "seq", axis=0, tiled=True)
    seg_block = lax.all_gather(key_seg, "seq", axis=0, tiled=True)
    scores, allowed = block_scores(key_block, seg_block)
    probs = jnp.where(allowed[None], jnp.exp(scores - log_heads[:, :, None]), 0.0)
    accumulated = jnp.einsum(
        "hqk,khd->qhd",
        probs.astype(jnp.bfloat16),
        to_heads(value_block),
        preferred_element_type=jnp.float32,
    )
    return (accumulated.reshape(row_count, model_width), log_heads.T)


def block_grads(
    query_heads,
    grad_heads,
    log_block,
    delta_block,
    query_seg,
    query_place,
    key_heads,
    value_heads,
    key_seg,
    key_place,
    causal,
    scaling,
):
    scores = (
        jnp.einsum("qhd,khd->hqk", query_heads, key_heads, preferred_element_type=jnp.float32)
        * scaling
    )
    allowed = query_seg[:, None] == key_seg[None, :]
    if causal:
        allowed = allowed & (key_place[None, :] <= query_place[:, None])
    probs = jnp.where(allowed[None], jnp.exp(scores - log_block.T[:, :, None]), 0.0)
    grad_probs = jnp.einsum(
        "qhd,khd->hqk", grad_heads, value_heads, preferred_element_type=jnp.float32
    )
    grad_scores = (probs * (grad_probs - delta_block.T[:, :, None])).astype(jnp.bfloat16)
    grad_values = jnp.einsum(
        "hqk,qhd->khd", probs.astype(jnp.bfloat16), grad_heads, preferred_element_type=jnp.float32
    )
    grad_keys = (
        jnp.einsum("hqk,qhd->khd", grad_scores, query_heads, preferred_element_type=jnp.float32)
        * scaling
    )
    grad_queries = (
        jnp.einsum("hqk,khd->qhd", grad_scores, key_heads, preferred_element_type=jnp.float32)
        * scaling
    )
    return (grad_queries, grad_keys, grad_values)


def own_keys_pass(
    keys_in, values, key_seg, own_place, all_queries, all_grads, all_log, all_delta, all_seg, causal
):
    row_count, model_width = keys_in.shape
    head_size = model_width // HEADS
    scaling = head_size ** (-0.5)
    length = all_queries.shape[0]
    block_rows = min(length, 512)
    block_count = length // block_rows
    key_heads = to_heads(keys_in)
    value_heads = to_heads(values)

    def visit_queries(grad_acc, block_in):
        query_block, grad_block, log_block, delta_block, seg_block, place_block = block_in
        grad_query, grad_key, grad_value = block_grads(
            query_block,
            grad_block,
            log_block,
            delta_block,
            seg_block,
            place_block,
            key_heads,
            value_heads,
            key_seg,
            own_place,
            causal,
            scaling,
        )
        return ((grad_acc[0] + grad_key, grad_acc[1] + grad_value), grad_query)

    start_grad = (
        jnp.zeros((row_count, HEADS, head_size), jnp.float32),
        jnp.zeros((row_count, HEADS, head_size), jnp.float32),
    )
    key_totals, query_terms = lax.scan(
        visit_queries,
        start_grad,
        (
            all_queries.reshape(block_count, block_rows, HEADS, head_size),
            all_grads.reshape(block_count, block_rows, HEADS, head_size),
            all_log.reshape(block_count, block_rows, HEADS),
            all_delta.reshape(block_count, block_rows, HEADS),
            all_seg.reshape(block_count, block_rows),
            jnp.arange(length, dtype=jnp.int32).reshape(block_count, block_rows),
        ),
    )
    return (
        query_terms.reshape(length, model_width),
        key_totals[0].reshape(row_count, model_width),
        key_totals[1].reshape(row_count, model_width),
    )


def attend_back(queries, keys_in, values, grad_mix, mixture, log_total, query_seg, key_seg, causal):
    row_count, model_width = queries.shape
    own_place = lax.axis_index("seq") * row_count + jnp.arange(row_count, dtype=jnp.int32)
    delta = jnp.sum(to_heads(grad_mix.astype(jnp.float32)) * to_heads(mixture), axis=2)
    all_queries, all_grads = (
        lax.all_gather(queries, "seq", axis=0, tiled=True),
        lax.all_gather(grad_mix, "seq", axis=0, tiled=True),
    )
    all_log, all_delta, all_seg = (
        lax.all_gather(log_total, "seq", axis=0, tiled=True),
        lax.all_gather(delta, "seq", axis=0, tiled=True),
        lax.all_gather(query_seg, "seq", axis=0, tiled=True),
    )
    query_terms, grad_keys, grad_values = own_keys_pass(
        keys_in,
        values,
        key_seg,
        own_place,
        all_queries,
        all_grads,
        all_log,
        all_delta,
        all_seg,
        causal,
    )
    grad_queries = lax.psum_scatter(
        query_terms.astype(jnp.bfloat16), "seq", scatter_dimension=0, tiled=True
    ).astype(jnp.float32)
    return (grad_queries, grad_keys, grad_values)


def attention_forward(query_in, key_in, qkv, out_weight, biases, query_seg, key_seg, causal):
    bias_values = biases.astype(jnp.float32)
    queries = (matmul(query_in, qkv[0]) + bias_values[0]).astype(jnp.bfloat16)
    keys_out = matmul(key_in, qkv[1]).astype(jnp.bfloat16)
    values = (matmul(key_in, qkv[2]) + bias_values[1]).astype(jnp.bfloat16)
    mixture, log_total = attend(queries, keys_out, values, query_seg, key_seg, causal)
    mixture_low = mixture.astype(jnp.bfloat16)
    branch = matmul(mixture_low, out_weight) + bias_values[2]
    return (branch, (queries, keys_out, values, mixture, mixture_low, log_total))


def attention_backward(
    grad_branch, query_in, key_in, qkv, out_weight, saved, query_seg, key_seg, causal
):
    queries, keys_out, values, mixture, mixture_low, log_total = saved
    grad_low = grad_branch.astype(jnp.bfloat16)
    grad_out_weight = outer_sum(mixture_low, grad_low)
    grad_out_bias = jnp.sum(grad_low.astype(jnp.float32), axis=0)
    grad_mix = back_matmul(grad_low, out_weight).astype(jnp.bfloat16)
    grad_query, grad_key, grad_value = attend_back(
        queries, keys_out, values, grad_mix, mixture, log_total, query_seg, key_seg, causal
    )
    grad_query = grad_query.astype(jnp.bfloat16)
    grad_key = grad_key.astype(jnp.bfloat16)
    grad_value = grad_value.astype(jnp.bfloat16)
    grad_qkv = jnp.stack(
        [
            outer_sum(query_in, grad_query),
            outer_sum(key_in, grad_key),
            outer_sum(key_in, grad_value),
        ]
    )
    grad_bias = jnp.stack(
        [
            jnp.sum(grad_query.astype(jnp.float32), axis=0),
            jnp.sum(grad_value.astype(jnp.float32), axis=0),
            grad_out_bias,
        ]
    )
    grad_query_in = back_matmul(grad_query, qkv[0])
    grad_key_in = back_matmul(grad_key, qkv[1]) + back_matmul(grad_value, qkv[2])
    return (grad_query_in, grad_key_in, grad_qkv, grad_bias, grad_out_weight)


def ffn_forward(rows_low, up_weight, up_bias, down_weight, down_bias):
    pre_act = matmul(rows_low, up_weight) + up_bias.astype(jnp.float32)
    hidden = gelu_exact(pre_act).astype(jnp.bfloat16)
    return (matmul(hidden, down_weight) + down_bias.astype(jnp.float32), (pre_act, hidden))


def ffn_backward(grad_out, rows_low, up_weight, down_weight, saved):
    pre_act, hidden = saved
    grad_low = grad_out.astype(jnp.bfloat16)
    grad_down = outer_sum(hidden, grad_low)
    grad_down_bias = jnp.sum(grad_low.astype(jnp.float32), axis=0)
    grad_hidden = back_matmul(grad_low, down_weight)
    grad_pre = jax.vjp(gelu_exact, pre_act)[1](grad_hidden)[0].astype(jnp.bfloat16)
    grad_up = outer_sum(rows_low, grad_pre)
    grad_up_bias = jnp.sum(grad_pre.astype(jnp.float32), axis=0)
    grad_rows = back_matmul(grad_pre, up_weight)
    return (grad_rows, grad_up, grad_up_bias, grad_down, grad_down_bias)


def one_row(encoder, decoder, source, target, source_seg, target_seg, cotangent):
    enc_gain = encoder[7].astype(jnp.float32)
    enc_shift = encoder[8].astype(jnp.float32)
    dec_gain = decoder[10].astype(jnp.float32)
    dec_shift = decoder[11].astype(jnp.float32)
    enc_branch, enc_attn_saved = attention_forward(
        source, source, encoder[0], encoder[1], encoder[2], source_seg, source_seg, False
    )
    enc_resid_one = source.astype(jnp.float32) + enc_branch
    enc_first = layer_norm(enc_resid_one, enc_gain[0], enc_shift[0])
    enc_first_low = enc_first.astype(jnp.bfloat16)
    enc_ffn_out, enc_ffn_saved = ffn_forward(
        enc_first_low, encoder[3], encoder[4], encoder[5], encoder[6]
    )
    enc_resid_two = enc_first + enc_ffn_out
    encoded = layer_norm(enc_resid_two, enc_gain[1], enc_shift[1])
    encoded_low = encoded.astype(jnp.bfloat16)
    self_branch, self_saved = attention_forward(
        target, target, decoder[0], decoder[1], decoder[2], target_seg, target_seg, True
    )
    dec_resid_one = target.astype(jnp.float32) + self_branch
    dec_first = layer_norm(dec_resid_one, dec_gain[0], dec_shift[0])
    dec_first_low = dec_first.astype(jnp.bfloat16)
    cross_branch, cross_saved = attention_forward(
        dec_first_low,
        encoded_low,
        decoder[3],
        decoder[4],
        decoder[5],
        target_seg,
        source_seg,
        False,
    )
    dec_resid_two = dec_first + cross_branch
    dec_second = layer_norm(dec_resid_two, dec_gain[1], dec_shift[1])
    dec_second_low = dec_second.astype(jnp.bfloat16)
    dec_ffn_out, dec_ffn_saved = ffn_forward(
        dec_second_low, decoder[6], decoder[7], decoder[8], decoder[9]
    )
    dec_resid_three = dec_second + dec_ffn_out
    dec_third = layer_norm(dec_resid_three, dec_gain[2], dec_shift[2])
    grad_resid_three, grad_gain_three, grad_shift_three = norm_back(
        dec_resid_three, dec_gain[2], dec_shift[2], cotangent.astype(jnp.float32)
    )
    dec_ffn_rows, grad_dec_up, grad_dec_up_bias, grad_dec_down, grad_dec_down_bias = ffn_backward(
        grad_resid_three, dec_second_low, decoder[6], decoder[8], dec_ffn_saved
    )
    grad_resid_two, grad_gain_two, grad_shift_two = norm_back(
        dec_resid_two, dec_gain[1], dec_shift[1], grad_resid_three + dec_ffn_rows
    )
    cross_query_in, cross_key_in, grad_cross_qkv, grad_cross_bias, grad_cross_out = (
        attention_backward(
            grad_resid_two,
            dec_first_low,
            encoded_low,
            decoder[3],
            decoder[4],
            cross_saved,
            target_seg,
            source_seg,
            False,
        )
    )
    grad_resid_one, grad_gain_one, grad_shift_one = norm_back(
        dec_resid_one, dec_gain[0], dec_shift[0], grad_resid_two + cross_query_in
    )
    self_query_in, self_key_in, grad_self_qkv, grad_self_bias, grad_self_out = attention_backward(
        grad_resid_one,
        target,
        target,
        decoder[0],
        decoder[1],
        self_saved,
        target_seg,
        target_seg,
        True,
    )
    target_grad = grad_resid_one + self_query_in + self_key_in
    dec_grads = (
        grad_self_qkv,
        grad_self_out,
        grad_self_bias,
        grad_cross_qkv,
        grad_cross_out,
        grad_cross_bias,
        grad_dec_up,
        grad_dec_up_bias,
        grad_dec_down,
        grad_dec_down_bias,
        jnp.stack([grad_gain_one, grad_gain_two, grad_gain_three]),
        jnp.stack([grad_shift_one, grad_shift_two, grad_shift_three]),
    )
    grad_enc_two, grad_enc_gain_two, grad_enc_shift_two = norm_back(
        enc_resid_two, enc_gain[1], enc_shift[1], cross_key_in
    )
    enc_ffn_rows, grad_enc_up, grad_enc_up_bias, grad_enc_down, grad_enc_down_bias = ffn_backward(
        grad_enc_two, enc_first_low, encoder[3], encoder[5], enc_ffn_saved
    )
    grad_enc_one, grad_enc_gain_one, grad_enc_shift_one = norm_back(
        enc_resid_one, enc_gain[0], enc_shift[0], grad_enc_two + enc_ffn_rows
    )
    enc_query_in, enc_key_in, grad_enc_qkv, grad_enc_bias, grad_enc_out = attention_backward(
        grad_enc_one,
        source,
        source,
        encoder[0],
        encoder[1],
        enc_attn_saved,
        source_seg,
        source_seg,
        False,
    )
    source_grad = grad_enc_one + enc_query_in + enc_key_in
    enc_grads = (
        grad_enc_qkv,
        grad_enc_out,
        grad_enc_bias,
        grad_enc_up,
        grad_enc_up_bias,
        grad_enc_down,
        grad_enc_down_bias,
        jnp.stack([grad_enc_gain_one, grad_enc_gain_two]),
        jnp.stack([grad_enc_shift_one, grad_enc_shift_two]),
    )
    return (dec_third.astype(jnp.bfloat16), source_grad, target_grad, enc_grads, dec_grads)


def on_device(
    src,
    tgt,
    src_seg,
    tgt_seg,
    enc_qkv,
    enc_out_w,
    enc_attn_bias,
    enc_up,
    enc_up_bias,
    enc_down,
    enc_down_bias,
    enc_gains,
    enc_shifts,
    dec_self_qkv,
    dec_self_out,
    dec_self_bias,
    dec_cross_qkv,
    dec_cross_out,
    dec_cross_bias,
    dec_up,
    dec_up_bias,
    dec_down,
    dec_down_bias,
    dec_gains,
    dec_shifts,
    out_grad,
):
    encoder = (
        lax.all_gather(enc_qkv, ("seq", "dp"), axis=1, tiled=True),
        lax.all_gather(enc_out_w, ("seq", "dp"), axis=0, tiled=True),
        lax.all_gather(enc_attn_bias, ("seq", "dp"), axis=1, tiled=True),
        lax.all_gather(enc_up, ("seq", "dp"), axis=0, tiled=True),
        lax.all_gather(enc_up_bias, ("seq", "dp"), axis=0, tiled=True),
        lax.all_gather(enc_down, ("seq", "dp"), axis=0, tiled=True),
        lax.all_gather(enc_down_bias, ("seq", "dp"), axis=0, tiled=True),
        lax.all_gather(enc_gains, ("seq", "dp"), axis=1, tiled=True),
        lax.all_gather(enc_shifts, ("seq", "dp"), axis=1, tiled=True),
    )
    decoder = (
        lax.all_gather(dec_self_qkv, ("seq", "dp"), axis=1, tiled=True),
        lax.all_gather(dec_self_out, ("seq", "dp"), axis=0, tiled=True),
        lax.all_gather(dec_self_bias, ("seq", "dp"), axis=1, tiled=True),
        lax.all_gather(dec_cross_qkv, ("seq", "dp"), axis=1, tiled=True),
        lax.all_gather(dec_cross_out, ("seq", "dp"), axis=0, tiled=True),
        lax.all_gather(dec_cross_bias, ("seq", "dp"), axis=1, tiled=True),
        lax.all_gather(dec_up, ("seq", "dp"), axis=0, tiled=True),
        lax.all_gather(dec_up_bias, ("seq", "dp"), axis=0, tiled=True),
        lax.all_gather(dec_down, ("seq", "dp"), axis=0, tiled=True),
        lax.all_gather(dec_down_bias, ("seq", "dp"), axis=0, tiled=True),
        lax.all_gather(dec_gains, ("seq", "dp"), axis=1, tiled=True),
        lax.all_gather(dec_shifts, ("seq", "dp"), axis=1, tiled=True),
    )
    decoded, source_grad, target_grad, enc_grads, dec_grads = one_row(
        encoder, decoder, src[0], tgt[0], src_seg[0], tgt_seg[0], out_grad[0]
    )
    decoded_rows = [decoded]
    source_rows = [source_grad]
    target_rows = [target_grad]
    (
        sum_self_qkv,
        sum_self_out,
        sum_self_bias,
        sum_cross_qkv,
        sum_cross_out,
        sum_cross_bias,
        sum_dec_up,
        sum_dec_up_bias,
        sum_dec_down,
        sum_dec_down_bias,
        sum_dec_gains,
        sum_dec_shifts,
    ) = dec_grads
    (
        sum_enc_qkv,
        sum_enc_out,
        sum_enc_bias,
        sum_enc_up,
        sum_enc_up_bias,
        sum_enc_down,
        sum_enc_down_bias,
        sum_enc_gains,
        sum_enc_shifts,
    ) = enc_grads
    dec_summed = (
        lax.psum_scatter(sum_self_qkv, ("seq", "dp"), scatter_dimension=1, tiled=True),
        lax.psum_scatter(sum_self_out, ("seq", "dp"), scatter_dimension=0, tiled=True),
        lax.psum_scatter(sum_self_bias, ("seq", "dp"), scatter_dimension=1, tiled=True),
        lax.psum_scatter(sum_cross_qkv, ("seq", "dp"), scatter_dimension=1, tiled=True),
        lax.psum_scatter(sum_cross_out, ("seq", "dp"), scatter_dimension=0, tiled=True),
        lax.psum_scatter(sum_cross_bias, ("seq", "dp"), scatter_dimension=1, tiled=True),
        lax.psum_scatter(sum_dec_up, ("seq", "dp"), scatter_dimension=0, tiled=True),
        lax.psum_scatter(sum_dec_up_bias, ("seq", "dp"), scatter_dimension=0, tiled=True),
        lax.psum_scatter(sum_dec_down, ("seq", "dp"), scatter_dimension=0, tiled=True),
        lax.psum_scatter(sum_dec_down_bias, ("seq", "dp"), scatter_dimension=0, tiled=True),
        lax.psum_scatter(sum_dec_gains, ("seq", "dp"), scatter_dimension=1, tiled=True),
        lax.psum_scatter(sum_dec_shifts, ("seq", "dp"), scatter_dimension=1, tiled=True),
    )
    enc_summed = (
        lax.psum_scatter(sum_enc_qkv, ("seq", "dp"), scatter_dimension=1, tiled=True),
        lax.psum_scatter(sum_enc_out, ("seq", "dp"), scatter_dimension=0, tiled=True),
        lax.psum_scatter(sum_enc_bias, ("seq", "dp"), scatter_dimension=1, tiled=True),
        lax.psum_scatter(sum_enc_up, ("seq", "dp"), scatter_dimension=0, tiled=True),
        lax.psum_scatter(sum_enc_up_bias, ("seq", "dp"), scatter_dimension=0, tiled=True),
        lax.psum_scatter(sum_enc_down, ("seq", "dp"), scatter_dimension=0, tiled=True),
        lax.psum_scatter(sum_enc_down_bias, ("seq", "dp"), scatter_dimension=0, tiled=True),
        lax.psum_scatter(sum_enc_gains, ("seq", "dp"), scatter_dimension=1, tiled=True),
        lax.psum_scatter(sum_enc_shifts, ("seq", "dp"), scatter_dimension=1, tiled=True),
    )
    heads_out = (jnp.stack(decoded_rows), jnp.stack(source_rows), jnp.stack(target_rows))
    return heads_out + tuple(enc_summed) + tuple(dec_summed)


def solution(mesh):
    in_specs = (
        P("dp", "seq", None),
        P("dp", "seq", None),
        P("dp", "seq"),
        P("dp", "seq"),
        P(None, ("seq", "dp"), None),
        P(("seq", "dp"), None),
        P(None, ("seq", "dp")),
        P(("seq", "dp"), None),
        P(("seq", "dp")),
        P(("seq", "dp"), None),
        P(("seq", "dp")),
        P(None, ("seq", "dp")),
        P(None, ("seq", "dp")),
        P(None, ("seq", "dp"), None),
        P(("seq", "dp"), None),
        P(None, ("seq", "dp")),
        P(None, ("seq", "dp"), None),
        P(("seq", "dp"), None),
        P(None, ("seq", "dp")),
        P(("seq", "dp"), None),
        P(("seq", "dp")),
        P(("seq", "dp"), None),
        P(("seq", "dp")),
        P(None, ("seq", "dp")),
        P(None, ("seq", "dp")),
        P("dp", "seq", None),
    )
    out_specs = (
        P("dp", "seq", None),
        P("dp", "seq", None),
        P("dp", "seq", None),
        P(None, ("seq", "dp"), None),
        P(("seq", "dp"), None),
        P(None, ("seq", "dp")),
        P(("seq", "dp"), None),
        P(("seq", "dp")),
        P(("seq", "dp"), None),
        P(("seq", "dp")),
        P(None, ("seq", "dp")),
        P(None, ("seq", "dp")),
        P(None, ("seq", "dp"), None),
        P(("seq", "dp"), None),
        P(None, ("seq", "dp")),
        P(None, ("seq", "dp"), None),
        P(("seq", "dp"), None),
        P(None, ("seq", "dp")),
        P(("seq", "dp"), None),
        P(("seq", "dp")),
        P(("seq", "dp"), None),
        P(("seq", "dp")),
        P(None, ("seq", "dp")),
        P(None, ("seq", "dp")),
    )
    return jax.shard_map(
        on_device, mesh=mesh, in_specs=in_specs, out_specs=out_specs, check_vma=False
    )
```

profile of v0, /device:TPU:0, one launch (start us, length us, event | category | flops | bytes accessed | tf_op | source)
XLA Modules:
  0.0 2837.8 jit_solution(9371413524168133600)
XLA Ops:
  8.7 65.1 %all-gather.40.cloned.1.call-done = bf16[3,768,768]{2,1,0:T(8,128)(2,1)} async-done(((bf16[3,24,768]{2,1,0:T(8,128)(2,1)}), bf16[3,768,768]{2,1,0:T(8,128)(2,1)}) %all-gather.40.cloned.1.call-update) | async-done | bytes 3538960 | tf_op jit(solution)/shard_map/all_gather | solution.py:431
  76.4 39.4 %all-gather.5 = bf16[32,24,3]{1,2,0:T(4,128)(2,1)S(1)} all-gather(bf16[1,24,3]{1,2,0:T(4,128)(2,1)S(1)} %bitcast.620), channel_id=1, replica_groups=mesh['seq'=8,'dp'=4] {'seq','dp'}, dimensions={0}, use_global_device_ids=true | all-gather | bytes 4752 | tf_op jit(solution)/shard_map/all_gather | solution.py:433
  138.2 39.4 %all-gather.2 = bf16[32,24,3]{1,2,0:T(4,128)(2,1)S(1)} all-gather(bf16[1,24,3]{1,2,0:T(4,128)(2,1)S(1)} %bitcast.621), channel_id=1, replica_groups=mesh['seq'=8,'dp'=4] {'seq','dp'}, dimensions={0}, use_global_device_ids=true | all-gather | bytes 4752 | tf_op jit(solution)/shard_map/all_gather | solution.py:444
  254.4 39.6 %all-gather.6 = bf16[32,24,2]{1,2,0:T(2,128)(2,1)S(1)} all-gather(bf16[1,24,2]{1,2,0:T(2,128)(2,1)S(1)} %bitcast.625), channel_id=1, replica_groups=mesh['seq'=8,'dp'=4] {'seq','dp'}, dimensions={0}, use_global_device_ids=true | all-gather | bytes 3168 | tf_op jit(solution)/shard_map/all_gather | solution.py:438
  358.6 55.3 %all-gather.50.cloned.1.call-done = bf16[3072,768]{1,0:T(8,128)(2,1)} async-done(((bf16[96,768]{1,0:T(8,128)(2,1)}), bf16[3072,768]{1,0:T(8,128)(2,1)}) %all-gather.50.cloned.1.call-update) | async-done | bytes 4718608 | tf_op jit(solution)/shard_map/all_gather | solution.py:436
  418.1 57.8 %all-gather.52.cloned.1.call-done = bf16[3,768,768]{2,1,0:T(8,128)(2,1)} async-done(((bf16[3,24,768]{2,1,0:T(8,128)(2,1)}), bf16[3,768,768]{2,1,0:T(8,128)(2,1)}) %all-gather.52.cloned.1.call-update) | async-done | bytes 3538960 | tf_op jit(solution)/shard_map/all_gather | solution.py:445
  478.2 39.4 %all-gather.8 = bf16[32,24,3]{1,2,0:T(4,128)(2,1)S(1)} all-gather(bf16[1,24,3]{1,2,0:T(4,128)(2,1)S(1)} %bitcast.622), channel_id=1, replica_groups=mesh['seq'=8,'dp'=4] {'seq','dp'}, dimensions={0}, use_global_device_ids=true | all-gather | bytes 4752 | tf_op jit(solution)/shard_map/all_gather | solution.py:447
  559.7 50.7 %all-gather.4 = bf16[32,24,3]{1,2,0:T(4,128)(2,1)S(1)} all-gather(bf16[1,24,3]{1,2,0:T(4,128)(2,1)S(1)} %bitcast.624), channel_id=1, replica_groups=mesh['seq'=8,'dp'=4] {'seq','dp'}, dimensions={0}, use_global_device_ids=true | all-gather | bytes 4752 | tf_op jit(solution)/shard_map/all_gather | solution.py:453
  629.7 39.2 %all-gather.56.cloned.1.call-done = bf16[1024,768]{1,0:T(8,128)(2,1)} async-done(((bf16[128,768]{1,0:T(8,128)(2,1)}), bf16[1024,768]{1,0:T(8,128)(2,1)}) %all-gather.56.cloned.1.call-update) | async-done | bytes 1572880 | tf_op jit(solution)/shard_map/all_gather | solution.py:74
  674.5 40.2 %all-gather.54.cloned.1.call-done = bf16[1024,768]{1,0:T(8,128)(2,1)} async-done(((bf16[128,768]{1,0:T(8,128)(2,1)}), bf16[1024,768]{1,0:T(8,128)(2,1)}) %all-gather.54.cloned.1.call-update) | async-done | bytes 1572880 | tf_op jit(solution)/shard_map/all_gather | solution.py:75
  720.4 50.0 %all-gather.58.cloned.1.call-done = bf16[768,768]{1,0:T(8,128)(2,1)} async-done(((bf16[24,768]{1,0:T(8,128)(2,1)}), bf16[768,768]{1,0:T(8,128)(2,1)}) %all-gather.58.cloned.1.call-update) | async-done | bytes 1179664 | tf_op jit(solution)/shard_map/all_gather | solution.py:446
  772.4 63.3 %all-gather.60.cloned.1.call-done = bf16[768,3072]{1,0:T(8,128)(2,1)} async-done(((bf16[24,3072]{1,0:T(8,128)(2,1)}), bf16[768,3072]{1,0:T(8,128)(2,1)}) %all-gather.60.cloned.1.call-update) | async-done | bytes 4718608 | tf_op jit(solution)/shard_map/all_gather | solution.py:448
  844.1 56.9 %all-gather.62.cloned.1.call-done = bf16[3072,768]{1,0:T(8,128)(2,1)} async-done(((bf16[96,768]{1,0:T(8,128)(2,1)}), bf16[3072,768]{1,0:T(8,128)(2,1)}) %all-gather.62.cloned.1.call-update) | async-done | bytes 4718608 | tf_op jit(solution)/shard_map/all_gather | solution.py:450
  1336.1 44.5 %reduce-scatter.45.cloned.1.call-done = bf16[128,768]{1,0:T(8,128)(2,1)} async-done(((bf16[1024,768]{1,0:T(8,128)(2,1)}), bf16[128,768]{1,0:T(8,128)(2,1)}) %reduce-scatter.45.cloned.1.call-update) | async-done | bytes 196624
  1447.6 66.7 %all-reduce.23.cloned.1.call-done = (f32[3,768]{1,0:T(4,128)}, f32[3072]{0:T(1024)}, f32[768]{0:T(1024)}, f32[2,768]{1,0:T(2,128)}, f32[2,768]{1,0:T(2,128)}, /*...) async-done(((f32[3,768]{1,0:T(4,128)}, f32[3072]{0:T(1024)}, f32[768]{0:T(1024)}, ...) | async-done | bytes 89104
  1528.7 297.0 %all-reduce.25.cloned.1.call-done = (f32[3,768,768]{2,0,1:T(4,128)}, f32[3,768,768]{2,0,1:T(4,128)}) async-done(((f32[3,768,768]{2,0,1:T(4,128)}, f32[3,768,768]{2,0,1:T(4,128)}), (f32[3,768,768]{2,0,1:T(4,128)}, f32[3,768,768]{2,0,1:T(4,128)})) %all-reduce.25.cloned.1.call-update) | async-done | bytes 14155792
  1829.2 101.4 %reduce-scatter.35.cloned.1.call-done = f32[24,768]{1,0:T(8,128)} async-done(((f32[768,768]{1,0:T(8,128)}), f32[24,768]{1,0:T(8,128)}) %reduce-scatter.35.cloned.1.call-update) | async-done | bytes 73744 | tf_op jit(solution)/shard_map/reduce_scatter | solution.py:491
  1930.6 104.7 %reduce-scatter.25.cloned.1.call-done = f32[24,768]{1,0:T(8,128)} async-done(((f32[768,768]{1,0:T(8,128)}), f32[24,768]{1,0:T(8,128)}) %reduce-scatter.25.cloned.1.call-update) | async-done | bytes 73744 | tf_op jit(solution)/shard_map/reduce_scatter | solution.py:502
  2035.3 103.8 %reduce-scatter.31.cloned.1.call-done = f32[24,768]{1,0:T(8,128)} async-done(((f32[768,768]{1,0:T(8,128)}), f32[24,768]{1,0:T(8,128)}) %reduce-scatter.31.cloned.1.call-update) | async-done | bytes 73744 | tf_op jit(solution)/shard_map/reduce_scatter | solution.py:488
  2139.1 142.0 %reduce-scatter.37.cloned.1.call-done = f32[24,3072]{1,0:T(8,128)} async-done(((f32[768,3072]{1,0:T(8,128)}), f32[24,3072]{1,0:T(8,128)}) %reduce-scatter.37.cloned.1.call-update) | async-done | bytes 294928 | tf_op jit(solution)/shard_map/reduce_scatter | solution.py:493
  2281.1 141.1 %reduce-scatter.39.cloned.1.call-done = f32[96,768]{1,0:T(8,128)} async-done(((f32[3072,768]{1,0:T(8,128)}), f32[96,768]{1,0:T(8,128)}) %reduce-scatter.39.cloned.1.call-update) | async-done | bytes 294928 | tf_op jit(solution)/shard_map/reduce_scatter | solution.py:495
  2422.2 125.4 %reduce-scatter.33.cloned.1.call-done = f32[3,24,768]{2,1,0:T(8,128)} async-done(((f32[3,768,768]{2,1,0:T(8,128)}), f32[3,24,768]{2,1,0:T(8,128)}) %reduce-scatter.33.cloned.1.call-update) | async-done | bytes 221200 | tf_op jit(solution)/shard_map/reduce_scatter | solution.py:490
  2547.6 141.3 %reduce-scatter.27.cloned.1.call-done = f32[24,3072]{1,0:T(8,128)} async-done(((f32[768,3072]{1,0:T(8,128)}), f32[24,3072]{1,0:T(8,128)}) %reduce-scatter.27.cloned.1.call-update) | async-done | bytes 294928 | tf_op jit(solution)/shard_map/reduce_scatter | solution.py:504
  2688.9 142.2 %reduce-scatter.29.cloned.1.call-done = f32[96,768]{1,0:T(8,128)} async-done(((f32[3072,768]{1,0:T(8,128)}), f32[96,768]{1,0:T(8,128)}) %reduce-scatter.29.cloned.1.call-update) | async-done | bytes 294928 | tf_op jit(solution)/shard_map/reduce_scatter | solution.py:506
  (882 shorter events, 842.8 us)
Async XLA Ops:
  8.7 326.7 %all-gather.44.cloned.1.call-start = ((), (), s32[]{:S(2)}) async-start(), calls=%async_computation.17 | async-start | bytes 1769472 | tf_op jit(solution)/shard_map/all_gather | solution.py:74
  76.3 264.8 %all-gather.42.cloned.1.call-start = ((), (), s32[]{:S(2)}) async-start(), calls=%async_computation.16 | async-start | bytes 1769472 | tf_op jit(solution)/shard_map/all_gather | solution.py:75
  119.5 294.4 %all-gather.50.cloned.1.call-start = ((), (), s32[]{:S(2)}) async-start(), calls=%async_computation.20 | async-start | bytes 4866048 | tf_op jit(solution)/shard_map/all_gather | solution.py:436
  120.3 355.6 %all-gather.52.cloned.1.call-start = ((), (), s32[]{:S(2)}) async-start(), calls=%async_computation.21 | async-start | bytes 3649536 | tf_op jit(solution)/shard_map/all_gather | solution.py:445
  121.0 493.9 %all-gather.36.cloned.1.call-start = ((), (), s32[]{:S(2)}) async-start(), calls=%async_computation.13 | async-start | bytes 1769472 | tf_op jit(solution)/shard_map/all_gather | solution.py:74
  138.2 478.5 %all-gather.34.cloned.1.call-start = ((), (), s32[]{:S(2)}) async-start(), calls=%async_computation.12 | async-start | bytes 1769472 | tf_op jit(solution)/shard_map/all_gather | solution.py:75
  180.9 444.3 %all-gather.38.cloned.1.call-start = ((), (), s32[]{:S(2)}) async-start(), calls=%async_computation.14 | async-start | bytes 1216512 | tf_op jit(solution)/shard_map/all_gather | solution.py:443
  181.6 487.3 %all-gather.56.cloned.1.call-start = ((), (), s32[]{:S(2)}) async-start(), calls=%async_computation.23 | async-start | bytes 1769472 | tf_op jit(solution)/shard_map/all_gather | solution.py:74
  478.2 236.5 %all-gather.54.cloned.1.call-start = ((), (), s32[]{:S(2)}) async-start(), calls=%async_computation.22 | async-start | bytes 1769472 | tf_op jit(solution)/shard_map/all_gather | solution.py:75
  520.9 249.5 %all-gather.58.cloned.1.call-start = ((), (), s32[]{:S(2)}) async-start(), calls=%async_computation.24 | async-start | bytes 1216512 | tf_op jit(solution)/shard_map/all_gather | solution.py:446
  521.5 314.2 %all-gather.60.cloned.1.call-start = ((), (), s32[]{:S(2)}) async-start(), calls=%async_computation.25 | async-start | bytes 4866048 | tf_op jit(solution)/shard_map/all_gather | solution.py:448
  522.0 378.9 %all-gather.62.cloned.1.call-start = ((), (), s32[]{:S(2)}) async-start(), calls=%async_computation.26 | async-start | bytes 4866048 | tf_op jit(solution)/shard_map/all_gather | solution.py:450
  522.6 459.1 %all-gather.64.cloned.1.call-start = ((), (), s32[]{:S(2)}) async-start(), calls=%async_computation.27 | async-start | bytes 1769472 | tf_op jit(solution)/shard_map/all_gather | solution.py:186
  629.7 362.0 %all-gather.66.cloned.1.call-start = ((), (), s32[]{:S(2)}) async-start(), calls=%async_computation.28 | async-start | bytes 1769472 | tf_op jit(solution)/shard_map/all_gather | solution.py:187
  917.6 242.5 %all-gather.70.cloned.1.call-start = ((), (), s32[]{:S(2)}) async-start(), calls=%async_computation.30 | async-start | bytes 1769472 | tf_op jit(solution)/shard_map/all_gather | solution.py:187
  1382.6 443.1 %all-reduce.25.cloned.1.call-start = ((), (), s32[]{:S(2)}) async-start(), calls=%async_computation.45 | async-start | bytes 37748736
  1399.2 531.4 %reduce-scatter.35.cloned.1.call-start = ((), (), s32[]{:S(2)}) async-start(), calls=%async_computation.38 | async-start | bytes 2433024 | tf_op jit(solution)/shard_map/reduce_scatter | solution.py:491
  1402.2 633.2 %reduce-scatter.25.cloned.1.call-start = ((), (), s32[]{:S(2)}) async-start(), calls=%async_computation.33 | async-start | bytes 2433024 | tf_op jit(solution)/shard_map/reduce_scatter | solution.py:502
  1405.1 734.0 %reduce-scatter.31.cloned.1.call-start = ((), (), s32[]{:S(2)}) async-start(), calls=%async_computation.36 | async-start | bytes 2433024 | tf_op jit(solution)/shard_map/reduce_scatter | solution.py:488
  1408.1 873.1 %reduce-scatter.37.cloned.1.call-start = ((), (), s32[]{:S(2)}) async-start(), calls=%async_computation.39 | async-start | bytes 9732096 | tf_op jit(solution)/shard_map/reduce_scatter | solution.py:493
  1414.5 1007.8 %reduce-scatter.39.cloned.1.call-start = ((), (), s32[]{:S(2)}) async-start(), calls=%async_computation.40 | async-start | bytes 9732096 | tf_op jit(solution)/shard_map/reduce_scatter | solution.py:495
  1420.6 1127.1 %reduce-scatter.33.cloned.1.call-start = ((), (), s32[]{:S(2)}) async-start(), calls=%async_computation.37 | async-start | bytes 7299072 | tf_op jit(solution)/shard_map/reduce_scatter | solution.py:490
  1427.0 1261.8 %reduce-scatter.27.cloned.1.call-start = ((), (), s32[]{:S(2)}) async-start(), calls=%async_computation.34 | async-start | bytes 9732096 | tf_op jit(solution)/shard_map/reduce_scatter | solution.py:504
  1433.3 1397.8 %reduce-scatter.29.cloned.1.call-start = ((), (), s32[]{:S(2)}) async-start(), calls=%async_computation.35 | async-start | bytes 9732096 | tf_op jit(solution)/shard_map/reduce_scatter | solution.py:506
  (235 other events, 6668.7 us)
Sparse Core Ops, SparseCore 0:
  11.0 62.8 all-gather.39
  76.8 58.9 all-gather.31
  230.0 53.1 all-gather.45
  286.0 62.4 all-gather.47
  351.4 62.4 all-gather.49
  416.9 58.9 all-gather.51
  570.3 52.8 all-gather.37
  717.5 52.8 all-gather.57
  773.1 62.5 all-gather.59
  838.5 62.4 all-gather.61
  1085.7 43.4 all-gather.69
  1132.6 63.6 reduce-scatter.42
  1249.9 63.4 reduce-scatter.40
  1316.8 63.8 reduce-scatter.44
  1388.1 126.2 all-reduce.22
  1520.6 305.0 all-reduce.24
  1831.5 99.0 reduce-scatter.34
  1937.3 97.9 reduce-scatter.24
  2041.0 97.9 reduce-scatter.30
  2146.6 134.4 reduce-scatter.36
  2287.6 134.5 reduce-scatter.38
  2429.3 118.2 reduce-scatter.32
  2554.1 134.7 reduce-scatter.26
  2696.3 134.7 reduce-scatter.28
  (11 shorter events, 473.6 us)
where the time goes:
time: 2850 us; the launch traced here: 2840 us
  waiting for transfers between devices  1890 us (66%)
  blocking collectives  540 us (19%)
  matrix products  187 us (7%)
  local copies, waits for them, and re-layouts  156 us (5%)
  other arithmetic  40.7 us (1%)
    unnamed x40, waiting for transfers between devices  442 us
    reduce_scatter x1, waiting for transfers between devices, on_device(): lax.psum_scatter(sum_enc_down, ('seq', 'dp'), scatter_dimension=0, tiled=...  142 us
    reduce_scatter x1, waiting for transfers between devices, on_device(): lax.psum_scatter(sum_dec_up, ('seq', 'dp'), scatter_dimension=0, tiled=True)  142 us
    reduce_scatter x1, waiting for transfers between devices, on_device(): lax.psum_scatter(sum_enc_up, ('seq', 'dp'), scatter_dimension=0, tiled=True)  141 us
    reduce_scatter x1, waiting for transfers between devices, on_device(): lax.psum_scatter(sum_dec_down, ('seq', 'dp'), scatter_dimension=0, tiled=...  141 us
    reduce_scatter x1, waiting for transfers between devices, on_device(): lax.psum_scatter(sum_cross_qkv, ('seq', 'dp'), scatter_dimension=1, tiled...  125 us
    reduce_scatter x1, waiting for transfers between devices, on_device(): lax.psum_scatter(sum_enc_out, ('seq', 'dp'), scatter_dimension=0, tiled=T...  105 us
    reduce_scatter x1, waiting for transfers between devices, on_device(): lax.psum_scatter(sum_self_out, ('seq', 'dp'), scatter_dimension=0, tiled=...  104 us
  transfers between devices with their start and end apart: 35, of which 22 were waited for; matrix products, arithmetic and copies ran while one was open for 12% of the time, Pallas kernels for 0%

commit v1 on v0

v1 whole, which is shorter than its diff:
```python
import functools

import jax
import jax.numpy as jnp
from jax import lax
from jax.experimental import pallas as pl
from jax.experimental.pallas import tpu as pltpu
from jax.sharding import Mesh
from jax.sharding import PartitionSpec as P

HEADS = 12
HEAD = 64
EPSILON = 1e-05
MASKED = -1e30
BLOCK = 128
F32 = jnp.float32
BF16 = jnp.bfloat16
AXES = ("z", "y", "x", "core")
PLANE = ("y", "x")
NT = (((1,), (1,)), ((), ()))
TN = (((0,), (0,)), ((), ()))


def matmul(left, right):
    return jnp.dot(left, right, preferred_element_type=F32)


def outer_sum(left, right):
    return lax.dot_general(left, right, TN, preferred_element_type=F32)


def back_matmul(left, right):
    return lax.dot_general(left, right, NT, preferred_element_type=F32)


def layer_norm(resid, gain, shift):
    center = resid - jnp.mean(resid, axis=-1, keepdims=True)
    second = jnp.mean(center * center, axis=-1, keepdims=True)
    return center * lax.rsqrt(second + EPSILON) * gain + shift


def norm_back(resid, gain, shift, grad_out):
    return jax.vjp(layer_norm, resid, gain, shift)[1](grad_out)


def gelu_exact(values):
    return jax.nn.gelu(values, approximate=False)


def positions(scal_ref, index):
    part, core, sub = scal_ref[0], scal_ref[1], scal_ref[2]
    group = lax.shift_right_logical(index, 10)
    half = lax.shift_right_logical(index, 9) & 1
    block = lax.shift_right_logical(index, 7) & 3
    return ((sub ^ group) << 10) + ((core ^ half) << 9) + ((part ^ block) << 7) + (index & 127)


def allowed_mask(scal_ref, start, width, keys, causal):
    query = positions(scal_ref, lax.broadcasted_iota(jnp.int32, (1, width), 1) + start)
    key = positions(scal_ref, lax.broadcasted_iota(jnp.int32, (keys, 1), 0))
    first = query >= scal_ref[3]
    second = query >= scal_ref[4]
    low = jnp.where(second, scal_ref[6], jnp.where(first, scal_ref[5], 0))
    high = jnp.where(second, scal_ref[7], jnp.where(first, scal_ref[6], scal_ref[5]))
    if causal:
        high = jnp.minimum(high, query + 1)
    return (key >= low) & (key < high)


def attn_fwd_kernel(causal, width, scal_ref, q_ref, k_ref, v_ref, o_ref, lse_ref, ot_ref):
    keys = k_ref.shape[0]
    heads = q_ref.shape[1] // HEAD
    for chunk in range(q_ref.shape[0] // width):
        rows = slice(chunk * width, (chunk + 1) * width)
        mask = allowed_mask(scal_ref, chunk * width, width, keys, causal)
        for head in range(heads):
            cols = slice(head * HEAD, (head + 1) * HEAD)
            scores = lax.dot_general(
                k_ref[:, cols], q_ref[rows, cols], NT, preferred_element_type=F32
            )
            scores = jnp.where(mask, scores, MASKED)
            peak = jnp.max(scores, axis=0, keepdims=True)
            weights = jnp.exp(scores - peak)
            total = jnp.sum(weights, axis=0, keepdims=True)
            probs = (weights * (1.0 / total)).astype(BF16)
            ot_ref[cols, rows] = lax.dot_general(
                v_ref[:, cols], probs, TN, preferred_element_type=F32
            )
            lse_ref[head : head + 1, rows] = peak + jnp.log(total)
    o_ref[...] = ot_ref[...].T.astype(BF16)


def attn_bwd_kernel(
    causal, width, scal_ref, q_ref, k_ref, v_ref, do_ref, lse_ref, dq_ref, dk_ref, dv_ref, dqt_ref
):
    keys = k_ref.shape[0]
    heads = q_ref.shape[1] // HEAD
    for chunk in range(q_ref.shape[0] // width):
        rows = slice(chunk * width, (chunk + 1) * width)
        mask = allowed_mask(scal_ref, chunk * width, width, keys, causal)
        for head in range(heads):
            cols = slice(head * HEAD, (head + 1) * HEAD)
            key, value = k_ref[:, cols], v_ref[:, cols]
            query, grad = q_ref[rows, cols], do_ref[rows, cols]
            scores = lax.dot_general(key, query, NT, preferred_element_type=F32)
            probs = jnp.where(mask, jnp.exp(scores - lse_ref[head : head + 1, rows]), 0.0)
            grad_probs = lax.dot_general(value, grad, NT, preferred_element_type=F32)
            product = probs * grad_probs
            delta = jnp.sum(product, axis=0, keepdims=True)
            grad_scores = (product - probs * delta).astype(BF16)
            grad_value = matmul(probs.astype(BF16), grad)
            grad_key = matmul(grad_scores, query)
            if chunk == 0:
                dv_ref[:, cols] = grad_value
                dk_ref[:, cols] = grad_key
            else:
                dv_ref[:, cols] += grad_value
                dk_ref[:, cols] += grad_key
            dqt_ref[cols, rows] = lax.dot_general(
                key, grad_scores, TN, preferred_element_type=F32
            ) * (HEAD**-0.5)
    dq_ref[...] = dqt_ref[...].T.astype(BF16)


def vmem_specs(count):
    return [pl.BlockSpec(memory_space=pltpu.VMEM)] * count


def attn_forward(scal, queries, keys, values, causal):
    rows, cols = queries.shape
    length = keys.shape[0]
    width = 256 if length <= 1024 else 128
    work = rows * length * cols
    return pl.pallas_call(
        functools.partial(attn_fwd_kernel, causal, width),
        out_shape=(
            jax.ShapeDtypeStruct((rows, cols), BF16),
            jax.ShapeDtypeStruct((8, rows), F32),
        ),
        in_specs=[pl.BlockSpec(memory_space=pltpu.SMEM)] + vmem_specs(3),
        out_specs=tuple(vmem_specs(2)),
        scratch_shapes=[pltpu.VMEM((cols, rows), F32)],
        compiler_params=pltpu.CompilerParams(vmem_limit_bytes=48 << 20),
        cost_estimate=pl.CostEstimate(
            flops=8 * work, transcendentals=work // HEAD, bytes_accessed=4 * length * cols
        ),
        name="attn_forward",
    )(scal, queries, keys, values)


def attn_backward(scal, queries, keys, values, grads, lse, causal):
    rows, cols = queries.shape
    length = keys.shape[0]
    width = 256 if length <= 1024 else 128
    work = rows * length * cols
    return pl.pallas_call(
        functools.partial(attn_bwd_kernel, causal, width),
        out_shape=(
            jax.ShapeDtypeStruct((rows, cols), BF16),
            jax.ShapeDtypeStruct((length, cols), F32),
            jax.ShapeDtypeStruct((length, cols), F32),
        ),
        in_specs=[pl.BlockSpec(memory_space=pltpu.SMEM)] + vmem_specs(5),
        out_specs=tuple(vmem_specs(3)),
        scratch_shapes=[pltpu.VMEM((cols, rows), F32)],
        compiler_params=pltpu.CompilerParams(vmem_limit_bytes=48 << 20),
        cost_estimate=pl.CostEstimate(
            flops=20 * work, transcendentals=work // HEAD, bytes_accessed=12 * length * cols
        ),
        name="attn_backward",
    )(scal, queries, keys, values, grads, lse)


def plane_swap(values, shift):
    return lax.ppermute(values, PLANE, [(i, i ^ shift) for i in range(4)])


def core_swap(values):
    return lax.ppermute(values, "core", [(0, 1), (1, 0)])


def plane_gather(values):
    return jnp.concatenate([values] + [plane_swap(values, k) for k in (1, 2, 3)], axis=0)


def plane_sum(left, right, contract):
    own = contract(left[:BLOCK], right)
    rest = contract(left[BLOCK:], right).astype(BF16)
    for k in (1, 2, 3):
        own = own + plane_swap(rest[(k - 1) * BLOCK : k * BLOCK], k).astype(F32)
    return own


class Layout:
    def __init__(self, groups, rows):
        self.groups = groups
        self.devices = groups * 8
        self.subs = groups // rows

    def index(self, z, y, x, c):
        return ((z * 2 + y) * 2 + x) * 2 + c

    def token_moves(self):
        moves = []
        for z in range(self.groups):
            for y in range(2):
                for x in range(2):
                    for c in range(2):
                        row, block = 2 * x + c, 2 * z + y
                        group, within = row * self.subs + block // 8, block % 8
                        core, part = within // 4, within % 4
                        moves.append(
                            (self.index(z, y, x, c), self.index(group, part // 2, part % 2, core))
                        )
        return moves

    def back_moves(self):
        return [(b, a) for a, b in self.token_moves()]

    def turn_moves(self):
        moves = []
        for part in range(4):
            for z in range(self.groups):
                owner, user = part * self.groups + z, z * 4 + part
                moves.append((owner, user))
        return moves


def on_device(lay, core, part, sub, params, tokens):
    (
        enc_qkv,
        enc_out_w,
        enc_attn_bias,
        enc_up,
        enc_up_bias,
        enc_down,
        enc_down_bias,
        enc_gains,
        enc_shifts,
        self_qkv,
        self_out,
        self_bias,
        cross_qkv,
        cross_out,
        cross_bias,
        dec_up,
        dec_up_bias,
        dec_down,
        dec_down_bias,
        dec_gains,
        dec_shifts,
    ) = params
    src, tgt, src_seg, tgt_seg, out_grad = tokens
    groups = lay.groups
    width = src.shape[1]
    rows = enc_out_w.shape[0]
    rows_ff = enc_down.shape[0]
    quarter = width // 4
    hidden = rows_ff * groups * 2
    heads_out = enc_qkv.shape[0] * quarter

    ids = jnp.concatenate([src_seg, tgt_seg]).astype(BF16)
    ids = jnp.pad(ids[None], ((0, 7), (0, width - 2 * BLOCK)))
    packed = lax.ppermute(jnp.concatenate([src, tgt, ids], axis=0), AXES, lay.token_moves())
    out_grad = lax.ppermute(out_grad, AXES, lay.token_moves())
    src, tgt = packed[:BLOCK], packed[BLOCK : 2 * BLOCK]
    pieces = [packed] + [plane_swap(packed, k) for k in (1, 2, 3)]
    src_rows = jnp.concatenate([piece[:BLOCK] for piece in pieces], axis=0)
    tgt_rows = jnp.concatenate([piece[BLOCK : 2 * BLOCK] for piece in pieces], axis=0)
    doc = jnp.concatenate([piece[2 * BLOCK : 2 * BLOCK + 1] for piece in pieces], axis=0)
    doc = doc[:, : 2 * BLOCK].astype(F32).reshape(4, 2, BLOCK)
    count = jnp.stack(
        [
            jnp.sum((doc < 0.5).astype(F32), axis=(0, 2)),
            jnp.sum((doc < 1.5).astype(F32), axis=(0, 2)),
        ]
    )
    count = jnp.pad(count, ((0, 6), (0, BLOCK - 2)))
    count = count + core_swap(count)
    for j in range(1, lay.subs):
        pass
    if lay.subs > 1:
        total = count
        for j in range(1, lay.subs):
            total = total + lax.ppermute(count, "z", [(z, z ^ j) for z in range(groups)])
        count = total
    count = count.astype(jnp.int32)
    length = jnp.int32(lay.subs * 8 * BLOCK)

    def scalars(query, key):
        return jnp.stack(
            [
                part,
                core,
                sub,
                count[0, query],
                count[1, query],
                count[0, key],
                count[1, key],
                length,
            ]
        ).astype(jnp.int32)

    def part_columns(values, pieces):
        return lax.all_to_all(values, PLANE, split_axis=0, concat_axis=0, tiled=True)

    def heads_split(qkv):
        parts = qkv.reshape(3, rows, 4, quarter)
        return parts.transpose(2, 1, 0, 3).reshape(4, rows, heads_out)

    def up_split(up):
        parts = up.reshape(rows, groups, 4, 2, rows_ff)
        return parts.transpose(2, 0, 3, 1, 4).reshape(4, rows, hidden)

    def both_cores(mine, axis):
        other = core_swap(mine)
        shape = [1] * (mine.ndim + 1)
        shape[axis] = 2
        which = lax.broadcasted_iota(jnp.int32, shape, axis) == core
        return jnp.where(which, jnp.expand_dims(mine, axis), jnp.expand_dims(other, axis))

    def whole_rows(split):
        split = lax.all_to_all(split, PLANE, split_axis=0, concat_axis=0, tiled=True)
        split = lax.all_gather(split, "z", axis=0)
        return both_cores(split, 2).reshape(width, split.shape[-1])

    first = whole_rows(jnp.concatenate([heads_split(enc_qkv), heads_split(self_qkv)], axis=2))
    w_enc, w_self = first[:, :heads_out], first[:, heads_out:]

    outs = jnp.concatenate([enc_out_w, self_out, cross_out], axis=1)
    outs = lax.ppermute(outs, ("z", "y", "x"), lay.turn_moves())
    outs = lax.all_gather(outs, "z", axis=0)
    outs = both_cores(outs, 1).reshape(quarter, 3 * width)
    wo_enc, wo_self, wo_cross = (outs[:, k * width : (k + 1) * width] for k in range(3))

    vectors = jnp.concatenate(
        [
            enc_attn_bias,
            self_bias,
            cross_bias,
            enc_down_bias[None],
            dec_down_bias[None],
            enc_gains,
            dec_gains,
            enc_shifts,
            dec_shifts,
        ],
        axis=0,
    )
    vector_count = vectors.shape[0]
    vectors = jnp.concatenate([vectors.reshape(-1), enc_up_bias, dec_up_bias])[None]
    vectors = lax.all_gather(vectors, AXES, axis=0, tiled=True).astype(F32)
    ups = vectors[:, vector_count * rows :].reshape(groups, 4, 2, 2, rows_ff)
    ups = lax.dynamic_index_in_dim(ups, part, axis=1, keepdims=False)
    ups = ups.transpose(2, 1, 0, 3).reshape(2, hidden)
    vectors = vectors[:, : vector_count * rows].reshape(lay.devices, vector_count, rows)
    vectors = vectors.transpose(1, 0, 2).reshape(vector_count, width)
    mine = lax.dynamic_slice_in_dim(vectors, part * quarter, quarter, axis=1)

    second = whole_rows(up_split(enc_up))
    w_up_enc = second
    w_down_enc = both_cores(lax.all_gather(enc_down, "z", axis=0), 0).reshape(hidden, width)
    third = whole_rows(jnp.concatenate([heads_split(cross_qkv), up_split(dec_up)], axis=2))
    w_cross, w_up_dec = third[:, :heads_out], third[:, heads_out:]
    w_down_dec = both_cores(lax.all_gather(dec_down, "z", axis=0), 0).reshape(hidden, width)

    scale = HEAD**-0.5

    def with_others(kv):
        kv = jnp.concatenate([kv, core_swap(kv)], axis=0)
        if lay.subs > 1:
            kv = jnp.concatenate(
                [kv]
                + [
                    lax.ppermute(kv, "z", [(z, z ^ j) for z in range(groups)])
                    for j in range(1, lay.subs)
                ],
                axis=0,
            )
        return kv

    def project(query_rows, key_rows, weight, bias):
        q = (matmul(query_rows, weight[:, :quarter]) + bias[0]).astype(BF16) * BF16(scale)
        shift = jnp.concatenate([jnp.zeros_like(bias[1]), bias[1]])
        kv = (matmul(key_rows, weight[:, quarter:]) + shift).astype(BF16)
        kv = with_others(kv)
        return q, kv[:, :quarter], kv[:, quarter:]

    def ffn(rows_in, up, up_bias, down):
        pre = matmul(rows_in, up) + up_bias
        act = gelu_exact(pre).astype(BF16)
        return plane_sum(act, down, matmul), pre, act

    scal_enc, scal_self, scal_cross = scalars(0, 0), scalars(1, 1), scalars(1, 0)
    q_enc, k_enc, v_enc = project(src_rows, src_rows, w_enc, mine[0:2])
    o_enc, lse_enc = attn_forward(scal_enc, q_enc, k_enc, v_enc, False)
    r_enc1 = src.astype(F32) + plane_sum(o_enc, wo_enc, matmul) + vectors[2]
    gains_enc, gains_dec = vectors[11:13], vectors[13:16]
    shifts_enc, shifts_dec = vectors[16:18], vectors[18:21]
    e1 = layer_norm(r_enc1, gains_enc[0], shifts_enc[0])
    e1_rows = plane_gather(e1.astype(BF16))
    branch, pre_enc, act_enc = ffn(e1_rows, w_up_enc, ups[0], w_down_enc)
    r_enc2 = e1 + branch + vectors[9]
    encoded = layer_norm(r_enc2, gains_enc[1], shifts_enc[1])
    encoded_rows = plane_gather(encoded.astype(BF16))

    q_self, k_self, v_self = project(tgt_rows, tgt_rows, w_self, mine[3:5])
    o_self, lse_self = attn_forward(scal_self, q_self, k_self, v_self, True)
    r_dec1 = tgt.astype(F32) + plane_sum(o_self, wo_self, matmul) + vectors[5]
    t1 = layer_norm(r_dec1, gains_dec[0], shifts_dec[0])
    t1_rows = plane_gather(t1.astype(BF16))

    q_cross, k_cross, v_cross = project(t1_rows, encoded_rows, w_cross, mine[6:8])
    o_cross, lse_cross = attn_forward(scal_cross, q_cross, k_cross, v_cross, False)
    r_dec2 = t1 + plane_sum(o_cross, wo_cross, matmul) + vectors[8]
    t2 = layer_norm(r_dec2, gains_dec[1], shifts_dec[1])
    t2_rows = plane_gather(t2.astype(BF16))
    branch, pre_dec, act_dec = ffn(t2_rows, w_up_dec, ups[1], w_down_dec)
    r_dec3 = t2 + branch + vectors[10]
    t3 = layer_norm(r_dec3, gains_dec[2], shifts_dec[2])

    def column_sum(values):
        return jnp.sum(values.astype(F32), axis=0)

    def ffn_back(grad, rows_in, up, down, pre, act):
        low = grad.astype(BF16)
        low_rows = plane_gather(low)
        grad_down = outer_sum(act, low_rows)
        grad_act = back_matmul(low_rows, down)
        grad_pre = jax.vjp(gelu_exact, pre)[1](grad_act)[0].astype(BF16)
        grad_up = outer_sum(rows_in, grad_pre)
        grad_in = plane_sum(grad_pre, up, back_matmul)
        return grad_in, grad_up, column_sum(grad_pre), grad_down, column_sum(low)

    def attn_back(grad, out_weight, scal, q, k, v, o, lse, causal):
        low = grad.astype(BF16)
        low_rows = plane_gather(low)
        grad_out_w = outer_sum(o, low_rows)
        grad_o = back_matmul(low_rows, out_weight).astype(BF16)
        dq, dk, dv = attn_backward(scal, q, k, v, grad_o, lse, causal)
        dkv = jnp.concatenate([dk, dv], axis=1)
        half = 4 * BLOCK
        if lay.subs > 1:
            total = dkv[: 2 * half]
            for j in range(1, lay.subs):
                total = total + lax.ppermute(
                    dkv[2 * half * j : 2 * half * (j + 1)],
                    "z",
                    [(z, z ^ j) for z in range(groups)],
                )
            dkv = total
        dkv = (dkv[:half] + core_swap(dkv[half:])).astype(BF16)
        return dq, dkv, grad_out_w, column_sum(low)

    d_r3, g_gain_d3, g_shift_d3 = norm_back(
        r_dec3, gains_dec[2], shifts_dec[2], out_grad.astype(F32)
    )
    d_t2, g_up_dec, g_upb_dec, g_down_dec, g_downb_dec = ffn_back(
        d_r3, t2_rows, w_up_dec, w_down_dec, pre_dec, act_dec
    )
    d_r2, g_gain_d2, g_shift_d2 = norm_back(r_dec2, gains_dec[1], shifts_dec[1], d_r3 + d_t2)
    dq, dkv, g_wo_cross, g_bout_cross = attn_back(
        d_r2, wo_cross, scal_cross, q_cross, k_cross, v_cross, o_cross, lse_cross, False
    )
    d_encoded = plane_sum(dkv, w_cross[:, quarter:], back_matmul)
    d_t1 = plane_sum(dq, w_cross[:, :quarter], back_matmul)
    g_cross = jnp.concatenate([outer_sum(t1_rows, dq), outer_sum(encoded_rows, dkv)], axis=1)
    g_bq_cross, g_bv_cross = column_sum(dq), column_sum(dkv[:, quarter:])

    d_r1, g_gain_d1, g_shift_d1 = norm_back(r_dec1, gains_dec[0], shifts_dec[0], d_r2 + d_t1)
    dq, dkv, g_wo_self, g_bout_self = attn_back(
        d_r1, wo_self, scal_self, q_self, k_self, v_self, o_self, lse_self, True
    )
    dqkv = jnp.concatenate([dq, dkv], axis=1)
    tgt_grad = d_r1 + plane_sum(dqkv, w_self, back_matmul)
    g_self = outer_sum(tgt_rows, dqkv)
    g_bq_self, g_bv_self = column_sum(dq), column_sum(dkv[:, quarter:])

    d_e2, g_gain_e2, g_shift_e2 = norm_back(r_enc2, gains_enc[1], shifts_enc[1], d_encoded)
    d_e1, g_up_enc, g_upb_enc, g_down_enc, g_downb_enc = ffn_back(
        d_e2, e1_rows, w_up_enc, w_down_enc, pre_enc, act_enc
    )
    d_r1e, g_gain_e1, g_shift_e1 = norm_back(r_enc1, gains_enc[0], shifts_enc[0], d_e2 + d_e1)
    dq, dkv, g_wo_enc, g_bout_enc = attn_back(
        d_r1e, wo_enc, scal_enc, q_enc, k_enc, v_enc, o_enc, lse_enc, False
    )
    dqkv = jnp.concatenate([dq, dkv], axis=1)
    src_grad = d_r1e + plane_sum(dqkv, w_enc, back_matmul)
    g_enc = outer_sum(src_rows, dqkv)
    g_bq_enc, g_bv_enc = column_sum(dq), column_sum(dkv[:, quarter:])

    def core_reduce(grad, axis):
        zero = lax.index_in_dim(grad, 0, axis, keepdims=False)
        one = lax.index_in_dim(grad, 1, axis, keepdims=False)
        send = jnp.where(core == 0, one, zero).astype(BF16)
        keep = jnp.where(core == 0, zero, one)
        return (keep + core_swap(send).astype(F32)).astype(BF16)

    def rows_reduce(grad):
        grad = core_reduce(grad.reshape(groups, 4, 2, rows, -1), 2)
        grad = lax.psum_scatter(grad, "z", scatter_dimension=0, tiled=False)
        return lax.all_to_all(grad, PLANE, split_axis=0, concat_axis=0, tiled=True)

    def heads_join(parts):
        parts = parts.reshape(4, rows, 3, quarter).transpose(2, 1, 0, 3)
        return parts.reshape(3, rows, width).astype(F32)

    def up_join(parts):
        parts = parts.reshape(4, rows, 2, groups, rows_ff).transpose(1, 3, 0, 2, 4)
        return parts.reshape(rows, -1).astype(F32)

    def down_reduce(grad):
        grad = core_reduce(grad.reshape(2, groups, rows_ff, width), 0)
        return lax.psum_scatter(grad, "z", scatter_dimension=0, tiled=False).astype(F32)

    def out_reduce(grad):
        grad = core_reduce(grad.reshape(groups, 2, rows, width), 1)
        grad = lax.psum_scatter(grad, "z", scatter_dimension=0, tiled=False)
        return lax.ppermute(
            grad, ("z", "y", "x"), [(b, a) for a, b in lay.turn_moves()]
        ).astype(F32)

    g_dec_down = down_reduce(g_down_dec)
    g_dec_up = up_join(rows_reduce(g_up_dec))
    g_cross_qkv = heads_join(rows_reduce(g_cross))
    g_cross_out = out_reduce(g_wo_cross)
    g_self_qkv = heads_join(rows_reduce(g_self))
    g_self_out = out_reduce(g_wo_self)
    g_enc_down = down_reduce(g_down_enc)
    g_enc_up = up_join(rows_reduce(g_up_enc))
    g_enc_out = out_reduce(g_wo_enc)
    g_enc_qkv = heads_join(rows_reduce(g_enc))

    placed = jnp.stack([g_bq_enc, g_bv_enc, g_bq_self, g_bv_self, g_bq_cross, g_bv_cross])
    placed = lax.dynamic_update_slice(
        jnp.zeros((6, width), F32), placed, (jnp.int32(0), part * quarter)
    )
    small = jnp.concatenate(
        [
            placed,
            jnp.stack(
                [
                    g_bout_enc,
                    g_bout_self,
                    g_bout_cross,
                    g_downb_enc,
                    g_downb_dec,
                    g_gain_e1,
                    g_gain_e2,
                    g_gain_d1,
                    g_gain_d2,
                    g_gain_d3,
                    g_shift_e1,
                    g_shift_e2,
                    g_shift_d1,
                    g_shift_d2,
                    g_shift_d3,
                ]
            ),
        ],
        axis=0,
    )
    small_count = small.shape[0]
    small = small.reshape(small_count, lay.devices, rows).transpose(1, 0, 2)
    small = small.reshape(lay.devices, small_count * rows)
    ups_g = jnp.stack([g_upb_enc, g_upb_dec]).reshape(2, 2, groups, rows_ff)
    ups_g = ups_g.transpose(2, 1, 0, 3)[:, None]
    ups_g = lax.dynamic_update_slice(
        jnp.zeros((groups, 4, 2, 2, rows_ff), F32),
        ups_g,
        (jnp.int32(0), part, jnp.int32(0), jnp.int32(0), jnp.int32(0)),
    ).reshape(lay.devices, 2 * rows_ff)
    small = jnp.concatenate([small, ups_g], axis=1)
    small = lax.all_to_all(small, AXES, split_axis=0, concat_axis=0, tiled=True)
    small = jnp.sum(small, axis=0)
    ups_g = small[small_count * rows :]
    small = small[: small_count * rows].reshape(small_count, rows)

    def home(values):
        return lax.ppermute(values.astype(BF16), AXES, lay.back_moves())

    return (
        home(t3)[None],
        home(src_grad).astype(F32)[None],
        home(tgt_grad).astype(F32)[None],
        g_enc_qkv,
        g_enc_out,
        jnp.stack([small[0], small[1], small[6]]),
        g_enc_up,
        ups_g[:rows_ff],
        g_enc_down,
        small[9],
        small[11:13],
        small[16:18],
        g_self_qkv,
        g_self_out,
        jnp.stack([small[2], small[3], small[7]]),
        g_cross_qkv,
        g_cross_out,
        jnp.stack([small[4], small[5], small[8]]),
        g_dec_up,
        ups_g[rows_ff:],
        g_dec_down,
        small[10],
        small[13:16],
        small[18:21],
    )


def solution(mesh):
    groups = mesh.shape["seq"] // 2
    rows = mesh.shape["dp"]
    lay = Layout(groups, rows)
    fine = Mesh(mesh.devices.reshape(groups, 2, 2, 2), AXES)
    seq, dp = ("z", "y"), ("x", "core")

    def run(
        src,
        tgt,
        src_seg,
        tgt_seg,
        enc_qkv,
        enc_out_w,
        enc_attn_bias,
        enc_up,
        enc_up_bias,
        enc_down,
        enc_down_bias,
        enc_gains,
        enc_shifts,
        self_qkv,
        self_out,
        self_bias,
        cross_qkv,
        cross_out,
        cross_bias,
        dec_up,
        dec_up_bias,
        dec_down,
        dec_down_bias,
        dec_gains,
        dec_shifts,
        out_grad,
    ):
        core = lax.axis_index("core")
        part = 2 * lax.axis_index("y") + lax.axis_index("x")
        sub = lax.axis_index("z") % lay.subs
        params = (
            enc_qkv,
            enc_out_w,
            enc_attn_bias,
            enc_up,
            enc_up_bias,
            enc_down,
            enc_down_bias,
            enc_gains,
            enc_shifts,
            self_qkv,
            self_out,
            self_bias,
            cross_qkv,
            cross_out,
            cross_bias,
            dec_up,
            dec_up_bias,
            dec_down,
            dec_down_bias,
            dec_gains,
            dec_shifts,
        )
        return on_device(
            lay, core, part, sub, params, (src[0], tgt[0], src_seg[0], tgt_seg[0], out_grad[0])
        )

    token = P(dp, seq, None)
    ids = P(dp, seq)
    stack = P(None, AXES, None)
    mat = P(AXES, None)
    vecs = P(None, AXES)
    vec = P(AXES)
    in_specs = (
        (token, token, ids, ids)
        + (stack, mat, vecs, mat, vec, mat, vec, vecs, vecs)
        + (stack, mat, vecs, stack, mat, vecs, mat, vec, mat, vec, vecs, vecs)
        + (token,)
    )
    out_specs = (
        (token, token, token)
        + (stack, mat, vecs, mat, vec, mat, vec, vecs, vecs)
        + (stack, mat, vecs, stack, mat, vecs, mat, vec, mat, vec, vecs, vecs)
    )
    return jax.shard_map(run, mesh=fine, in_specs=in_specs, out_specs=out_specs, check_vma=False)
```

time: 2850 us -> 742 us (0.26)
  waiting for transfers between devices: 1890 us -> 151 us
  blocking collectives: 540 us -> 159 us
  starting transfers between devices: 2.17 us -> 150 us
  matrix products: 187 us -> 67.4 us
  local copies, waits for them, and re-layouts: 156 us -> 80.5 us
  Pallas kernels: 0 us -> 37.5 us
    reduce_scatter x8 -> x10, waiting for transfers between devices: 1000 us -> 12.4 us  [the longest x2 12.4 us: down_reduce(): lax.psum_scatter(grad, 'z', scatter_dimension=0, tiled=False).astype(F32)]
    all_gather x22 -> x0, waiting for transfers between devices: 449 us -> none  [the longest x1 65.1 us: on_device(): lax.all_gather(enc_qkv, ('seq', 'dp'), axis=1, tiled=True)]
    unnamed x40 -> x10, waiting for transfers between devices: 442 us -> 0.16 us
    all_gather x15 -> x6, blocking collectives: 503 us -> 112 us  [the longest x3 59.3 us: whole_rows(): split = lax.all_gather(split, 'z', axis=0)]
    dot_general x84 -> x46, matrix products: 187 us -> 67.4 us  [the longest x18 26.5 us: matmul(): return jnp.dot(left, right, preferred_element_type=F32)]
    ppermute x0 -> x95, waiting for transfers between devices: none -> 116 us  [the longest x63 116 us: plane_swap(): return lax.ppermute(values, PLANE, [(i, i ^ shift) for i in range(4)])]
    ppermute x0 -> x95, starting transfers between devices: none -> 101 us  [the longest x63 77.7 us: plane_swap(): return lax.ppermute(values, PLANE, [(i, i ^ shift) for i in range(4)])]
    all_to_all x0 -> x9, starting transfers between devices: none -> 47.9 us  [the longest x5 29.5 us: rows_reduce(): return lax.all_to_all(grad, PLANE, split_axis=0, concat_axis=0, tiled=True)]
  transfers between devices with their start and end apart: 35 -> 114, of which waited for: 22 -> 44; matrix products, arithmetic and copies ran while one was open for 12% -> 23% of each run, Pallas kernels for 0% -> 3%
where the time goes in v1:
time: 742 us; the launch traced here: 732 us
  blocking collectives  159 us (21%)
  waiting for transfers between devices  151 us (20%)
  starting transfers between devices  150 us (20%)
  local copies, waits for them, and re-layouts  80.5 us (11%)
  other arithmetic  69.1 us (9%)
  matrix products  67.4 us (9%)
  Pallas kernels  37.5 us (5%)
  between operations  17.9 us (2%)
    ppermute x63, waiting for transfers between devices, plane_swap(): return lax.ppermute(values, PLANE, [(i, i ^ shift) for i in range(4)])  116 us
    ppermute x63, starting transfers between devices, plane_swap(): return lax.ppermute(values, PLANE, [(i, i ^ shift) for i in range(4)])  77.7 us
    all_gather x3, blocking collectives, whole_rows(): split = lax.all_gather(split, 'z', axis=0)  59.3 us
    unnamed x1, blocking collectives  46.4 us
    all_to_all x5, starting transfers between devices, rows_reduce(): return lax.all_to_all(grad, PLANE, split_axis=0, concat_axis=0, tiled=True)  29.5 us
    dot_general x18, matrix products, matmul(): return jnp.dot(left, right, preferred_element_type=F32)  26.5 us
    dot_general x17, matrix products, back_matmul(): return lax.dot_general(left, right, NT, preferred_element_type=F32)  26.1 us
    unnamed x459, local copies, waits for them, and re-layouts  20.4 us
  transfers between devices with their start and end apart: 114, of which 44 were waited for; matrix products, arithmetic and copies ran while one was open for 23% of the time, Pallas kernels for 3%

profile of v1, /device:TPU:0, one launch (start us, length us, event | category | flops | bytes accessed | tf_op | source)
XLA Modules:
  0.0 732.2 jit_solution(13004021175021119719)
XLA Ops:
  7.2 18.5 %all-gather.5 = bf16[384,768]{1,0:T(8,128)(2,1)S(1)} all-gather(bf16[96,768]{1,0:T(8,128)(2,1)} %param.35), channel_id=7, replica_groups=mesh['z'=4,'y'=2,'x'=2,'core'=2] {'z'}, dimensions={0}, use_global_device_ids=true | all-gather | bytes 737280 | tf_op jit(solution)/shard_map/all_gather | solution.py:362
  26.0 19.0 %all-gather.6 = bf16[384,768]{1,0:T(8,128)(2,1)} all-gather(bf16[96,768]{1,0:T(8,128)(2,1)} %param.47), channel_id=8, replica_groups=mesh['z'=4,'y'=2,'x'=2,'core'=2] {'z'}, dimensions={0}, use_global_device_ids=true | all-gather | bytes 737280 | tf_op jit(solution)/shard_map/all_gather | solution.py:365
  58.9 46.4 %all-reduce.5 = bf16[22272]{0:T(1024)(128)(2,1)S(1)} all-reduce(bf16[22272]{0:T(1024)(128)(2,1)S(1)} %dynamic-update-slice), channel_id=3, replica_groups=mesh['z'=4,'y'=2,'x'=2,'core'=2] {'z','y','x','core'}, use_global_device_ids=true, to_apply=%add.5 | all-reduce | flops 22272 | bytes 89088
  118.2 15.3 %all-gather.2 = bf16[96,2304]{1,0:T(8,128)(2,1)S(1)} all-gather(bf16[24,2304]{1,0:T(8,128)(2,1)S(1)} %collective-permute-done.7), channel_id=4, replica_groups=mesh['z'=4,'y'=2,'x'=2,'core'=2] {'z'}, dimensions={0}, use_global_device_ids=true | all-gather | bytes 552960 | tf_op jit(solution)/shard_map/all_gather | solution.py:332
  137.2 16.6 %all-gather.4 = bf16[16,24,768]{2,1,0:T(8,128)(2,1)} all-gather(bf16[4,24,768]{2,1,0:T(8,128)(2,1)S(1)} %all-to-all-done.2), channel_id=6, replica_groups=mesh['z'=4,'y'=2,'x'=2,'core'=2] {'z'}, dimensions={0}, use_global_device_ids=true | all-gather | bytes 737280 | tf_op jit(solution)/shard_map/all_gather | solution.py:324
  157.7 20.6 %all-gather = bf16[16,24,1152]{2,1,0:T(8,128)(2,1)S(1)} all-gather(bf16[4,24,1152]{2,1,0:T(8,128)(2,1)S(1)} %all-to-all-done), channel_id=2, replica_groups=mesh['z'=4,'y'=2,'x'=2,'core'=2] {'z'}, dimensions={0}, use_global_device_ids=true | all-gather | bytes 1105920 | tf_op jit(solution)/shard_map/all_gather | solution.py:324
  182.7 22.1 %all-gather.3 = bf16[16,24,1344]{2,1,0:T(8,128)(2,1)S(1)} all-gather(bf16[4,24,1344]{2,1,0:T(8,128)(2,1)S(1)} %all-to-all-done.1), channel_id=5, replica_groups=mesh['z'=4,'y'=2,'x'=2,'core'=2] {'z'}, dimensions={0}, use_global_device_ids=true | all-gather | bytes 1290240 | tf_op jit(solution)/shard_map/all_gather | solution.py:324
  236.0 6.1 attn_forward.3
  242.7 6.3 attn_forward.4
  278.6 5.7 multiply_convert_fusion.1
  288.7 5.2 collective-permute-done.27
  321.5 6.1 attn_forward.5
  353.8 8.0 %multiply_convert_fusion = (bf16[512,768]{1,0:T(8,128)(2,1)S(1)}, f32[512,768]{1,0:T(8,128)}, f32[512,768]{1,0:T(8,128)}) fusion(f32[768]{0:T(1024)S(1)} %add.510, bf16[768,1344]{1,0:T(8,128)(2,1)} %copy-done.49, bf16[128,768]{1,0:T(8,128)(2,1)S(1)} %collective-permute-done.37, bf16[128,768]{1,0:T(8,128)(2,1)S(1)} %collective-permute-done.36, ...), kind=kOutput, calls=%fused_computation.17 | convolution fusion | flops 633077760 | bytes 5901312 | tf_op jit(solution)/shard_map/dot_general | solution.py:25
  379.9 5.8 collective-permute-start.46
  428.9 6.4 attn_backward.3
  460.7 5.2 collective-permute-done.56
  546.1 6.2 attn_backward.4
  560.1 6.4 attn_backward.5
  600.5 8.2 %all-to-all-start.8 = ((bf16[4,24,768]{2,1,0:T(8,128)(2,1)}), bf16[4,24,768]{2,1,0:T(8,128)(2,1)S(1)}, u32[]{:S(2)}, u32[]{:S(2)}) async-start(bf16[4,24,768]{2,1,0:T(8,128)(2,1)} %bitcast.372), calls=%async_computation.17 | async-start | bytes 294912 | tf_op jit(solution)/shard_map/all_to_all | solution.py:502
  619.7 9.3 %all-to-all-start.7 = ((bf16[4,24,576]{2,1,0:T(8,128)(2,1)}), bf16[4,24,576]{2,1,0:T(8,128)(2,1)S(1)}, u32[]{:S(2)}, u32[]{:S(2)}) async-start(bf16[4,24,576]{2,1,0:T(8,128)(2,1)} %bitcast.376), calls=%async_computation.14 | async-start | bytes 245760 | tf_op jit(solution)/shard_map/all_to_all | solution.py:502
  649.1 6.0 all-to-all-start.4
  656.8 6.9 all-to-all-done.4
  685.2 6.8 all-to-all-done.5
  705.1 12.4 %reduce-scatter.17.cloned.1.call-done = bf16[1,96,768]{2,1,0:T(8,128)(2,1)} async-done(((bf16[4,96,768]{2,1,0:T(8,128)(2,1)}), bf16[1,96,768]{2,1,0:T(8,128)(2,1)}) %reduce-scatter.17.cloned.1.call-update) | async-done | bytes 147472 | tf_op jit(solution)/shard_map/reduce_scatter | solution.py:514
  (972 shorter events, 438.9 us)
Async XLA Ops:
  25.9 156.0 %collective-permute-start.24 = (bf16[4,96,768]{2,1,0:T(8,128)(2,1)S(1)}, bf16[4,96,768]{2,1,0:T(8,128)(2,1)S(1)}, u32[]{:S(2)}, u32[]{:S(2)}) collective-permute-start(bf16[4,96,768]{2,1,0:T(8,128)(2,1)S(1)} %bitcast.349), channel_id=1, source_target_pairs={{0,1},{1,0},{2,3},{3,2},{4,5},{5,4},{6,7},{7,6},{8,9},{9,8},{10,11... | collective-permute-start | bytes 1769480 | tf_op jit(solution)/shard_map/ppermute | solution.py:179
  44.9 163.2 %collective-permute-start.38 = (bf16[4,96,768]{2,1,0:T(8,128)(2,1)}, bf16[4,96,768]{2,1,0:T(8,128)(2,1)}, u32[]{:S(2)}, u32[]{:S(2)}) collective-permute-start(bf16[4,96,768]{2,1,0:T(8,128)(2,1)} %bitcast.44), channel_id=1, source_target_pairs={{0,1},{1,0},{2,3},{3,2},{4,5},{5,4},{6,7},{7,6},{8,9},{9,8},{10,11... | collective-permute-start | bytes 1769480 | tf_op jit(solution)/shard_map/ppermute | solution.py:179
  45.8 72.4 %collective-permute-start.7 = (bf16[24,2304]{1,0:T(8,128)(2,1)S(1)}, bf16[24,2304]{1,0:T(8,128)(2,1)S(1)}, u32[]{:S(2)}, u32[]{:S(2)}) collective-permute-start(bf16[24,2304]{1,0:T(8,128)(2,1)S(1)} %pad_maximum_fusion.43), channel_id=1, source_target_pairs={{0,0},{2,8},{4,16},{6,24},{8,2},{10,10},{12,18},{14,26},{16,4},{18... | collective-permute-start | bytes 331784 | tf_op jit(solution)/shard_map/ppermute | solution.py:331
  47.3 131.0 %collective-permute-start = (bf16[264,768]{1,0:T(8,128)(2,1)}, bf16[264,768]{1,0:T(8,128)(2,1)}, u32[]{:S(2)}, u32[]{:S(2)}) collective-permute-start(bf16[264,768]{1,0:T(8,128)(2,1)} %pad_maximum_fusion.18), channel_id=1, source_target_pairs={{0,0},{1,8},{2,16},{3,24},{4,2},{5,10},{6,18},{7,26},{8,4},{9,12},... | collective-permute-start | bytes 1216520 | tf_op jit(solution)/shard_map/ppermute | solution.py:264
  53.3 80.2 %all-to-all-start.2 = ((bf16[4,24,768]{2,1,0:T(8,128)(2,1)}), bf16[4,24,768]{2,1,0:T(8,128)(2,1)S(1)}, u32[]{:S(2)}, u32[]{:S(2)}) async-start(bf16[4,24,768]{2,1,0:T(8,128)(2,1)} %reshape.590), calls=%async_computation.2 | async-start | bytes 294912 | tf_op jit(solution)/shard_map/all_to_all | solution.py:323
  133.5 47.7 %collective-permute-start.8 = (bf16[4,24,2304]{2,1,0:T(8,128)(2,1)S(1)}, bf16[4,24,2304]{2,1,0:T(8,128)(2,1)S(1)}, u32[]{:S(2)}, u32[]{:S(2)}) collective-permute-start(bf16[4,24,2304]{2,1,0:T(8,128)(2,1)S(1)} %bitcast.351), channel_id=1, source_target_pairs={{0,1},{1,0},{2,3},{3,2},{4,5},{5,4},{6,7},{7,6},{8,9},{9,8},{10,11... | collective-permute-start | bytes 1327112 | tf_op jit(solution)/shard_map/ppermute | solution.py:179
  153.8 57.7 %collective-permute-start.23 = (bf16[4,4,24,768]{3,2,1,0:T(8,128)(2,1)}, bf16[4,4,24,768]{3,2,1,0:T(8,128)(2,1)}, u32[]{:S(2)}, u32[]{:S(2)}) collective-permute-start(bf16[4,4,24,768]{3,2,1,0:T(8,128)(2,1)} %bitcast.34), channel_id=1, source_target_pairs={{0,1},{1,0},{2,3},{3,2},{4,5},{5,4},{6,7},{7,6},{8,9},{9,8},{10,11... | collective-permute-start | bytes 1769480 | tf_op jit(solution)/shard_map/ppermute | solution.py:179
  157.7 429.6 %reduce-scatter.25.cloned.1.call-start = ((), (), s32[]{:S(2)}) async-start(), calls=%async_computation.26 | async-start | bytes 184320 | tf_op jit(solution)/shard_map/reduce_scatter | solution.py:518
  178.3 35.9 %collective-permute-start.3 = (bf16[264,768]{1,0:T(8,128)(2,1)}, bf16[264,768]{1,0:T(8,128)(2,1)}, u32[]{:S(2)}, u32[]{:S(2)}) collective-permute-start(bf16[264,768]{1,0:T(8,128)(2,1)} %collective-permute-done), channel_id=1, source_target_pairs={{0,6},{2,4},{4,2},{6,0},{1,7},{3,5},{5,3},{7,1},{8,14},{10,12},{12... | collective-permute-start | bytes 1216520 | tf_op jit(solution)/shard_map/ppermute | solution.py:175
  181.9 33.8 %collective-permute-start.1 = (bf16[264,768]{1,0:T(8,128)(2,1)}, bf16[264,768]{1,0:T(8,128)(2,1)}, u32[]{:S(2)}, u32[]{:S(2)}) collective-permute-start(bf16[264,768]{1,0:T(8,128)(2,1)} %collective-permute-done), channel_id=1, source_target_pairs={{0,2},{2,0},{4,6},{6,4},{1,3},{3,1},{5,7},{7,5},{8,10},{10,8},{12,... | collective-permute-start | bytes 1216520 | tf_op jit(solution)/shard_map/ppermute | solution.py:175
  404.6 39.8 %collective-permute-start.93 = (bf16[4,4,24,768]{3,2,1,0:T(8,128)(2,1)}, bf16[4,4,24,768]{3,2,1,0:T(8,128)(2,1)}, u32[]{:S(2)}, u32[]{:S(2)}) collective-permute-start(bf16[4,4,24,768]{3,2,1,0:T(8,128)(2,1)} %fusion.92), channel_id=1, source_target_pairs={{0,1},{1,0},{2,3},{3,2},{4,5},{5,4},{6,7},{7,6},{8,9},{9,8},{10,11... | collective-permute-start | bytes 1769480 | tf_op jit(solution)/shard_map/ppermute | solution.py:179
  416.4 123.5 %collective-permute-start.94 = (bf16[4,96,768]{2,1,0:T(8,128)(2,1)}, bf16[4,96,768]{2,1,0:T(8,128)(2,1)}, u32[]{:S(2)}, u32[]{:S(2)}) collective-permute-start(bf16[4,96,768]{2,1,0:T(8,128)(2,1)} %bitcast.120), channel_id=1, source_target_pairs={{0,1},{1,0},{2,3},{3,2},{4,5},{5,4},{6,7},{7,6},{8,9},{9,8},{10,11... | collective-permute-start | bytes 1769480 | tf_op jit(solution)/shard_map/ppermute | solution.py:179
  441.8 158.8 %reduce-scatter.27.cloned.1.call-start = ((), (), s32[]{:S(2)}) async-start(), calls=%async_computation.27 | async-start | bytes 737280 | tf_op jit(solution)/shard_map/reduce_scatter | solution.py:501
  448.1 168.7 %reduce-scatter.13.cloned.1.call-start = ((), (), s32[]{:S(2)}) async-start(), calls=%async_computation.20 | async-start | bytes 184320 | tf_op jit(solution)/shard_map/reduce_scatter | solution.py:518
  492.9 40.8 %collective-permute-start.90 = (bf16[4,4,24,576]{3,2,1,0:T(8,128)(2,1)}, bf16[4,4,24,576]{3,2,1,0:T(8,128)(2,1)}, u32[]{:S(2)}, u32[]{:S(2)}) collective-permute-start(bf16[4,4,24,576]{3,2,1,0:T(8,128)(2,1)} %fusion.104), channel_id=1, source_target_pairs={{0,1},{1,0},{2,3},{3,2},{4,5},{5,4},{6,7},{7,6},{8,9},{9,8},{10,11... | collective-permute-start | bytes 1327112 | tf_op jit(solution)/shard_map/ppermute | solution.py:179
  526.0 92.2 %reduce-scatter.21.cloned.1.call-start = ((), (), s32[]{:S(2)}) async-start(), calls=%async_computation.24 | async-start | bytes 184320 | tf_op jit(solution)/shard_map/reduce_scatter | solution.py:518
  530.5 89.2 %reduce-scatter.23.cloned.1.call-start = ((), (), s32[]{:S(2)}) async-start(), calls=%async_computation.25 | async-start | bytes 614400 | tf_op jit(solution)/shard_map/reduce_scatter | solution.py:501
  533.2 35.5 %collective-permute-start.85 = (bf16[4,4,24,768]{3,2,1,0:T(8,128)(2,1)}, bf16[4,4,24,768]{3,2,1,0:T(8,128)(2,1)}, u32[]{:S(2)}, u32[]{:S(2)}) collective-permute-start(bf16[4,4,24,768]{3,2,1,0:T(8,128)(2,1)} %fusion.91), channel_id=1, source_target_pairs={{0,1},{1,0},{2,3},{3,2},{4,5},{5,4},{6,7},{7,6},{8,9},{9,8},{10,11... | collective-permute-start | bytes 1769480 | tf_op jit(solution)/shard_map/ppermute | solution.py:179
  535.6 119.5 %reduce-scatter.29.cloned.1.call-start = ((), (), s32[]{:S(2)}) async-start(), calls=%async_computation.28 | async-start | bytes 737280 | tf_op jit(solution)/shard_map/reduce_scatter | solution.py:514
  542.1 138.2 %reduce-scatter.15.cloned.1.call-start = ((), (), s32[]{:S(2)}) async-start(), calls=%async_computation.21 | async-start | bytes 737280 | tf_op jit(solution)/shard_map/reduce_scatter | solution.py:501
  570.8 121.2 %reduce-scatter.11.cloned.1.call-start = ((), (), s32[]{:S(2)}) async-start(), calls=%async_computation.19 | async-start | bytes 614400 | tf_op jit(solution)/shard_map/reduce_scatter | solution.py:501
  582.4 115.0 %reduce-scatter.19.cloned.1.call-start = ((), (), s32[]{:S(2)}) async-start(), calls=%async_computation.23 | async-start | bytes 614400 | tf_op jit(solution)/shard_map/reduce_scatter | solution.py:501
  592.4 36.6 %collective-permute-start.86 = (bf16[4,96,768]{2,1,0:T(8,128)(2,1)}, bf16[4,96,768]{2,1,0:T(8,128)(2,1)S(1)}, u32[]{:S(2)}, u32[]{:S(2)}) collective-permute-start(bf16[4,96,768]{2,1,0:T(8,128)(2,1)} %bitcast.82), channel_id=1, source_target_pairs={{0,1},{1,0},{2,3},{3,2},{4,5},{5,4},{6,7},{7,6},{8,9},{9,8},{10,11... | collective-permute-start | bytes 1769480 | tf_op jit(solution)/shard_map/ppermute | solution.py:179
  629.0 88.5 %reduce-scatter.17.cloned.1.call-start = ((), (), s32[]{:S(2)}) async-start(), calls=%async_computation.22 | async-start | bytes 737280 | tf_op jit(solution)/shard_map/reduce_scatter | solution.py:514
  (310 other events, 3681.3 us)
Sparse Core Ops, SparseCore 0:
  441.9 19.2 reduce-scatter.24
  463.6 20.1 reduce-scatter.26
  526.2 19.0 reduce-scatter.12
  547.3 17.4 reduce-scatter.20
  567.1 21.6 reduce-scatter.22
  590.9 21.9 reduce-scatter.28
  615.2 22.3 reduce-scatter.14
  639.9 25.0 reduce-scatter.10
  667.4 25.9 reduce-scatter.18
  695.6 21.8 reduce-scatter.16

commit v2 on v1

v2 whole, which is shorter than its diff:
```python
import functools

import jax
import jax.numpy as jnp
from jax import lax
from jax.experimental import pallas as pl
from jax.experimental.pallas import tpu as pltpu
from jax.sharding import Mesh
from jax.sharding import PartitionSpec as P

HEADS = 12
HEAD = 64
EPSILON = 1e-05
MASKED = -1e30
BLOCK = 128
F32 = jnp.float32
BF16 = jnp.bfloat16
AXES = ("z", "y", "x", "core")
PLANE = ("y", "x")
NT = (((1,), (1,)), ((), ()))
TN = (((0,), (0,)), ((), ()))


def matmul(left, right):
    return jnp.dot(left, right, preferred_element_type=F32)


def outer_sum(left, right):
    return lax.dot_general(left, right, TN, preferred_element_type=F32)


def back_matmul(left, right):
    return lax.dot_general(left, right, NT, preferred_element_type=F32)


def layer_norm(resid, gain, shift):
    center = resid - jnp.mean(resid, axis=-1, keepdims=True)
    second = jnp.mean(center * center, axis=-1, keepdims=True)
    return center * lax.rsqrt(second + EPSILON) * gain + shift


def positions(subs, index):
    core = lax.axis_index("core")
    part = 2 * lax.axis_index("y") + lax.axis_index("x")
    sub = lax.axis_index("z") & (subs - 1)
    group = lax.shift_right_logical(index, 10)
    half = lax.shift_right_logical(index, 9) & 1
    block = lax.shift_right_logical(index, 7) & 3
    return ((sub ^ group) << 10) + ((core ^ half) << 9) + ((part ^ block) << 7) + (index & 127)


def allowed_mask(form, count_ref, start, width, keys):
    query_kind, key_kind, causal = form
    subs = keys // (8 * BLOCK)
    query = positions(subs, lax.broadcasted_iota(jnp.int32, (1, width), 1) + start)
    key = positions(subs, lax.broadcasted_iota(jnp.int32, (keys, 1), 0))
    one, two = count_ref[0, key_kind], count_ref[1, key_kind]
    first = query >= count_ref[0, query_kind]
    second = query >= count_ref[1, query_kind]
    low = jnp.where(second, two, jnp.where(first, one, 0))
    high = jnp.where(second, keys, jnp.where(first, two, one))
    if causal:
        high = jnp.minimum(high, query + 1)
    return (key >= low) & (key < high)


def joined(refs):
    return jnp.concatenate([ref[...] for ref in refs], axis=0)


def spread(value, out_refs):
    out_refs[0][...] = value[:BLOCK]
    for k in (1, 2, 3):
        out_refs[k][...] = value[k * BLOCK : (k + 1) * BLOCK].astype(BF16)


def spread_shapes(width):
    return [jax.ShapeDtypeStruct((BLOCK, width), F32)] + [
        jax.ShapeDtypeStruct((BLOCK, width), BF16)
    ] * 3


def split_shapes(split, shape, core_axis):
    if not split:
        rows = 1
        for size in shape[:-1]:
            rows *= size
        return [jax.ShapeDtypeStruct((rows, shape[-1]), F32)]
    half = shape[:core_axis] + shape[core_axis + 1 :]
    return [jax.ShapeDtypeStruct(half, F32), jax.ShapeDtypeStruct(half, BF16)]


def put_halves(all_ref, core_axis, out_refs):
    core = lax.axis_index("core")
    lead = (slice(None),) * core_axis
    out_refs[0][...] = all_ref[lead + (core,)]
    out_refs[1][...] = all_ref[lead + (1 - core,)].astype(BF16)


class Chain:
    def __init__(self):
        self.token = jnp.zeros((8, BLOCK), F32)

    def tie(self, *values):
        self.token, *values = lax.optimization_barrier((self.token, *values))
        return values


def call(chain, kernel, name, ins, outs, scratch=(), smem=0, flops=0, trans=0):
    size = sum(x.size * x.dtype.itemsize for x in ins)
    size += sum(x.size * jnp.dtype(x.dtype).itemsize for x in outs)
    count, made = len(ins), len(outs)

    def body(*refs):
        refs[count + 1 + made][...] = refs[count][...]
        kernel(*refs[:count], *refs[count + 1 : count + 1 + made], *refs[count + 2 + made :])

    results = pl.pallas_call(
        body,
        out_shape=(*outs, jax.ShapeDtypeStruct((8, BLOCK), F32)),
        in_specs=[pl.BlockSpec(memory_space=pltpu.SMEM)] * smem + vmem_specs(count - smem + 1),
        out_specs=tuple(vmem_specs(made + 1)),
        scratch_shapes=[pltpu.VMEM(shape, F32) for shape in scratch],
        compiler_params=pltpu.CompilerParams(vmem_limit_bytes=48 << 20),
        cost_estimate=pl.CostEstimate(flops=flops, transcendentals=trans, bytes_accessed=size),
        name=name,
    )(*ins, chain.token)
    chain.token = results[-1]
    return results[:-1]


def vmem_specs(count):
    return [pl.BlockSpec(memory_space=pltpu.VMEM)] * count


def project_kernel(wants, bias_row, count, *refs):
    x_refs, (w_ref, bias_ref), out_refs = refs[:count], refs[count : count + 2], refs[count + 2 :]
    rows = joined(x_refs)
    quarter = bias_ref.shape[1]
    out_refs = list(out_refs)
    if "q" in wants:
        value = matmul(rows, w_ref[:, :quarter]) + bias_ref[bias_row : bias_row + 1]
        out_refs.pop(0)[...] = value.astype(BF16) * BF16(HEAD**-0.5)
    if "k" in wants:
        out_ref = out_refs.pop(0)
        out_ref[:, :quarter] = matmul(rows, w_ref[:, quarter : 2 * quarter]).astype(BF16)
        value = matmul(rows, w_ref[:, 2 * quarter :]) + bias_ref[bias_row + 1 : bias_row + 2]
        out_ref[:, quarter:] = value.astype(BF16)


def project(chain, wants, bias_row, pieces, weight, biases):
    quarter = biases.shape[1]
    rows = BLOCK * len(pieces)
    outs = [jax.ShapeDtypeStruct((rows, quarter), BF16)] if "q" in wants else []
    if "k" in wants:
        outs.append(jax.ShapeDtypeStruct((rows, 2 * quarter), BF16))
    return call(
        chain,
        functools.partial(project_kernel, wants, bias_row, len(pieces)),
        "project_heads",
        [*pieces, weight, biases],
        outs,
        flops=2 * rows * weight.size,
    )


def attn_fwd_kernel(form, width, halves, count_ref, q_ref, wo_ref, *refs):
    kv_refs, (o_ref, lse_ref), out_refs = refs[:halves], refs[halves : halves + 2], refs[halves + 2 : -1]
    ot_ref = refs[-1]
    quarter = q_ref.shape[1]
    keys = sum(ref.shape[0] for ref in kv_refs)
    for chunk in range(q_ref.shape[0] // width):
        rows = slice(chunk * width, (chunk + 1) * width)
        mask = allowed_mask(form, count_ref, chunk * width, width, keys)
        for head in range(quarter // HEAD):
            cols = slice(head * HEAD, (head + 1) * HEAD)
            wide = slice(quarter + head * HEAD, quarter + (head + 1) * HEAD)
            key = jnp.concatenate([ref[:, cols] for ref in kv_refs], axis=0)
            value = jnp.concatenate([ref[:, wide] for ref in kv_refs], axis=0)
            scores = lax.dot_general(key, q_ref[rows, cols], NT, preferred_element_type=F32)
            scores = jnp.where(mask, scores, MASKED)
            peak = jnp.max(scores, axis=0, keepdims=True)
            weights = jnp.exp(scores - peak)
            total = jnp.sum(weights, axis=0, keepdims=True)
            probs = (weights * (1.0 / total)).astype(BF16)
            ot_ref[cols, rows] = lax.dot_general(value, probs, TN, preferred_element_type=F32)
            lse_ref[head : head + 1, rows] = peak + jnp.log(total)
    mixture = ot_ref[...].T.astype(BF16)
    o_ref[...] = mixture
    spread(matmul(mixture, wo_ref[...]), out_refs)


def attn_forward(chain, form, count, queries, kv, out_weight):
    rows, cols = queries.shape
    length = rows * len(kv)
    width = 256 if length <= 1024 else 128
    work = rows * length * cols
    outs = [jax.ShapeDtypeStruct((rows, cols), BF16), jax.ShapeDtypeStruct((8, rows), F32)]
    o, lse, *sent = call(
        chain,
        functools.partial(attn_fwd_kernel, form, width, len(kv)),
        "attn_forward",
        [count, queries, out_weight, *kv],
        outs + spread_shapes(out_weight.shape[1]),
        scratch=[(cols, rows)],
        smem=1,
        flops=8 * work,
        trans=work // HEAD,
    )
    return o, lse, sent


def attn_bwd_kernel(form, width, halves, split, count_ref, q_ref, wo_ref, o_ref, lse_ref, *refs):
    kv_refs, low_refs = refs[:halves], refs[halves : halves + 4]
    refs = refs[halves + 4 :]
    dq_ref, dkv_refs, w_refs = refs[0], refs[1 : 1 + halves], refs[1 + halves : -3]
    dqt_ref, do_ref, all_ref = refs[-3:]
    quarter = q_ref.shape[1]
    half = kv_refs[0].shape[0]
    keys = half * halves
    low = joined(low_refs)
    do_ref[...] = back_matmul(low, wo_ref[...])
    grad_w = outer_sum(o_ref[...], low)
    if split:
        all_ref[...] = grad_w.reshape(all_ref.shape)
        put_halves(all_ref, 1, w_refs)
    else:
        w_refs[0][...] = grad_w
    for chunk in range(q_ref.shape[0] // width):
        rows = slice(chunk * width, (chunk + 1) * width)
        mask = allowed_mask(form, count_ref, chunk * width, width, keys)
        for head in range(quarter // HEAD):
            cols = slice(head * HEAD, (head + 1) * HEAD)
            wide = slice(quarter + head * HEAD, quarter + (head + 1) * HEAD)
            key = jnp.concatenate([ref[:, cols] for ref in kv_refs], axis=0)
            value = jnp.concatenate([ref[:, wide] for ref in kv_refs], axis=0)
            query, grad = q_ref[rows, cols], do_ref[rows, cols].astype(BF16)
            scores = lax.dot_general(key, query, NT, preferred_element_type=F32)
            probs = jnp.where(mask, jnp.exp(scores - lse_ref[head : head + 1, rows]), 0.0)
            grad_probs = lax.dot_general(value, grad, NT, preferred_element_type=F32)
            product = probs * grad_probs
            delta = jnp.sum(product, axis=0, keepdims=True)
            grad_scores = (product - probs * delta).astype(BF16)
            grad_value = matmul(probs.astype(BF16), grad)
            grad_key = matmul(grad_scores, query)
            for j, ref in enumerate(dkv_refs):
                own = slice(j * half, (j + 1) * half)
                if chunk == 0:
                    ref[:, cols] = grad_key[own]
                    ref[:, wide] = grad_value[own]
                else:
                    ref[:, cols] += grad_key[own]
                    ref[:, wide] += grad_value[own]
            dqt_ref[cols, rows] = lax.dot_general(
                key, grad_scores, TN, preferred_element_type=F32
            ) * (HEAD**-0.5)
    dq_ref[...] = dqt_ref[...].T.astype(BF16)


def attn_backward(chain, form, split, count, queries, kv, low, out_weight, o, lse, view):
    rows, cols = queries.shape
    length = rows * len(kv)
    width = 256 if length <= 1024 else 128
    work = rows * length * cols
    halves = len(kv)
    outs = [jax.ShapeDtypeStruct((rows, cols), BF16)]
    outs += [jax.ShapeDtypeStruct((rows, 2 * cols), F32)] * halves
    outs += split_shapes(split, view, 1)
    dq, *rest = call(
        chain,
        functools.partial(attn_bwd_kernel, form, width, halves, split),
        "attn_backward",
        [count, queries, out_weight, o, lse, *kv, *low],
        outs,
        scratch=[(cols, rows), (rows, cols), view if split else (8, BLOCK)],
        smem=1,
        flops=20 * work,
        trans=work // HEAD,
    )
    return dq, rest[:halves], rest[halves:]


def project_back_kernel(cross, split, picks, *refs):
    count = 8 if cross else 4
    x_refs, (w_ref, dq_ref, own_ref, got_ref) = refs[:count], refs[count : count + 4]
    refs = refs[count + 4 :]
    made = len({source for source, _, _ in picks})
    vec_refs, out_refs, refs = refs[:made], refs[made : made + count], refs[made + count :]
    bias_ref, w_refs, all_ref = refs[0], refs[1:-1], refs[-1]
    quarter = dq_ref.shape[1]
    dq = dq_ref[...]
    dkv = (own_ref[...] + got_ref[...]).astype(BF16)
    bias_ref[...] = jnp.zeros_like(bias_ref)
    bias_ref[0:1] = jnp.sum(dq.astype(F32), axis=0, keepdims=True)
    bias_ref[1:2] = jnp.sum(dkv[:, quarter:].astype(F32), axis=0, keepdims=True)
    from_q = back_matmul(dq, w_ref[:, :quarter])
    from_kv = back_matmul(dkv, w_ref[:, quarter:])
    if cross:
        spread(from_q, out_refs[:4])
        spread(from_kv, out_refs[4:])
        rows_q, rows_kv = joined(x_refs[:4]), joined(x_refs[4:])
    else:
        spread(from_q + from_kv, out_refs)
        rows_q = rows_kv = joined(x_refs)
    grads = (
        (slice(0, quarter), outer_sum(rows_q, dq)),
        (slice(quarter, 3 * quarter), outer_sum(rows_kv, dkv)),
    )
    for cols, grad in grads:
        if split:
            all_ref[..., cols] = grad.reshape(all_ref.shape[:-1] + (grad.shape[-1],))
        else:
            w_refs[0][:, cols] = grad
    if split:
        part = 2 * lax.axis_index("y") + lax.axis_index("x")
        lines = [None] * 8
        for source, row, lane in picks:
            lines[lane] = vec_refs[source][row : row + 1]
        blank = jnp.zeros_like(vec_refs[0][0:1])
        lines = jnp.concatenate([blank if line is None else line for line in lines], axis=0)
        extra = slice(3 * quarter, 3 * quarter + 8)
        all_ref[..., 3 * quarter :] = jnp.zeros_like(all_ref[..., 3 * quarter :])
        all_ref[..., extra] = lines.T.reshape(all_ref.shape[:-1] + (8,))
        heads = slice(3 * quarter, 3 * quarter + 2)
        all_ref[part, :, :, :, heads] = bias_ref[...].T[:, :2].reshape(all_ref.shape[1:-1] + (2,))
        put_halves(all_ref, 2, w_refs)


def project_back(chain, cross, split, pieces, weight, dq, own, got, view, vecs, picks):
    rows, quarter = dq.shape
    width = weight.shape[0]
    outs = spread_shapes(width) * (2 if cross else 1)
    outs += [jax.ShapeDtypeStruct((8, quarter), F32)] + split_shapes(split, view, 2)
    results = call(
        chain,
        functools.partial(project_back_kernel, cross, split, picks),
        "project_back",
        [*pieces, weight, dq, own, got, *vecs],
        outs,
        scratch=[view if split else (8, BLOCK)],
        flops=4 * rows * weight.size,
    )
    count = len(pieces)
    return results[:count], results[count], results[count + 1 :]


def norm_kernel(bias_row, gain_row, shift_row, has_sent, base_ref, *refs):
    sent_refs, vec_ref, out_refs = refs[:4], refs[4], refs[5:]
    resid = base_ref[...].astype(F32) + vec_ref[bias_row : bias_row + 1]
    for ref in sent_refs:
        resid = resid + ref[...].astype(F32)
    out_refs[0][...] = resid
    gain, shift = vec_ref[gain_row : gain_row + 1], vec_ref[shift_row : shift_row + 1]
    value = layer_norm(resid, gain, shift)
    out_refs[1][...] = value
    out_refs[2][...] = value.astype(BF16)


def norm(chain, base, sent, vectors, bias_row, gain_row, shift_row):
    shape = base.shape
    return call(
        chain,
        functools.partial(norm_kernel, bias_row, gain_row, shift_row, True),
        "layer_norm",
        [base, *sent, vectors],
        [
            jax.ShapeDtypeStruct(shape, F32),
            jax.ShapeDtypeStruct(shape, F32),
            jax.ShapeDtypeStruct(shape, BF16),
        ],
    )


def norm_back_kernel(gain_row, count, *refs):
    grad_refs, (resid_ref, vec_ref), out_refs = refs[:count], refs[count : count + 2], refs[count + 2 :]
    grad = grad_refs[0][...].astype(F32)
    for ref in grad_refs[1:]:
        grad = grad + ref[...].astype(F32)
    resid = resid_ref[...]
    center = resid - jnp.mean(resid, axis=-1, keepdims=True)
    scale = lax.rsqrt(jnp.mean(center * center, axis=-1, keepdims=True) + EPSILON)
    unit = center * scale
    weighted = grad * vec_ref[gain_row : gain_row + 1]
    both = grad * unit
    first = jnp.mean(weighted, axis=-1, keepdims=True)
    second = jnp.mean(weighted * unit, axis=-1, keepdims=True)
    value = (weighted - first - unit * second) * scale
    low = value.astype(BF16)
    out_refs[0][...] = value
    out_refs[1][...] = low
    out_refs[2][...] = jnp.zeros_like(out_refs[2])
    for row, terms in enumerate((both, grad, low.astype(F32))):
        out_refs[2][row : row + 1] = jnp.sum(terms, axis=0, keepdims=True)


def norm_back(chain, grads, resid, vectors, gain_row):
    shape = resid.shape
    return call(
        chain,
        functools.partial(norm_back_kernel, gain_row, len(grads)),
        "layer_norm_back",
        [*grads, resid, vectors],
        [
            jax.ShapeDtypeStruct(shape, F32),
            jax.ShapeDtypeStruct(shape, BF16),
            jax.ShapeDtypeStruct((8, shape[1]), F32),
        ],
    )


def total_kernel(*refs):
    total = refs[0][...].astype(F32)
    for ref in refs[1:-1]:
        total = total + ref[...].astype(F32)
    refs[-1][...] = total.astype(BF16)


def rounded_total(chain, parts):
    (out,) = call(
        chain, total_kernel, "sum_parts", list(parts), [jax.ShapeDtypeStruct(parts[0].shape, BF16)]
    )
    return out


def normal_cdf(values):
    return 0.5 + 0.5 * lax.erf(values * (0.5**0.5))


def ffn_fwd_kernel(layer, y0, y1, y2, y3, up_ref, bias_ref, down_ref, *out_refs):
    rows = joined((y0, y1, y2, y3))
    hidden = up_ref.shape[1]
    total = None
    for cols in (slice(0, hidden // 2), slice(hidden // 2, hidden)):
        pre = matmul(rows, up_ref[:, cols]) + bias_ref[layer : layer + 1, cols]
        act = (pre * normal_cdf(pre)).astype(BF16)
        part = matmul(act, down_ref[cols])
        total = part if total is None else total + part
    spread(total, out_refs)


def ffn_forward(chain, layer, pieces, up, biases, down):
    return call(
        chain,
        functools.partial(ffn_fwd_kernel, layer),
        "ffn_forward",
        [*pieces, up, biases, down],
        spread_shapes(down.shape[1]),
        flops=16 * BLOCK * up.size,
        trans=4 * BLOCK * up.shape[1],
    )


def ffn_bwd_kernel(layer, split, *refs):
    rows, low = joined(refs[:4]), joined(refs[4:8])
    up_ref, bias_ref, down_ref = refs[8:11]
    out_refs = refs[11:15]
    up_all, down_all, bias_all = refs[-3:]
    if split:
        bias_refs, up_refs, down_refs = refs[15:17], refs[17:19], refs[19:21]
        bias_all[...] = jnp.zeros_like(bias_all)
    else:
        bias_refs, up_refs, down_refs = refs[15:16], refs[16:17], refs[17:18]
    hidden = up_ref.shape[1]
    total = None
    for c, cols in enumerate((slice(0, hidden // 2), slice(hidden // 2, hidden))):
        pre = matmul(rows, up_ref[:, cols]) + bias_ref[layer : layer + 1, cols]
        cdf = normal_cdf(pre)
        act = (pre * cdf).astype(BF16)
        slope = cdf + pre * (jnp.exp(-0.5 * pre * pre) * (2.0 * jnp.pi) ** -0.5)
        grad = (back_matmul(low, down_ref[cols]) * slope).astype(BF16)
        grad_bias = jnp.sum(grad.astype(F32), axis=0, keepdims=True)
        grad_down, grad_up = outer_sum(act, low), outer_sum(rows, grad)
        if split:
            down_all[c] = grad_down.reshape(down_all.shape[1:])
            up_all[..., cols] = grad_up.reshape(up_all.shape[:-1] + (hidden // 2,))
            size = down_all.shape[2]
            for z in range(4):
                bias_all[c, z, 0:1, :size] = grad_bias[:, z * size : (z + 1) * size]
        else:
            bias_refs[0][:, cols] = grad_bias
            down_refs[0][cols] = grad_down
            up_refs[0][:, cols] = grad_up
        part = back_matmul(grad, up_ref[:, cols])
        total = part if total is None else total + part
    spread(total, out_refs)
    if split:
        put_halves(up_all, 2, up_refs)
        put_halves(down_all, 0, down_refs)
        put_halves(bias_all, 0, bias_refs)


def ffn_backward(chain, layer, split, pieces, low, up, biases, down, up_view, down_view):
    hidden = up.shape[1]
    bias_view = (2, 4, 8, BLOCK) if split else (1, hidden)
    outs = spread_shapes(down.shape[1]) + split_shapes(split, bias_view, 0)
    outs += split_shapes(split, up_view, 2) + split_shapes(split, down_view, 0)
    tiny = (8, BLOCK)
    results = call(
        chain,
        functools.partial(ffn_bwd_kernel, layer, split),
        "ffn_backward",
        [*pieces, *low, up, biases, down],
        outs,
        scratch=[up_view, down_view, bias_view] if split else [tiny] * 3,
        flops=48 * BLOCK * up.size,
        trans=8 * BLOCK * hidden,
    )
    per = 2 if split else 1
    rest = results[4:]
    return results[:4], rest[:per], rest[per : 2 * per], rest[2 * per :]


def combine_kernel(count, *refs):
    out_ref = refs[-1]
    row = 0
    for keep_ref, got_ref in zip(refs[:count], refs[count:-1], strict=True):
        total = (keep_ref[...] + got_ref[...].astype(F32)).astype(BF16)
        _, size, cols = total.shape
        out_ref[:, row : row + size, :cols] = total
        if cols < out_ref.shape[2]:
            rest = jnp.zeros((total.shape[0], size, out_ref.shape[2] - cols), BF16)
            out_ref[:, row : row + size, cols:] = rest
        row += size


def combine(chain, keeps, gots, width):
    keeps = [x.reshape(x.shape[0], -1, x.shape[-1]) for x in keeps]
    gots = [x.reshape(x.shape[0], -1, x.shape[-1]) for x in gots]
    shape = (4, sum(x.shape[1] for x in keeps), width)
    (out,) = call(
        chain,
        functools.partial(combine_kernel, len(keeps)),
        "combine_gradients",
        [*keeps, *gots],
        [jax.ShapeDtypeStruct(shape, BF16)],
    )
    return out


def shares_kernel(keep_ref, got_ref, keep_out, got_out, *out_refs):
    group = lax.axis_index("z")
    cols, wide = keep_ref.shape[-1], out_refs[0].shape[-1]
    for k, ref in enumerate(out_refs):
        z = group ^ k
        ref[:4, :, :cols] = (keep_ref[z] + got_ref[z].astype(F32)).astype(ref.dtype)
        ref[:4, :, cols:] = jnp.zeros((4, ref.shape[1], wide - cols), ref.dtype)
        ref[4] = (keep_out[z] + got_out[z].astype(F32)).astype(ref.dtype)


def shares(chain, heads, out, width):
    shape = (5, heads[0].shape[2], width)
    return call(
        chain,
        shares_kernel,
        "group_shares",
        [*heads, *out],
        [jax.ShapeDtypeStruct(shape, F32)] + [jax.ShapeDtypeStruct(shape, BF16)] * 3,
    )


def join_heads(part_ref, col, out_ref):
    quarter = out_ref.shape[-1] // 4
    for j in range(3):
        for p in range(4):
            value = part_ref[p, :, col + j * quarter : col + (j + 1) * quarter]
            out_ref[j, :, p * quarter : (p + 1) * quarter] = value.astype(F32)


def join_up(part_ref, col, out_ref):
    size = out_ref.shape[1] // 32
    for z in range(4):
        for p in range(4):
            for c in range(2):
                start = ((z * 4 + p) * 2 + c) * size
                first = col + (c * 4 + z) * size
                out_ref[:, start : start + size] = part_ref[p, :, first : first + size].astype(F32)


def join_lines(part_ref, col, out_ref):
    total = part_ref[0, :, col : col + BLOCK].astype(F32)
    for p in (1, 2, 3):
        total = total + part_ref[p, :, col : col + BLOCK].astype(F32)
    out_ref[...] = total.T[:8]


def join_layer_kernel(heads_out, part_ref, up_ref, heads_ref, line_ref):
    hidden = part_ref.shape[-1] - heads_out - BLOCK
    join_up(part_ref, 0, up_ref)
    join_heads(part_ref, hidden, heads_ref)
    join_lines(part_ref, hidden + heads_out, line_ref)


def join_layer(chain, parts, heads_out):
    _, rows, _ = parts.shape
    return call(
        chain,
        functools.partial(join_layer_kernel, heads_out),
        "join_gradients",
        [parts],
        [
            jax.ShapeDtypeStruct((rows, 128 * rows), F32),
            jax.ShapeDtypeStruct((3, rows, 32 * rows), F32),
            jax.ShapeDtypeStruct((8, rows), F32),
        ],
    )


def join_last_kernel(heads_out, part_ref, cross_ref, self_ref, heads_ref, *refs):
    line_ref = refs[-1]
    join_heads(part_ref, 0, heads_ref)
    join_lines(part_ref, heads_out, line_ref)
    lines = {"e": line_ref, "s": self_ref, "c": cross_ref}
    for ref, picks in zip(refs[:-1], LINES, strict=True):
        for row, (name, line) in enumerate(picks):
            ref[row : row + 1] = lines[name][line : line + 1]


LINES = (
    (("e", 0), ("e", 1), ("e", 2)),
    (("s", 3),),
    (("e", 4), ("s", 6)),
    (("e", 5), ("s", 7)),
    (("s", 0), ("s", 1), ("s", 2)),
    (("c", 0), ("c", 1), ("c", 2)),
    (("c", 3),),
    (("s", 4), ("c", 6), ("c", 4)),
    (("s", 5), ("c", 7), ("c", 5)),
)


def join_last(chain, parts, cross_lines, self_lines, heads_out):
    _, rows, _ = parts.shape
    return call(
        chain,
        functools.partial(join_last_kernel, heads_out),
        "join_gradients",
        [parts, cross_lines, self_lines],
        [jax.ShapeDtypeStruct((3, rows, 32 * rows), F32)]
        + [jax.ShapeDtypeStruct((len(picks), rows), F32) for picks in LINES],
        scratch=[(8, rows)],
    )


def place_kernel(plan, turned, mine_ref, other_ref, *out_refs):
    group, core = lax.axis_index("z"), lax.axis_index("core")
    for piece_ref, c in ((mine_ref, core), (other_ref, 1 - core)):
        for k in range(4):
            z = group ^ k if turned else k
            for (kind, row, col), out_ref in zip(plan, out_refs, strict=True):
                count, cols = out_ref.shape[-2:]
                for p in range(4 if kind == "rows" else 1):
                    first = row + p * count
                    value = piece_ref[k, first : first + count, col : col + cols]
                    if kind == "rows":
                        out_ref[z, p, c] = value
                    elif kind == "down":
                        out_ref[c, z] = value
                    else:
                        out_ref[z, c] = value


def place(chain, plan, shapes, turned, mine, other):
    lead = {"rows": (4, 4, 2), "down": (2, 4), "out": (4, 2)}
    outs = call(
        chain,
        functools.partial(place_kernel, plan, turned),
        "place_weights",
        [mine, other],
        [
            jax.ShapeDtypeStruct(lead[entry[0]] + shape, mine.dtype)
            for entry, shape in zip(plan, shapes, strict=True)
        ],
    )
    return [out.reshape(-1, out.shape[-1]) for out in outs]


def place_first_kernel(
    cols, count, mine_ref, other_ref, w_ref, out_w_ref, vec_ref, up_ref, part_ref, all_ref
):
    group, core = lax.axis_index("z"), lax.axis_index("core")
    part = 2 * lax.axis_index("y") + lax.axis_index("x")
    for piece_ref, c in ((mine_ref, core), (other_ref, 1 - core)):
        for k in range(4):
            for p in range(4):
                w_ref[group ^ k, p, c] = piece_ref[k, p, :, :cols]
                all_ref[group ^ k, p, c] = piece_ref[k, p, :, cols:].astype(F32)
            out_w_ref[group ^ k, c] = piece_ref[k, 4]
    rows = all_ref.shape[3]
    rows_ff = 4 * rows
    for z in range(4):
        for p in range(4):
            for c in range(2):
                start = ((z * 4 + p) * 2 + c) * rows
                vec_ref[:, start : start + rows] = all_ref[z, p, c, :, :rows]
    for c in range(2):
        for z in range(4):
            start = (c * 4 + z) * rows_ff
            up_ref[:, start : start + rows_ff] = all_ref[z, part, c, count : count + 2, :rows_ff]
    for p in range(4):
        for c in range(2):
            start = (p * 2 + c) * rows
            part_ref[:, start : start + rows] = all_ref[part, p, c, :, :rows]


def place_first(chain, mine, other, cols, count):
    _, _, rows, wide = mine.shape
    width = 32 * rows
    return call(
        chain,
        functools.partial(place_first_kernel, cols, count),
        "place_first_weights",
        [mine, other],
        [
            jax.ShapeDtypeStruct((4, 4, 2, rows, cols), mine.dtype),
            jax.ShapeDtypeStruct((4, 2, rows, wide), mine.dtype),
            jax.ShapeDtypeStruct((rows, width), F32),
            jax.ShapeDtypeStruct((2, 32 * rows), F32),
            jax.ShapeDtypeStruct((rows, 8 * rows), F32),
        ],
        scratch=[(4, 4, 2, rows, wide - cols)],
    )


def plane_swap(values, shift):
    return lax.ppermute(values, PLANE, [(i, i ^ shift) for i in range(4)])


def z_swap(values, shift):
    groups = lax.axis_size("z")
    return lax.ppermute(values, "z", [(z, z ^ shift) for z in range(groups)])


def core_swap(values):
    return lax.ppermute(values, "core", [(0, 1), (1, 0)])


def plane_gather(values):
    return [values] + [plane_swap(values, k) for k in (1, 2, 3)]


def tie(*values):
    return lax.optimization_barrier(values)


def plane_send(spreads):
    return [spreads[0]] + [plane_swap(spreads[k], k) for k in (1, 2, 3)]


def plane_total(sent):
    total = sent[0]
    for part in sent[1:]:
        total = total + part.astype(F32)
    return total


class Layout:
    def __init__(self, groups, rows):
        self.groups = groups
        self.devices = groups * 8
        self.subs = groups // rows

    def index(self, z, y, x, c):
        return ((z * 2 + y) * 2 + x) * 2 + c

    def token_moves(self):
        moves = []
        for z in range(self.groups):
            for y in range(2):
                for x in range(2):
                    for c in range(2):
                        row, block = 2 * x + c, 2 * z + y
                        group, within = row * self.subs + block // 8, block % 8
                        core, part = within // 4, within % 4
                        moves.append(
                            (self.index(z, y, x, c), self.index(group, part // 2, part % 2, core))
                        )
        return moves

    def back_moves(self):
        return [(b, a) for a, b in self.token_moves()]

    def turn_moves(self):
        moves = []
        for part in range(4):
            for z in range(self.groups):
                owner, user = part * self.groups + z, z * 4 + part
                moves.append((owner, user))
        return moves


def on_device(lay, core, part, sub, params, tokens):
    (
        enc_qkv,
        enc_out_w,
        enc_attn_bias,
        enc_up,
        enc_up_bias,
        enc_down,
        enc_down_bias,
        enc_gains,
        enc_shifts,
        self_qkv,
        self_out,
        self_bias,
        cross_qkv,
        cross_out,
        cross_bias,
        dec_up,
        dec_up_bias,
        dec_down,
        dec_down_bias,
        dec_gains,
        dec_shifts,
    ) = params
    src, tgt, src_seg, tgt_seg, out_grad = tokens
    groups = lay.groups
    width = src.shape[1]
    rows = enc_out_w.shape[0]
    rows_ff = enc_down.shape[0]
    quarter = width // 4
    hidden = rows_ff * groups * 2
    heads_out = enc_qkv.shape[0] * quarter

    chain = Chain()
    split = groups == 4
    ids = jnp.concatenate([src_seg, tgt_seg]).astype(BF16)
    ids = jnp.pad(ids[None], ((0, 7), (0, width - 2 * BLOCK)))
    packed = lax.ppermute(jnp.concatenate([src, ids], axis=0), AXES, lay.token_moves())

    def heads_split(qkv):
        parts = qkv.reshape(3, rows, 4, quarter)
        return parts.transpose(2, 1, 0, 3).reshape(4, rows, heads_out)

    def up_split(up):
        parts = up.reshape(rows, groups, 4, 2, rows_ff)
        return parts.transpose(2, 0, 3, 1, 4).reshape(4, rows, hidden)

    def both_cores(mine, axis):
        other = core_swap(mine)
        shape = [1] * (mine.ndim + 1)
        shape[axis] = 2
        which = lax.broadcasted_iota(jnp.int32, shape, axis) == core
        return jnp.where(which, jnp.expand_dims(mine, axis), jnp.expand_dims(other, axis))

    def whole(kind, piece):
        cols = piece.shape[-1]
        piece = lax.all_gather(piece, "z", axis=0)
        return both_cores(piece, {"rows": 2, "down": 0, "out": 1}[kind]).reshape(-1, cols)

    def plane_turn(values):
        return lax.all_to_all(values, PLANE, split_axis=0, concat_axis=0, tiled=True)

    def out_turn(values):
        return lax.ppermute(values, ("z", "y", "x"), lay.turn_moves())

    vectors = jnp.concatenate(
        [
            enc_attn_bias,
            self_bias,
            cross_bias,
            enc_down_bias[None],
            dec_down_bias[None],
            enc_gains,
            dec_gains,
            enc_shifts,
            dec_shifts,
        ],
        axis=0,
    )
    vector_count = vectors.shape[0]
    if split:
        wide = width - heads_out
        extra = jnp.concatenate(
            [
                jnp.pad(vectors, ((0, 0), (0, wide - rows))),
                jnp.pad(jnp.stack([enc_up_bias, dec_up_bias]), ((0, 1), (0, wide - rows_ff))),
            ],
            axis=0,
        )
        extra = jnp.broadcast_to(extra[None], (4, rows, wide))
        pieces = plane_turn(
            jnp.concatenate(
                [
                    heads_split(enc_qkv),
                    extra,
                    heads_split(self_qkv),
                    heads_split(cross_qkv),
                    up_split(enc_up),
                    up_split(dec_up),
                ],
                axis=2,
            )
        )
        outs = out_turn(jnp.concatenate([enc_out_w, self_out, cross_out], axis=0))
        pieces, packed = tie(pieces, packed)
        first = jnp.concatenate([pieces[:, :, :width], outs[None, :rows]], axis=0)
        first = jnp.stack([first] + [z_swap(first, k) for k in (1, 2, 3)])
        rest = pieces[:, :, width:].reshape(4 * rows, -1)
        narrow = ((0, 0), (0, width - heads_out))
        w_self = jnp.pad(rest[:, :heads_out], narrow)
        w_cross = jnp.pad(rest[:, heads_out : 2 * heads_out], narrow)
        up = rest[:, 2 * heads_out : 2 * heads_out + hidden]
        one = jnp.concatenate([up, enc_down, outs[rows:], w_self], axis=0)
        one = lax.all_gather(one, "z", axis=0)
        up = rest[:, 2 * heads_out + hidden :]
        two = jnp.concatenate([up, dec_down, w_cross], axis=0)
        two = lax.all_gather(two, "z", axis=0)
        ffn_plan = [("rows", 0, 0), ("down", 4 * rows, 0)]
        ffn_shapes = [(rows, hidden), (rows_ff, width)]
        row = 4 * rows + rows_ff

    src = packed[:BLOCK]
    blocks = [packed] + [plane_swap(packed, k) for k in (1, 2, 3)]
    src_rows = [block[:BLOCK] for block in blocks]
    doc = jnp.concatenate([block[BLOCK : BLOCK + 1] for block in blocks], axis=0)
    doc = doc[:, : 2 * BLOCK].astype(F32).reshape(4, 2, BLOCK)
    count = jnp.stack(
        [
            jnp.sum((doc < 0.5).astype(F32), axis=(0, 2)),
            jnp.sum((doc < 1.5).astype(F32), axis=(0, 2)),
        ]
    )
    count = jnp.pad(count, ((0, 6), (0, BLOCK - 2)))
    count = count + core_swap(count)
    total = count
    for j in range(1, lay.subs):
        total = total + z_swap(count, j)
    count = total.astype(jnp.int32)

    if split:
        w_enc, wo_enc, vectors, ups, mine = place_first(
            chain, first, core_swap(first), heads_out, vector_count
        )
        w_enc, wo_enc = w_enc.reshape(width, heads_out), wo_enc.reshape(quarter, width)
    else:
        w_enc = whole("rows", plane_turn(heads_split(enc_qkv)))
        vectors = jnp.concatenate([vectors.reshape(-1), enc_up_bias, dec_up_bias])[None]
        vectors = lax.all_gather(vectors, AXES, axis=0, tiled=True).astype(F32)
        ups = vectors[:, vector_count * rows :].reshape(groups, 4, 2, 2, rows_ff)
        ups = lax.dynamic_index_in_dim(ups, part, axis=1, keepdims=False)
        ups = ups.transpose(2, 1, 0, 3).reshape(2, hidden)
        vectors = vectors[:, : vector_count * rows].reshape(lay.devices, vector_count, rows)
        vectors = vectors.transpose(1, 0, 2).reshape(vector_count, width)
        mine = lax.dynamic_slice_in_dim(vectors, part * quarter, quarter, axis=1)
        w_self = whole("rows", plane_turn(heads_split(self_qkv)))
        outs = out_turn(jnp.concatenate([enc_out_w, self_out, cross_out], axis=1))
        outs = whole("out", outs)
        wo_enc, wo_self, wo_cross = (outs[:, k * width : (k + 1) * width] for k in range(3))
        w_up_enc = whole("rows", plane_turn(up_split(enc_up)))
        w_down_enc = whole("down", enc_down)
        w_cross = whole("rows", plane_turn(heads_split(cross_qkv)))
        w_up_dec = whole("rows", plane_turn(up_split(dec_up)))
        w_down_dec = whole("down", dec_down)

    row_view = (4, 4, 2, rows)

    def with_others(kv):
        kv = [kv, core_swap(kv)]
        return kv + [z_swap(half, j) for j in range(1, lay.subs) for half in kv]

    def own_part(halves):
        own, other = halves[:2]
        for j in range(1, lay.subs):
            own = own + z_swap(halves[2 * j], j)
            other = other + z_swap(halves[2 * j + 1], j)
        return own, core_swap(other)

    enc_form, self_form, cross_form = (0, 0, False), (1, 1, True), (1, 0, False)
    q_enc, kv_enc = project(chain, "qk", 0, src_rows, w_enc, mine)
    kv_enc = with_others(kv_enc)
    kv_enc, tgt = tie(kv_enc, tgt)
    tgt = lax.ppermute(tgt, AXES, lay.token_moves())
    o_enc, lse_enc, sent = attn_forward(chain, enc_form, count, q_enc, kv_enc, wo_enc)
    sent = plane_send(sent)
    sent, tgt = tie(sent, tgt)
    r_enc1, e1, e1_low = norm(chain, src, sent, vectors, 2, 11, 16)
    e1_rows = plane_gather(e1_low)
    if split:
        e1_rows, one = tie(e1_rows, one)
        w_up_enc, w_down_enc, wo_self, wo_cross, w_self = place(
            chain,
            ffn_plan + [("out", row, 0), ("out", row + rows, 0), ("rows", row + 2 * rows, 0)],
            ffn_shapes + [(rows, width)] * 2 + [(rows, heads_out)],
            False,
            one,
            core_swap(one),
        )
    e1_rows, tgt = tie(e1_rows, tgt)
    tgt_rows = plane_gather(tgt)
    sent = plane_send(ffn_forward(chain, 0, e1_rows, w_up_enc, ups, w_down_enc))
    q_self, kv_self = project(chain, "qk", 3, tgt_rows, w_self, mine)
    kv_self = with_others(kv_self)
    o_self, lse_self, self_sent = attn_forward(chain, self_form, count, q_self, kv_self, wo_self)
    r_enc2, encoded, encoded_low = norm(chain, e1, sent, vectors, 9, 12, 17)
    self_sent = plane_send(self_sent)
    encoded_rows = plane_gather(encoded_low)
    r_dec1, t1, t1_low = norm(chain, tgt, self_sent, vectors, 5, 13, 18)
    t1_rows = plane_gather(t1_low)
    if split:
        encoded_rows, two = tie(encoded_rows, two)
        w_up_dec, w_down_dec, w_cross = place(
            chain,
            ffn_plan + [("rows", row, 0)],
            ffn_shapes + [(rows, heads_out)],
            False,
            two,
            core_swap(two),
        )
    (kv_cross,) = project(chain, "k", 6, encoded_rows, w_cross, mine)
    kv_cross = with_others(kv_cross)
    (q_cross,) = project(chain, "q", 6, t1_rows, w_cross, mine)
    q_cross, out_grad = tie(q_cross, out_grad)
    out_grad = lax.ppermute(out_grad, AXES, lay.token_moves())
    o_cross, lse_cross, sent = attn_forward(chain, cross_form, count, q_cross, kv_cross, wo_cross)
    r_dec2, t2, t2_low = norm(chain, t1, plane_send(sent), vectors, 8, 14, 19)
    t2_rows = plane_gather(t2_low)
    sent = plane_send(ffn_forward(chain, 1, t2_rows, w_up_dec, ups, w_down_dec))
    sent, out_grad = tie(sent, out_grad)
    r_dec3, _, t3_low = norm(chain, t2, sent, vectors, 10, 15, 20)

    heads_view = row_view + (heads_out + BLOCK,)
    up_view = row_view + (hidden,)
    down_view = (2, 4, rows_ff, width)
    out_view = (4, 2, rows, width)
    if not split:
        heads_view, up_view = (width, heads_out), (width, hidden)
        down_view, out_view = (hidden, width), (quarter, width)

    def core_send(grad, kind):
        if split:
            return grad[0], core_swap(grad[1])
        axis = {"rows": 2, "down": 0, "out": 1}[kind]
        shape = {
            "rows": (groups, 4, 2, rows, -1),
            "down": (2, groups, rows_ff, width),
            "out": (groups, 2, rows, width),
        }[kind]
        grad = grad[0].reshape(shape)
        zero = lax.index_in_dim(grad, 0, axis, keepdims=False)
        one = lax.index_in_dim(grad, 1, axis, keepdims=False)
        send = jnp.where(core == 0, one, zero).astype(BF16)
        return jnp.where(core == 0, zero, one), core_swap(send)

    def stacked(*sends):
        keeps, gots = [x[0] for x in sends], [x[1] for x in sends]
        if split:
            return combine(chain, keeps, gots, width)
        sums = []
        for keep, got in zip(keeps, gots, strict=True):
            total = (keep + got.astype(F32)).astype(BF16)
            total = total.reshape(groups, -1, total.shape[-1])
            sums.append(jnp.pad(total, ((0, 0), (0, 0), (0, width - total.shape[-1]))))
        return jnp.concatenate(sums, axis=1)

    def z_reduce(grad):
        return lax.psum_scatter(grad, "z", scatter_dimension=0, tiled=False)

    def ffn_sends(bias, up, down):
        sends = [core_send(up, "rows"), core_send(down, "down")]
        if split:
            sends.append(core_send(bias, "bias"))
        return sends

    d_r3, low3, sums3 = norm_back(chain, [out_grad], r_dec3, vectors, 15)
    spreads, *grads = ffn_backward(
        chain, 1, split, t2_rows, plane_gather(low3), w_up_dec, ups, w_down_dec, up_view, down_view
    )
    upb_dec = grads[0]
    sent = plane_send(spreads)
    sends = ffn_sends(*grads)
    sent, sends = tie(sent, sends)
    d_r2, low2, sums2 = norm_back(chain, [d_r3, *sent], r_dec2, vectors, 14)

    low2_rows = plane_gather(low2)
    dec_ffn = z_reduce(stacked(*sends))
    dq, dkv, g_wo_cross = attn_backward(
        chain,
        cross_form,
        split,
        count,
        q_cross,
        kv_cross,
        low2_rows,
        wo_cross,
        o_cross,
        lse_cross,
        out_view,
    )
    spreads, g_bias_cross, g_cross = project_back(
        chain,
        True,
        split,
        t1_rows + encoded_rows,
        w_cross,
        dq,
        *own_part(dkv),
        heads_view,
        [sums2, sums3],
        ((0, 2, 2), (1, 2, 3), (1, 0, 4), (1, 1, 5), (0, 0, 6), (0, 1, 7)),
    )
    sent = plane_send(spreads[4:])
    sends = [core_send(g_cross, "rows"), core_send(g_wo_cross, "out")]
    sent, sends = tie(sent, sends)

    d_e2, low_e2, sums_e2 = norm_back(chain, sent, r_enc2, vectors, 12)
    low_e2_rows = plane_gather(low_e2)
    d_t1_sent = plane_send(spreads[:4])
    cross = z_reduce(stacked(*sends))
    spreads, *grads = ffn_backward(
        chain, 0, split, e1_rows, low_e2_rows, w_up_enc, ups, w_down_enc, up_view, down_view
    )
    upb_enc = grads[0]
    sent = plane_send(spreads)
    d_r1, low1, sums1 = norm_back(chain, [d_r2, *d_t1_sent], r_dec1, vectors, 13)
    sends = ffn_sends(*grads)
    sent, sends = tie(sent, sends)
    low1_rows = plane_gather(low1)
    d_r1e, low_e1, sums_e1 = norm_back(chain, [d_e2, *sent], r_enc1, vectors, 11)

    low_e1_rows = plane_gather(low_e1)
    enc_ffn = z_reduce(stacked(*sends))
    dq_self, dkv_self, g_wo_self = attn_backward(
        chain,
        self_form,
        split,
        count,
        q_self,
        kv_self,
        low1_rows,
        wo_self,
        o_self,
        lse_self,
        out_view,
    )
    dq_enc, dkv_enc, g_wo_enc = attn_backward(
        chain,
        enc_form,
        split,
        count,
        q_enc,
        kv_enc,
        low_e1_rows,
        wo_enc,
        o_enc,
        lse_enc,
        out_view,
    )
    spreads_self, g_bias_self, g_self = project_back(
        chain,
        False,
        split,
        tgt_rows,
        w_self,
        dq_self,
        *own_part(dkv_self),
        heads_view,
        [sums1, sums_e2],
        ((0, 2, 2), (1, 2, 3), (0, 0, 4), (0, 1, 5), (1, 0, 6), (1, 1, 7)),
    )
    spreads, g_bias_enc, g_enc = project_back(
        chain,
        False,
        split,
        src_rows,
        w_enc,
        dq_enc,
        *own_part(dkv_enc),
        heads_view,
        [sums_e1],
        ((0, 2, 2), (0, 0, 4), (0, 1, 5)),
    )
    g_enc, g_wo_enc = core_send(g_enc, "rows"), core_send(g_wo_enc, "out")
    sent = plane_send(spreads)
    self_sent = plane_send(spreads_self)
    self_sends = [core_send(g_self, "rows"), core_send(g_wo_self, "out")]

    if split:
        parts = shares(chain, g_enc, g_wo_enc, width)
        parts = [parts[0]] + [z_swap(parts[k], k) for k in (1, 2, 3)]
        own_self = z_reduce(stacked(*self_sends))
        src_low = rounded_total(chain, [d_r1e, *sent])
        tgt_low = rounded_total(chain, [d_r1, *self_sent])
        dec_parts = jnp.concatenate(
            [
                dec_ffn[: 4 * rows].reshape(4, rows, hidden),
                cross[: 4 * rows, : heads_out + BLOCK].reshape(4, rows, heads_out + BLOCK),
            ],
            axis=2,
        )
        g_dec_up, g_cross_qkv, cross_lines = join_layer(chain, plane_turn(dec_parts), heads_out)
        enc_parts = jnp.concatenate(
            [
                enc_ffn[: 4 * rows].reshape(4, rows, hidden),
                own_self[: 4 * rows, : heads_out + BLOCK].reshape(4, rows, heads_out + BLOCK),
            ],
            axis=2,
        )
        last = rounded_total(chain, parts)
        g_enc_up, g_self_qkv, self_lines = join_layer(chain, plane_turn(enc_parts), heads_out)
        outs = jnp.concatenate([last[4], own_self[4 * rows :], cross[4 * rows :]], axis=0)
        outs = lax.ppermute(outs, ("z", "y", "x"), [(b, a) for a, b in lay.turn_moves()])
        outs = outs.astype(F32)
        g_enc_qkv, *small = join_last(
            chain, plane_turn(last[:4]), cross_lines, self_lines, heads_out
        )
        small = [x[0] if x.shape[0] == 1 else x for x in small]
        tail = 4 * rows + rows_ff
        g_upb_enc, g_upb_dec = (x[tail, :rows_ff].astype(F32) for x in (enc_ffn, dec_ffn))
        g_enc_down, g_dec_down = (x[4 * rows : tail].astype(F32) for x in (enc_ffn, dec_ffn))
    else:

        def heads_join(parts):
            parts = plane_turn(parts[:, :heads_out].reshape(4, rows, heads_out))
            parts = parts.reshape(4, rows, 3, quarter).transpose(2, 1, 0, 3)
            return parts.reshape(3, rows, width).astype(F32)

        def up_join(parts):
            parts = plane_turn(parts.reshape(4, rows, hidden))
            parts = parts.reshape(4, rows, 2, groups, rows_ff).transpose(1, 3, 0, 2, 4)
            return parts.reshape(rows, -1).astype(F32)

        src_low = plane_total([d_r1e + sent[0], *sent[1:]]).astype(BF16)
        tgt_low = plane_total([d_r1 + self_sent[0], *self_sent[1:]]).astype(BF16)
        own_self = z_reduce(stacked(*self_sends))
        last = z_reduce(stacked(g_enc, g_wo_enc))
        g_dec_up, g_enc_up = up_join(dec_ffn[: 4 * rows]), up_join(enc_ffn[: 4 * rows])
        g_enc_down, g_dec_down = (x[4 * rows :].astype(F32) for x in (enc_ffn, dec_ffn))
        g_cross_qkv, g_self_qkv, g_enc_qkv = (
            heads_join(x[: 4 * rows]) for x in (cross, own_self, last)
        )
        outs = jnp.concatenate([x[4 * rows :] for x in (last, own_self, cross)], axis=0)
        outs = lax.ppermute(outs, ("z", "y", "x"), [(b, a) for a, b in lay.turn_moves()])
        outs = outs.astype(F32)
        placed = jnp.concatenate([g_bias_enc[:2], g_bias_self[:2], g_bias_cross[:2]], axis=0)
        placed = lax.dynamic_update_slice(
            jnp.zeros((6, width), F32), placed, (jnp.int32(0), part * quarter)
        )
        lines = jnp.concatenate(
            [placed, sums_e1[:3], sums_e2[:3], sums1[:3], sums2[:3], sums3[:3]], axis=0
        )
        line_count = lines.shape[0]
        lines = lines.reshape(line_count, lay.devices, rows).transpose(1, 0, 2)
        lines = lines.reshape(lay.devices, line_count * rows)
        upb = jnp.concatenate([upb_enc[0], upb_dec[0]]).reshape(2, 2, groups, rows_ff)
        upb = lax.dynamic_update_slice(
            jnp.zeros((groups, 4, 2, 2, rows_ff), F32),
            upb.transpose(2, 1, 0, 3)[:, None],
            (jnp.int32(0), part, jnp.int32(0), jnp.int32(0), jnp.int32(0)),
        )
        lines = jnp.concatenate([lines, upb.reshape(lay.devices, 2 * rows_ff)], axis=1)
        lines = lax.all_to_all(lines, AXES, split_axis=0, concat_axis=0, tiled=True)
        lines = jnp.sum(lines, axis=0)
        upb = lines[line_count * rows :]
        g_upb_enc, g_upb_dec = upb[:rows_ff], upb[rows_ff:]
        lines = lines[: line_count * rows].reshape(line_count, rows)
        small = [
            jnp.stack([lines[0], lines[1], lines[8]]),
            lines[11],
            jnp.stack([lines[6], lines[9]]),
            jnp.stack([lines[7], lines[10]]),
            jnp.stack([lines[2], lines[3], lines[14]]),
            jnp.stack([lines[4], lines[5], lines[17]]),
            lines[20],
            jnp.stack([lines[12], lines[15], lines[18]]),
            jnp.stack([lines[13], lines[16], lines[19]]),
        ]
    g_enc_out, g_self_out, g_cross_out = outs[:rows], outs[rows : 2 * rows], outs[2 * rows :]

    def home(values):
        return lax.ppermute(values, AXES, lay.back_moves())

    bias_enc, down_enc, gains_enc, shifts_enc = small[:4]
    bias_self, bias_cross, down_dec, gains_dec, shifts_dec = small[4:]
    return (
        home(t3_low)[None],
        home(src_low).astype(F32)[None],
        home(tgt_low).astype(F32)[None],
        g_enc_qkv,
        g_enc_out,
        bias_enc,
        g_enc_up,
        g_upb_enc,
        g_enc_down,
        down_enc,
        gains_enc,
        shifts_enc,
        g_self_qkv,
        g_self_out,
        bias_self,
        g_cross_qkv,
        g_cross_out,
        bias_cross,
        g_dec_up,
        g_upb_dec,
        g_dec_down,
        down_dec,
        gains_dec,
        shifts_dec,
    )


def solution(mesh):
    groups = mesh.shape["seq"] // 2
    rows = mesh.shape["dp"]
    lay = Layout(groups, rows)
    fine = Mesh(mesh.devices.reshape(groups, 2, 2, 2), AXES)
    seq, dp = ("z", "y"), ("x", "core")

    def run(
        src,
        tgt,
        src_seg,
        tgt_seg,
        enc_qkv,
        enc_out_w,
        enc_attn_bias,
        enc_up,
        enc_up_bias,
        enc_down,
        enc_down_bias,
        enc_gains,
        enc_shifts,
        self_qkv,
        self_out,
        self_bias,
        cross_qkv,
        cross_out,
        cross_bias,
        dec_up,
        dec_up_bias,
        dec_down,
        dec_down_bias,
        dec_gains,
        dec_shifts,
        out_grad,
    ):
        core = lax.axis_index("core")
        part = 2 * lax.axis_index("y") + lax.axis_index("x")
        sub = lax.axis_index("z") % lay.subs
        params = (
            enc_qkv,
            enc_out_w,
            enc_attn_bias,
            enc_up,
            enc_up_bias,
            enc_down,
            enc_down_bias,
            enc_gains,
            enc_shifts,
            self_qkv,
            self_out,
            self_bias,
            cross_qkv,
            cross_out,
            cross_bias,
            dec_up,
            dec_up_bias,
            dec_down,
            dec_down_bias,
            dec_gains,
            dec_shifts,
        )
        return on_device(
            lay, core, part, sub, params, (src[0], tgt[0], src_seg[0], tgt_seg[0], out_grad[0])
        )

    token = P(dp, seq, None)
    ids = P(dp, seq)
    stack = P(None, AXES, None)
    mat = P(AXES, None)
    vecs = P(None, AXES)
    vec = P(AXES)
    in_specs = (
        (token, token, ids, ids)
        + (stack, mat, vecs, mat, vec, mat, vec, vecs, vecs)
        + (stack, mat, vecs, stack, mat, vecs, mat, vec, mat, vec, vecs, vecs)
        + (token,)
    )
    out_specs = (
        (token, token, token)
        + (stack, mat, vecs, mat, vec, mat, vec, vecs, vecs)
        + (stack, mat, vecs, stack, mat, vecs, mat, vec, mat, vec, vecs, vecs)
    )
    return jax.shard_map(run, mesh=fine, in_specs=in_specs, out_specs=out_specs, check_vma=False)
```

time: 742 us -> 535 us (0.72)
  blocking collectives: 159 us -> 0 us
  matrix products: 67.4 us -> 0 us
  Pallas kernels: 37.5 us -> 101 us
  other arithmetic: 69.1 us -> 11.2 us
  waiting for transfers between devices: 151 us -> 185 us
  local copies, waits for them, and re-layouts: 80.5 us -> 57.4 us
  starting transfers between devices: 150 us -> 159 us
    all_gather x6 -> x0, blocking collectives: 112 us -> none  [the longest x3 59.3 us: whole_rows(): split = lax.all_gather(split, 'z', axis=0)]
    dot_general x46 -> x0, matrix products: 67.4 us -> none  [the longest x18 26.5 us: matmul(): return jnp.dot(left, right, preferred_element_type=F32)]
    pallas_call x6 -> x41, Pallas kernels: 37.5 us -> 101 us  [call(): pl.pallas_call(body, out_shape=(*outs, jax.ShapeDtypeStruct((8, BLOCK), F...]
    unnamed x1 -> x0, blocking collectives: 46.4 us -> none
    convert_element_type x33 -> x5, other arithmetic: 33.9 us -> 6 us  [the longest x2 3.55 us: on_device(): x[4 * rows:tail].astype(F32)]
    unnamed x459 -> x293, local copies, waits for them, and re-layouts: 20.4 us -> 47.1 us
    ppermute x63 -> x66, waiting for transfers between devices: 116 us -> 140 us  [plane_swap(): return lax.ppermute(values, PLANE, [(i, i ^ shift) for i in range(4)])]
    all_to_all x9 -> x4, starting transfers between devices: 47.9 us -> 25.6 us  [plane_turn(): lax.all_to_all(values, PLANE, split_axis=0, concat_axis=0, tiled=True)]
  transfers between devices with their start and end apart: 114 -> 112, of which waited for: 44 -> 50; matrix products, arithmetic and copies ran while one was open for 23% -> 3% of each run, Pallas kernels for 3% -> 13%
where the time goes in v2:
time: 535 us; the launch traced here: 530 us
  waiting for transfers between devices  185 us (35%)
  starting transfers between devices  159 us (30%)
  Pallas kernels  101 us (19%)
  local copies, waits for them, and re-layouts  57.4 us (11%)
  between operations  16.1 us (3%)
  other arithmetic  11.2 us (2%)
    ppermute x66, waiting for transfers between devices, plane_swap(): return lax.ppermute(values, PLANE, [(i, i ^ shift) for i in range(4)])  140 us
    pallas_call x41, Pallas kernels, call(): pl.pallas_call(body, out_shape=(*outs, jax.ShapeDtypeStruct((8, BLOCK), F...  101 us
    ppermute x66, starting transfers between devices, plane_swap(): return lax.ppermute(values, PLANE, [(i, i ^ shift) for i in range(4)])  96.2 us
    unnamed x293, local copies, waits for them, and re-layouts  47.1 us
    all_to_all x4, starting transfers between devices, plane_turn(): lax.all_to_all(values, PLANE, split_axis=0, concat_axis=0, tiled=True)  25.6 us
    all_to_all x4, waiting for transfers between devices, plane_turn(): lax.all_to_all(values, PLANE, split_axis=0, concat_axis=0, tiled=True)  17.5 us
    ppermute x6, waiting for transfers between devices, z_swap(): return lax.ppermute(values, 'z', [(z, z ^ shift) for z in range(groups)])  16.3 us
    ppermute x22, starting transfers between devices, core_swap(): return lax.ppermute(values, 'core', [(0, 1), (1, 0)])  16 us
  transfers between devices with their start and end apart: 112, of which 50 were waited for; matrix products, arithmetic and copies ran while one was open for 3% of the time, Pallas kernels for 13%

profile of v2, /device:TPU:0, one launch (start us, length us, event | category | flops | bytes accessed | tf_op | source)
XLA Modules:
  0.0 529.6 jit_solution(6902278403229157885)
XLA Ops:
  13.0 5.3 all-to-all-start
  20.0 10.2 %all-to-all-done = bf16[4,24,3456]{2,1,0:T(8,128)(2,1)S(1)} async-done(((bf16[4,24,3456]{2,1,0:T(8,128)(2,1)}), bf16[4,24,3456]{2,1,0:T(8,128)(2,1)S(1)}, u32[]{:S(2)}, u32[]{:S(2)}) %all-to-all-start) | async-done | bytes 663584 | tf_op jit(solution)/shard_map/all_to_all | solution.py:851
  31.3 6.9 %collective-permute-start.7 = (bf16[5,24,768]{2,1,0:T(8,128)(2,1)S(1)}, bf16[5,24,768]{2,1,0:T(8,128)(2,1)S(1)}, u32[]{:S(2)}, u32[]{:S(2)}) collective-permute-start(bf16[5,24,768]{2,1,0:T(8,128)(2,1)S(1)} %get-tuple-element.548), channel_id=1, source_target_pairs={{0,16},{8,24},{16,0},{24,8},{1,17},{9,25},{17,1},{25,9},{2,18},{10... | collective-permute-start | bytes 552968 | tf_op jit(solution)/shard_map/ppermute | solution.py:730
  47.0 9.2 %collective-permute-done.8 = bf16[5,24,768]{2,1,0:T(8,128)(2,1)S(1)} collective-permute-done((bf16[5,24,768]{2,1,0:T(8,128)(2,1)S(1)}, bf16[5,24,768]{2,1,0:T(8,128)(2,1)S(1)}, u32[]{:S(2)}, u32[]{:S(2)}) %collective-permute-start.8) | collective-permute-done | bytes 184352 | tf_op jit(solution)/shard_map/ppermute | solution.py:730
  67.4 5.7 %collective-permute-done.2 = bf16[136,768]{1,0:T(8,128)(2,1)S(1)} collective-permute-done((bf16[136,768]{1,0:T(8,128)(2,1)S(1)}, bf16[136,768]{1,0:T(8,128)(2,1)S(1)}, u32[]{:S(2)}, u32[]{:S(2)}) %collective-permute-start.2) | collective-permute-done | bytes 208928 | tf_op jit(solution)/shard_map/ppermute | solution.py:725
  79.1 6.3 %attn_forward.3 = (bf16[512,192]{1,0:T(8,128)(2,1)S(1)}, f32[8,512]{1,0:T(8,128)S(1)}, f32[128,768]{1,0:T(8,128)S(1)}, bf16[128,768]{1,0:T(8,128)(2,1)S(1)}, bf1...) custom-call(s32[8,128]{1,0:T(8,128)S(1)} %add_convert_fusion.refs_0_, ...), custom_call_target="tpu_custom_call" | custom-call | flops 805306368 | bytes 2478080 | tf_op jit(solution)/shard_map/attn_forward/pallas_call | solution.py:118
  85.5 11.5 %collective-permute-start.11 = (bf16[128,768]{1,0:T(8,128)(2,1)S(1)}, bf16[128,768]{1,0:T(8,128)(2,1)S(1)}, u32[]{:S(2)}, u32[]{:S(2)}) collective-permute-start(bf16[128,768]{1,0:T(8,128)(2,1)S(1)} %get-tuple-element.293), channel_id=1, source_target_pairs={{0,2},{2,0},{4,6},{6,4},{1,3},{3,1},{5,7},{7,5},{8,10},{10,8},{12,... | collective-permute-start | bytes 589832 | tf_op jit(solution)/shard_map/ppermute | solution.py:725
  141.5 6.3 %attn_forward.4 = (bf16[512,192]{1,0:T(8,128)(2,1)S(1)}, f32[8,512]{1,0:T(8,128)S(1)}, f32[128,768]{1,0:T(8,128)S(1)}, bf16[128,768]{1,0:T(8,128)(2,1)S(1)}, bf1...) custom-call(s32[8,128]{1,0:T(8,128)S(1)} %add_convert_fusion.refs_0_, ...), custom_call_target="tpu_custom_call" | custom-call | flops 805306368 | bytes 2478080 | tf_op jit(solution)/shard_map/attn_forward/pallas_call | solution.py:118
  156.1 7.2 %all-gather.7.cloned.1.call-done = bf16[1152,768]{1,0:T(8,128)(2,1)} async-done(((bf16[288,768]{1,0:T(8,128)(2,1)}), bf16[1152,768]{1,0:T(8,128)(2,1)}) %all-gather.7.cloned.1.call-update) | async-done | bytes 1769488 | tf_op jit(solution)/shard_map/all_gather | solution.py:907
  189.9 5.2 collective-permute-done.31.refs_3_
  199.6 15.7 %attn_forward.5 = (bf16[512,192]{1,0:T(8,128)(2,1)S(1)}, f32[8,512]{1,0:T(8,128)S(1)}, f32[128,768]{1,0:T(8,128)S(1)}, bf16[128,768]{1,0:T(8,128)(2,1)S(1)}, bf1...) custom-call(s32[8,128]{1,0:T(8,128)S(1)} %add_convert_fusion.refs_0_, ...), custom_call_target="tpu_custom_call" | custom-call | flops 805306368 | bytes 2478080 | tf_op jit(solution)/shard_map/attn_forward/pallas_call | solution.py:118
  243.6 5.7 %collective-permute-start.44 = (bf16[128,768]{1,0:T(8,128)(2,1)S(1)}, bf16[128,768]{1,0:T(8,128)(2,1)S(1)}, u32[]{:S(2)}, u32[]{:S(2)}) collective-permute-start(bf16[128,768]{1,0:T(8,128)(2,1)S(1)} %get-tuple-element.366), channel_id=1, source_target_pairs={{0,4},{2,6},{4,0},{6,2},{1,5},{3,7},{5,1},{7,3},{8,12},{10,14},{12... | collective-permute-start | bytes 589832 | tf_op jit(solution)/shard_map/ppermute | solution.py:725
  251.4 5.2 collective-permute-done.44.refs_3_
  267.5 6.8 %ffn_backward.2 = (f32[128,768]{1,0:T(8,128)S(1)}, bf16[128,768]{1,0:T(8,128)(2,1)S(1)}, bf16[128,768]{1,0:T(8,128)(2,1)S(1)}, bf16[128,768]{1,0:T(8,128)(2,1)S(...) custom-call(bf16[128,768]{1,0:T(8,128)(2,1)S(1)} %get-tuple-element., ...), custom_call_target="tpu_custom_call" | custom-call | flops 3623878656 | bytes 8484864 | tf_op jit(solution)/shard_map/ffn_backward/pallas_call | solution.py:118
  282.7 5.3 collective-permute-done.52.refs_3_
  294.7 5.5 %collective-permute-done.59.refs_10_ = bf16[128,768]{1,0:T(8,128)(2,1)S(1)} collective-permute-done((bf16[128,768]{1,0:T(8,128)(2,1)}, bf16[128,768]{1,0:T(8,128)(2,1)S(1)}, u32[]{:S(2)}, u32[]{:S(2)}) %collective-permute-start.59) | collective-permute-done | bytes 196640 | tf_op jit(solution)/shard_map/ppermute | solution.py:725
  308.5 6.9 %attn_backward.3 = (bf16[512,192]{1,0:T(8,128)(2,1)S(1)}, f32[512,384]{1,0:T(8,128)S(1)}, f32[512,384]{1,0:T(8,128)S(1)}, f32[4,24,768]{2,1,0:T(8,128)S(1)}, bf1...) custom-call(s32[8,128]{1,0:T(8,128)S(1)} %add_convert_fusion.refs_0_, bf16[512,192]{1,0:T(8,128)(2,1)S(1)} %copy-done.79, ...), custom_call_target="tpu_custom_call" | custom-call | flops 2013265920 | bytes 4493312 | tf_op jit(solution)/shard_map/attn_backward/pallas_call | solution.py:118
  342.8 5.5 %collective-permute-done.68.refs_7_ = bf16[128,768]{1,0:T(8,128)(2,1)S(1)} collective-permute-done((bf16[128,768]{1,0:T(8,128)(2,1)}, bf16[128,768]{1,0:T(8,128)(2,1)S(1)}, u32[]{:S(2)}, u32[]{:S(2)}) %collective-permute-start.68) | collective-permute-done | bytes 196640 | tf_op jit(solution)/shard_map/ppermute | solution.py:725
  355.4 7.0 %ffn_backward.3 = (f32[128,768]{1,0:T(8,128)S(1)}, bf16[128,768]{1,0:T(8,128)(2,1)S(1)}, bf16[128,768]{1,0:T(8,128)(2,1)S(1)}, bf16[128,768]{1,0:T(8,128)(2,1)S(...) custom-call(bf16[128,768]{1,0:T(8,128)(2,1)S(1)} %copy-done.82, ...), custom_call_target="tpu_custom_call" | custom-call | flops 3623878656 | bytes 8484864 | tf_op jit(solution)/shard_map/ffn_backward/pallas_call | solution.py:118
  407.5 6.9 %attn_backward.4 = (bf16[512,192]{1,0:T(8,128)(2,1)S(1)}, f32[512,384]{1,0:T(8,128)S(1)}, f32[512,384]{1,0:T(8,128)S(1)}, f32[4,24,768]{2,1,0:T(8,128)S(1)}, bf1...) custom-call(s32[8,128]{1,0:T(8,128)S(1)} %add_convert_fusion.refs_0_, bf16[512,192]{1,0:T(8,128)(2,1)S(1)} %copy-done.77, ...), custom_call_target="tpu_custom_call" | custom-call | flops 2013265920 | bytes 4493312 | tf_op jit(solution)/shard_map/attn_backward/pallas_call | solution.py:118
  415.2 7.1 %attn_backward.5 = (bf16[512,192]{1,0:T(8,128)(2,1)S(1)}, f32[512,384]{1,0:T(8,128)S(1)}, f32[512,384]{1,0:T(8,128)S(1)}, f32[4,24,768]{2,1,0:T(8,128)S(1)}, bf1...) custom-call(s32[8,128]{1,0:T(8,128)S(1)} %add_convert_fusion.refs_0_, bf16[512,192]{1,0:T(8,128)(2,1)S(1)} %copy-done.75, ...), custom_call_target="tpu_custom_call" | custom-call | flops 2013265920 | bytes 4493312 | tf_op jit(solution)/shard_map/attn_backward/pallas_call | solution.py:118
  433.3 12.4 %collective-permute-start.90 = (bf16[4,24,768]{2,1,0:T(8,128)(2,1)}, bf16[4,24,768]{2,1,0:T(8,128)(2,1)S(1)}, u32[]{:S(2)}, u32[]{:S(2)}) collective-permute-start(bf16[4,24,768]{2,1,0:T(8,128)(2,1)} %get-tuple-element.493), channel_id=1, source_target_pairs={{0,1},{1,0},{2,3},{3,2},{4,5},{5,4},{6,7},{7,6},{8,9},{9,8},{10,11... | collective-permute-start | bytes 442376 | tf_op jit(solution)/shard_map/ppermute | solution.py:734
  473.7 7.4 %collective-permute-done.95.refs_3_ = bf16[128,768]{1,0:T(8,128)(2,1)S(1)} collective-permute-done((bf16[128,768]{1,0:T(8,128)(2,1)}, bf16[128,768]{1,0:T(8,128)(2,1)S(1)}, u32[]{:S(2)}, u32[]{:S(2)}) %collective-permute-start.95) | collective-permute-done | bytes 196640 | tf_op jit(solution)/shard_map/ppermute | solution.py:725
  493.2 11.6 %all-to-all-start.3 = ((bf16[4,24,1472]{2,1,0:T(8,128)(2,1)}), bf16[4,24,1472]{2,1,0:T(8,128)(2,1)S(1)}, u32[]{:S(2)}, u32[]{:S(2)}) async-start(bf16[4,24,1472]{2,1,0:T(8,128)(2,1)} %pad_maximum_fusion.3), calls=%async_computation.7 | async-start | bytes 589824 | tf_op jit(solution)/shard_map/all_to_all | solution.py:851
  (604 shorter events, 330.8 us)
Async XLA Ops:
  13.0 17.1 %all-to-all-start = ((bf16[4,24,3456]{2,1,0:T(8,128)(2,1)}), bf16[4,24,3456]{2,1,0:T(8,128)(2,1)S(1)}, u32[]{:S(2)}, u32[]{:S(2)}) async-start(bf16[4,24,3456]{2,1,0:T(8,128)(2,1)} %concatenate.49), calls=%async_computation | async-start | bytes 1327104 | tf_op jit(solution)/shard_map/all_to_all | solution.py:851
  18.3 104.8 %all-gather.5.cloned.1.call-start = ((), (), s32[]{:S(2)}) async-start(), calls=%async_computation.12 | async-start | bytes 2580480 | tf_op jit(solution)/shard_map/all_gather | solution.py:904
  31.2 132.1 %all-gather.7.cloned.1.call-start = ((), (), s32[]{:S(2)}) async-start(), calls=%async_computation.13 | async-start | bytes 2211840 | tf_op jit(solution)/shard_map/all_gather | solution.py:907
  56.3 18.8 %collective-permute-start.9 = (bf16[4,5,24,768]{3,2,1,0:T(8,128)(2,1)S(1)}, bf16[4,5,24,768]{3,2,1,0:T(8,128)(2,1)S(1)}, u32[]{:S(2)}, u32[]{:S(2)}) collective-permute-start(bf16[4,5,24,768]{3,2,1,0:T(8,128)(2,1)S(1)} %pad_maximum_fusion.refs_0_), channel_id=1, source_target_pairs={{0,1},{1,0},{2,3},{3,2},{4,5},{5,4},{6,7},{7,6},{8,9},{9,8},{10,11... | collective-permute-start | bytes 2211848 | tf_op jit(solution)/shard_map/ppermute | solution.py:734
  78.4 20.3 %collective-permute-start.14 = (bf16[128,768]{1,0:T(8,128)(2,1)S(1)}, bf16[128,768]{1,0:T(8,128)(2,1)S(1)}, u32[]{:S(2)}, u32[]{:S(2)}) collective-permute-start(bf16[128,768]{1,0:T(8,128)(2,1)S(1)} %bitcast.160), channel_id=1, source_target_pairs={{0,0},{1,8},{2,16},{3,24},{4,2},{5,10},{6,18},{7,26},{8,4},{9,12},... | collective-permute-start | bytes 589832 | tf_op jit(solution)/shard_map/ppermute | solution.py:972
  85.5 17.1 %collective-permute-start.11 = (bf16[128,768]{1,0:T(8,128)(2,1)S(1)}, bf16[128,768]{1,0:T(8,128)(2,1)S(1)}, u32[]{:S(2)}, u32[]{:S(2)}) collective-permute-start(bf16[128,768]{1,0:T(8,128)(2,1)S(1)} %get-tuple-element.293), channel_id=1, source_target_pairs={{0,2},{2,0},{4,6},{6,4},{1,3},{3,1},{5,7},{7,5},{8,10},{10,8},{12,... | collective-permute-start | bytes 589832 | tf_op jit(solution)/shard_map/ppermute | solution.py:725
  124.1 321.6 %reduce-scatter.5.cloned.1.call-start = ((), (), s32[]{:S(2)}) async-start(), calls=%async_computation.8 | async-start | bytes 1536000 | tf_op jit(solution)/shard_map/reduce_scatter | solution.py:1056
  230.8 18.5 %collective-permute-start.46 = (bf16[128,768]{1,0:T(8,128)(2,1)S(1)}, bf16[128,768]{1,0:T(8,128)(2,1)S(1)}, u32[]{:S(2)}, u32[]{:S(2)}) collective-permute-start(bf16[128,768]{1,0:T(8,128)(2,1)S(1)} %bitcast.161), channel_id=1, source_target_pairs={{0,0},{1,8},{2,16},{3,24},{4,2},{5,10},{6,18},{7,26},{8,4},{9,12},... | collective-permute-start | bytes 589832 | tf_op jit(solution)/shard_map/ppermute | solution.py:1013
  290.9 162.8 %reduce-scatter.7.cloned.1.call-start = ((), (), s32[]{:S(2)}) async-start(), calls=%async_computation.9 | async-start | bytes 921600 | tf_op jit(solution)/shard_map/reduce_scatter | solution.py:1056
  338.8 151.0 %reduce-scatter.9.cloned.1.call-start = ((), (), s32[]{:S(2)}) async-start(), calls=%async_computation.10 | async-start | bytes 1536000 | tf_op jit(solution)/shard_map/reduce_scatter | solution.py:1056
  362.4 23.1 %collective-permute-start.72 = (bf16[4,4,24,768]{3,2,1,0:T(8,128)(2,1)S(1)}, bf16[4,4,24,768]{3,2,1,0:T(8,128)(2,1)S(1)}, u32[]{:S(2)}, u32[]{:S(2)}) collective-permute-start(bf16[4,4,24,768]{3,2,1,0:T(8,128)(2,1)S(1)} %get-tuple-element.441), channel_id=1, source_target_pairs={{0,1},{1,0},{2,3},{3,2},{4,5},{5,4},{6,7},{7,6},{8,9},{9,8},{10,11... | collective-permute-start | bytes 1769480 | tf_op jit(solution)/shard_map/ppermute | solution.py:734
  362.7 22.9 %collective-permute-start.73 = (bf16[4,96,768]{2,1,0:T(8,128)(2,1)S(1)}, bf16[4,96,768]{2,1,0:T(8,128)(2,1)S(1)}, u32[]{:S(2)}, u32[]{:S(2)}) collective-permute-start(bf16[4,96,768]{2,1,0:T(8,128)(2,1)S(1)} %get-tuple-element.443), channel_id=1, source_target_pairs={{0,1},{1,0},{2,3},{3,2},{4,5},{5,4},{6,7},{7,6},{8,9},{9,8},{10,11... | collective-permute-start | bytes 1769480 | tf_op jit(solution)/shard_map/ppermute | solution.py:734
  388.6 102.9 %reduce-scatter.11.cloned.1.call-start = ((), (), s32[]{:S(2)}) async-start(), calls=%async_computation.11 | async-start | bytes 921600 | tf_op jit(solution)/shard_map/reduce_scatter | solution.py:1056
  392.4 22.8 %collective-permute-start.80 = (bf16[128,768]{1,0:T(8,128)(2,1)}, bf16[128,768]{1,0:T(8,128)(2,1)S(1)}, u32[]{:S(2)}, u32[]{:S(2)}) collective-permute-start(bf16[128,768]{1,0:T(8,128)(2,1)} %copy-done.102), channel_id=1, source_target_pairs={{0,6},{2,4},{4,2},{6,0},{1,7},{3,5},{5,3},{7,1},{8,14},{10,12},{12... | collective-permute-start | bytes 589832 | tf_op jit(solution)/shard_map/ppermute | solution.py:725
  393.8 21.3 %collective-permute-start.79 = (bf16[128,768]{1,0:T(8,128)(2,1)}, bf16[128,768]{1,0:T(8,128)(2,1)S(1)}, u32[]{:S(2)}, u32[]{:S(2)}) collective-permute-start(bf16[128,768]{1,0:T(8,128)(2,1)} %copy-done.102), channel_id=1, source_target_pairs={{0,4},{2,6},{4,0},{6,2},{1,5},{3,7},{5,1},{7,3},{8,12},{10,14},{12... | collective-permute-start | bytes 589832 | tf_op jit(solution)/shard_map/ppermute | solution.py:725
  397.9 17.3 %collective-permute-start.78 = (bf16[128,768]{1,0:T(8,128)(2,1)}, bf16[128,768]{1,0:T(8,128)(2,1)S(1)}, u32[]{:S(2)}, u32[]{:S(2)}) collective-permute-start(bf16[128,768]{1,0:T(8,128)(2,1)} %copy-done.102), channel_id=1, source_target_pairs={{0,2},{2,0},{4,6},{6,4},{1,3},{3,1},{5,7},{7,5},{8,10},{10,8},{12,... | collective-permute-start | bytes 589832 | tf_op jit(solution)/shard_map/ppermute | solution.py:725
  432.2 18.4 %collective-permute-start.89 = (bf16[4,4,24,704]{3,2,1,0:T(8,128)(2,1)}, bf16[4,4,24,704]{3,2,1,0:T(8,128)(2,1)S(1)}, u32[]{:S(2)}, u32[]{:S(2)}) collective-permute-start(bf16[4,4,24,704]{3,2,1,0:T(8,128)(2,1)} %get-tuple-element.492), channel_id=1, source_target_pairs={{0,1},{1,0},{2,3},{3,2},{4,5},{5,4},{6,7},{7,6},{8,9},{9,8},{10,11... | collective-permute-start | bytes 1622024 | tf_op jit(solution)/shard_map/ppermute | solution.py:734
  433.3 16.5 %collective-permute-start.90 = (bf16[4,24,768]{2,1,0:T(8,128)(2,1)}, bf16[4,24,768]{2,1,0:T(8,128)(2,1)S(1)}, u32[]{:S(2)}, u32[]{:S(2)}) collective-permute-start(bf16[4,24,768]{2,1,0:T(8,128)(2,1)} %get-tuple-element.493), channel_id=1, source_target_pairs={{0,1},{1,0},{2,3},{3,2},{4,5},{5,4},{6,7},{7,6},{8,9},{9,8},{10,11... | collective-permute-start | bytes 442376 | tf_op jit(solution)/shard_map/ppermute | solution.py:734
  459.5 24.1 %all-to-all-start.1 = ((bf16[4,24,1472]{2,1,0:T(8,128)(2,1)}), bf16[4,24,1472]{2,1,0:T(8,128)(2,1)S(1)}, u32[]{:S(2)}, u32[]{:S(2)}) async-start(bf16[4,24,1472]{2,1,0:T(8,128)(2,1)} %pad_maximum_fusion.2), calls=%async_computation.3 | async-start | bytes 589824 | tf_op jit(solution)/shard_map/all_to_all | solution.py:851
  463.4 17.7 %collective-permute-start.95 = (bf16[128,768]{1,0:T(8,128)(2,1)}, bf16[128,768]{1,0:T(8,128)(2,1)S(1)}, u32[]{:S(2)}, u32[]{:S(2)}) collective-permute-start(bf16[128,768]{1,0:T(8,128)(2,1)} %get-tuple-element.505), channel_id=1, source_target_pairs={{0,4},{2,6},{4,0},{6,2},{1,5},{3,7},{5,1},{7,3},{8,12},{10,14},{12... | collective-permute-start | bytes 589832 | tf_op jit(solution)/shard_map/ppermute | solution.py:725
  465.4 15.7 %collective-permute-start.96 = (bf16[128,768]{1,0:T(8,128)(2,1)}, bf16[128,768]{1,0:T(8,128)(2,1)S(1)}, u32[]{:S(2)}, u32[]{:S(2)}) collective-permute-start(bf16[128,768]{1,0:T(8,128)(2,1)} %get-tuple-element.506), channel_id=1, source_target_pairs={{0,6},{2,4},{4,2},{6,0},{1,7},{3,5},{5,3},{7,1},{8,14},{10,12},{12... | collective-permute-start | bytes 589832 | tf_op jit(solution)/shard_map/ppermute | solution.py:725
  466.9 17.5 %collective-permute-start.98 = (bf16[5,24,768]{2,1,0:T(8,128)(2,1)}, bf16[5,24,768]{2,1,0:T(8,128)(2,1)}, u32[]{:S(2)}, u32[]{:S(2)}) collective-permute-start(bf16[5,24,768]{2,1,0:T(8,128)(2,1)} %get-tuple-element.510), channel_id=1, source_target_pairs={{0,8},{8,0},{16,24},{24,16},{1,9},{9,1},{17,25},{25,17},{2,10},{10... | collective-permute-start | bytes 552968 | tf_op jit(solution)/shard_map/ppermute | solution.py:730
  469.1 17.2 %collective-permute-start.99 = (bf16[5,24,768]{2,1,0:T(8,128)(2,1)}, bf16[5,24,768]{2,1,0:T(8,128)(2,1)}, u32[]{:S(2)}, u32[]{:S(2)}) collective-permute-start(bf16[5,24,768]{2,1,0:T(8,128)(2,1)} %get-tuple-element.511), channel_id=1, source_target_pairs={{0,16},{8,24},{16,0},{24,8},{1,17},{9,25},{17,1},{25,9},{2,18},{10... | collective-permute-start | bytes 552968 | tf_op jit(solution)/shard_map/ppermute | solution.py:730
  493.2 18.0 %all-to-all-start.3 = ((bf16[4,24,1472]{2,1,0:T(8,128)(2,1)}), bf16[4,24,1472]{2,1,0:T(8,128)(2,1)S(1)}, u32[]{:S(2)}, u32[]{:S(2)}) async-start(bf16[4,24,1472]{2,1,0:T(8,128)(2,1)} %pad_maximum_fusion.3), calls=%async_computation.7 | async-start | bytes 589824 | tf_op jit(solution)/shard_map/all_to_all | solution.py:851
  (234 other events, 1789.6 us)
Sparse Core Ops, SparseCore 0:
  31.3 60.3 all-gather.4
  124.2 39.0 all-gather.6
  291.0 29.5 reduce-scatter.4
  338.9 23.1 reduce-scatter.6
  388.7 29.6 reduce-scatter.8
  452.6 24.2 reduce-scatter.10

commit v3 on v2

--- a/solution.py
+++ b/solution.py
@@ -41,11 +41,12 @@
 
 def positions(subs, index):
     core = lax.axis_index("core")
-    part = 2 * lax.axis_index("y") + lax.axis_index("x")
+    part = 2 * lax.axis_index("x") + lax.axis_index("y")
     sub = lax.axis_index("z") & (subs - 1)
     group = lax.shift_right_logical(index, 10)
     half = lax.shift_right_logical(index, 9) & 1
     block = lax.shift_right_logical(index, 7) & 3
+    block = ((block & 1) << 1) | lax.shift_right_logical(block, 1)
     return ((sub ^ group) << 10) + ((core ^ half) << 9) + ((part ^ block) << 7) + (index & 127)
 
 
@@ -64,19 +65,20 @@
     return (key >= low) & (key < high)
 
 
-def joined(refs):
-    return jnp.concatenate([ref[...] for ref in refs], axis=0)
-
-
-def spread(value, out_refs):
+def joined(refs, start=0):
+    return jnp.concatenate([ref[start : start + BLOCK] for ref in refs], axis=0)
+
+
+def spread(value, out_refs, start=0):
     out_refs[0][...] = value[:BLOCK]
     for k in (1, 2, 3):
-        out_refs[k][...] = value[k * BLOCK : (k + 1) * BLOCK].astype(BF16)
-
-
-def spread_shapes(width):
+        block = value[k * BLOCK : (k + 1) * BLOCK]
+        out_refs[k][start : start + BLOCK] = block.astype(BF16)
+
+
+def spread_shapes(width, blocks=1):
     return [jax.ShapeDtypeStruct((BLOCK, width), F32)] + [
-        jax.ShapeDtypeStruct((BLOCK, width), BF16)
+        jax.ShapeDtypeStruct((blocks * BLOCK, width), BF16)
     ] * 3
 
 
@@ -121,7 +123,7 @@
         in_specs=[pl.BlockSpec(memory_space=pltpu.SMEM)] * smem + vmem_specs(count - smem + 1),
         out_specs=tuple(vmem_specs(made + 1)),
         scratch_shapes=[pltpu.VMEM(shape, F32) for shape in scratch],
-        compiler_params=pltpu.CompilerParams(vmem_limit_bytes=48 << 20),
+        compiler_params=pltpu.CompilerParams(vmem_limit_bytes=24 << 20),
         cost_estimate=pl.CostEstimate(flops=flops, transcendentals=trans, bytes_accessed=size),
         name=name,
     )(*ins, chain.token)
@@ -133,41 +135,45 @@
     return [pl.BlockSpec(memory_space=pltpu.VMEM)] * count
 
 
-def project_kernel(wants, bias_row, count, *refs):
-    x_refs, (w_ref, bias_ref), out_refs = refs[:count], refs[count : count + 2], refs[count + 2 :]
-    rows = joined(x_refs)
+def project_kernel(bias_row, q_start, x0, x1, x2, x3, w_ref, bias_ref, q_ref, kv_ref, rows_ref):
+    pieces = (x0, x1, x2, x3)
     quarter = bias_ref.shape[1]
-    out_refs = list(out_refs)
-    if "q" in wants:
-        value = matmul(rows, w_ref[:, :quarter]) + bias_ref[bias_row : bias_row + 1]
-        out_refs.pop(0)[...] = value.astype(BF16) * BF16(HEAD**-0.5)
-    if "k" in wants:
-        out_ref = out_refs.pop(0)
-        out_ref[:, :quarter] = matmul(rows, w_ref[:, quarter : 2 * quarter]).astype(BF16)
-        value = matmul(rows, w_ref[:, 2 * quarter :]) + bias_ref[bias_row + 1 : bias_row + 2]
-        out_ref[:, quarter:] = value.astype(BF16)
-
-
-def project(chain, wants, bias_row, pieces, weight, biases):
+    rows = joined(pieces, q_start)
+    if q_start:
+        rows_ref[4 * BLOCK :] = rows
+    value = matmul(rows, w_ref[:, :quarter]) + bias_ref[bias_row : bias_row + 1]
+    q_ref[...] = value.astype(BF16) * BF16(HEAD**-0.5)
+    rows = joined(pieces)
+    rows_ref[: 4 * BLOCK] = rows
+    kv_ref[:, :quarter] = matmul(rows, w_ref[:, quarter : 2 * quarter]).astype(BF16)
+    value = matmul(rows, w_ref[:, 2 * quarter :]) + bias_ref[bias_row + 1 : bias_row + 2]
+    kv_ref[:, quarter:] = value.astype(BF16)
+
+
+def project(chain, bias_row, pieces, weight, biases, q_start=0):
     quarter = biases.shape[1]
-    rows = BLOCK * len(pieces)
-    outs = [jax.ShapeDtypeStruct((rows, quarter), BF16)] if "q" in wants else []
-    if "k" in wants:
-        outs.append(jax.ShapeDtypeStruct((rows, 2 * quarter), BF16))
+    rows = 4 * BLOCK
     return call(
         chain,
-        functools.partial(project_kernel, wants, bias_row, len(pieces)),
+        functools.partial(project_kernel, bias_row, q_start),
         "project_heads",
         [*pieces, weight, biases],
-        outs,
+        [
+            jax.ShapeDtypeStruct((rows, quarter), BF16),
+            jax.ShapeDtypeStruct((rows, 2 * quarter), BF16),
+            jax.ShapeDtypeStruct((rows * (2 if q_start else 1), weight.shape[0]), BF16),
+        ],
         flops=2 * rows * weight.size,
     )
 
 
 def attn_fwd_kernel(form, width, halves, count_ref, q_ref, wo_ref, *refs):
-    kv_refs, (o_ref, lse_ref), out_refs = refs[:halves], refs[halves : halves + 2], refs[halves + 2 : -1]
+    kv_refs, (kept_ref, lse_ref), out_refs = refs[:halves], refs[halves : halves + 2], refs[halves + 2 : -1]
     ot_ref = refs[-1]
     quarter = q_ref.shape[1]
+    kept_ref[:, :quarter] = q_ref[...]
+    for j, ref in enumerate(kv_refs):
+        kept_ref[:, (2 + 2 * j) * quarter : (4 + 2 * j) * quarter] = ref[...]
     keys = sum(ref.shape[0] for ref in kv_refs)
     for chunk in range(q_ref.shape[0] // width):
         rows = slice(chunk * width, (chunk + 1) * width)
@@ -186,7 +192,7 @@
             ot_ref[cols, rows] = lax.dot_general(value, probs, TN, preferred_element_type=F32)
             lse_ref[head : head + 1, rows] = peak + jnp.log(total)
     mixture = ot_ref[...].T.astype(BF16)
-    o_ref[...] = mixture
+    kept_ref[:, quarter : 2 * quarter] = mixture
     spread(matmul(mixture, wo_ref[...]), out_refs)
 
 
@@ -195,8 +201,11 @@
     length = rows * len(kv)
     width = 256 if length <= 1024 else 128
     work = rows * length * cols
-    outs = [jax.ShapeDtypeStruct((rows, cols), BF16), jax.ShapeDtypeStruct((8, rows), F32)]
-    o, lse, *sent = call(
+    outs = [
+        jax.ShapeDtypeStruct((rows, cols * (2 + 2 * len(kv))), BF16),
+        jax.ShapeDtypeStruct((8, rows), F32),
+    ]
+    kept, lse, *rest = call(
         chain,
         functools.partial(attn_fwd_kernel, form, width, len(kv)),
         "attn_forward",
@@ -207,34 +216,37 @@
         flops=8 * work,
         trans=work // HEAD,
     )
-    return o, lse, sent
-
-
-def attn_bwd_kernel(form, width, halves, split, count_ref, q_ref, wo_ref, o_ref, lse_ref, *refs):
-    kv_refs, low_refs = refs[:halves], refs[halves : halves + 4]
-    refs = refs[halves + 4 :]
+    return (kept, out_weight, lse), rest
+
+
+def attn_bwd_kernel(form, width, halves, split, start, count_ref, kept_ref, wo_ref, lse_ref, *refs):
+    low_refs, refs = refs[:4], refs[4:]
+    quarter = wo_ref.shape[0]
+
+    def kept(first):
+        starts = [(2 + 2 * j) * quarter + first for j in range(halves)]
+        return jnp.concatenate([kept_ref[:, at : at + HEAD] for at in starts], axis=0)
+
     dq_ref, dkv_refs, w_refs = refs[0], refs[1 : 1 + halves], refs[1 + halves : -3]
     dqt_ref, do_ref, all_ref = refs[-3:]
-    quarter = q_ref.shape[1]
-    half = kv_refs[0].shape[0]
+    half = kept_ref.shape[0]
     keys = half * halves
-    low = joined(low_refs)
+    low = joined(low_refs, start)
     do_ref[...] = back_matmul(low, wo_ref[...])
-    grad_w = outer_sum(o_ref[...], low)
+    grad_w = outer_sum(kept_ref[:, quarter : 2 * quarter], low)
     if split:
         all_ref[...] = grad_w.reshape(all_ref.shape)
         put_halves(all_ref, 1, w_refs)
     else:
         w_refs[0][...] = grad_w
-    for chunk in range(q_ref.shape[0] // width):
+    for chunk in range(half // width):
         rows = slice(chunk * width, (chunk + 1) * width)
         mask = allowed_mask(form, count_ref, chunk * width, width, keys)
         for head in range(quarter // HEAD):
             cols = slice(head * HEAD, (head + 1) * HEAD)
             wide = slice(quarter + head * HEAD, quarter + (head + 1) * HEAD)
-            key = jnp.concatenate([ref[:, cols] for ref in kv_refs], axis=0)
-            value = jnp.concatenate([ref[:, wide] for ref in kv_refs], axis=0)
-            query, grad = q_ref[rows, cols], do_ref[rows, cols].astype(BF16)
+            key, value = kept(head * HEAD), kept(quarter + head * HEAD)
+            query, grad = kept_ref[rows, cols], do_ref[rows, cols].astype(BF16)
             scores = lax.dot_general(key, query, NT, preferred_element_type=F32)
             probs = jnp.where(mask, jnp.exp(scores - lse_ref[head : head + 1, rows]), 0.0)
             grad_probs = lax.dot_general(value, grad, NT, preferred_element_type=F32)
@@ -257,20 +269,21 @@
     dq_ref[...] = dqt_ref[...].T.astype(BF16)
 
 
-def attn_backward(chain, form, split, count, queries, kv, low, out_weight, o, lse, view):
-    rows, cols = queries.shape
-    length = rows * len(kv)
+def attn_backward(chain, form, split, count, saved, low, view, start=0):
+    kept, out_weight, lse = saved
+    rows, cols = kept.shape[0], out_weight.shape[0]
+    halves = kept.shape[1] // (2 * cols) - 1
+    length = rows * halves
     width = 256 if length <= 1024 else 128
     work = rows * length * cols
-    halves = len(kv)
     outs = [jax.ShapeDtypeStruct((rows, cols), BF16)]
     outs += [jax.ShapeDtypeStruct((rows, 2 * cols), F32)] * halves
     outs += split_shapes(split, view, 1)
     dq, *rest = call(
         chain,
-        functools.partial(attn_bwd_kernel, form, width, halves, split),
+        functools.partial(attn_bwd_kernel, form, width, halves, split, start),
         "attn_backward",
-        [count, queries, out_weight, o, lse, *kv, *low],
+        [count, kept, out_weight, lse, *low],
         outs,
         scratch=[(cols, rows), (rows, cols), view if split else (8, BLOCK)],
         smem=1,
@@ -280,12 +293,14 @@
     return dq, rest[:halves], rest[halves:]
 
 
-def project_back_kernel(cross, split, picks, *refs):
-    count = 8 if cross else 4
-    x_refs, (w_ref, dq_ref, own_ref, got_ref) = refs[:count], refs[count : count + 4]
-    refs = refs[count + 4 :]
+def project_back_kernel(cross, joins, split, picks, *refs):
+    rows_ref, w_ref, dq_ref, own_ref, got_ref = refs[:5]
+    refs = refs[5:]
     made = len({source for source, _, _ in picks})
-    vec_refs, out_refs, refs = refs[:made], refs[made : made + count], refs[made + count :]
+    vec_refs, refs = refs[:made], refs[made:]
+    mate_refs, refs = (refs[:3], refs[3:]) if joins else ((), refs)
+    own_q_ref, refs = (refs[0], refs[1:]) if cross else (None, refs)
+    out_refs, refs = refs[:4], refs[4:]
     bias_ref, w_refs, all_ref = refs[0], refs[1:-1], refs[-1]
     quarter = dq_ref.shape[1]
     dq = dq_ref[...]
@@ -296,12 +311,15 @@
     from_q = back_matmul(dq, w_ref[:, :quarter])
     from_kv = back_matmul(dkv, w_ref[:, quarter:])
     if cross:
-        spread(from_q, out_refs[:4])
-        spread(from_kv, out_refs[4:])
-        rows_q, rows_kv = joined(x_refs[:4]), joined(x_refs[4:])
+        spread(from_kv, out_refs)
+        spread(from_q, (own_q_ref, *out_refs[1:]), BLOCK)
     else:
         spread(from_q + from_kv, out_refs)
-        rows_q = rows_kv = joined(x_refs)
+    for ref, out_ref in zip(mate_refs, out_refs[1:], strict=False):
+        out_ref[BLOCK:] = ref[...]
+    rows_q = rows_kv = rows_ref[: 4 * BLOCK]
+    if cross:
+        rows_q = rows_ref[4 * BLOCK :]
     grads = (
         (slice(0, quarter), outer_sum(rows_q, dq)),
         (slice(quarter, 3 * quarter), outer_sum(rows_kv, dkv)),
@@ -326,56 +344,71 @@
         put_halves(all_ref, 2, w_refs)
 
 
-def project_back(chain, cross, split, pieces, weight, dq, own, got, view, vecs, picks):
+def project_back(
+    chain, split, kept_rows, weight, dq, own, got, view, vecs, picks, mates=()
+):
     rows, quarter = dq.shape
     width = weight.shape[0]
-    outs = spread_shapes(width) * (2 if cross else 1)
+    cross = kept_rows.shape[0] > rows
+    outs = [jax.ShapeDtypeStruct((BLOCK, width), F32)] if cross else []
+    outs += spread_shapes(width, 2 if cross or mates else 1)
+    count = len(outs)
     outs += [jax.ShapeDtypeStruct((8, quarter), F32)] + split_shapes(split, view, 2)
     results = call(
         chain,
-        functools.partial(project_back_kernel, cross, split, picks),
+        functools.partial(project_back_kernel, cross, bool(mates), split, picks),
         "project_back",
-        [*pieces, weight, dq, own, got, *vecs],
+        [kept_rows, weight, dq, own, got, *vecs, *mates],
         outs,
         scratch=[view if split else (8, BLOCK)],
         flops=4 * rows * weight.size,
     )
-    count = len(pieces)
     return results[:count], results[count], results[count + 1 :]
 
 
-def norm_kernel(bias_row, gain_row, shift_row, has_sent, base_ref, *refs):
-    sent_refs, vec_ref, out_refs = refs[:4], refs[4], refs[5:]
-    resid = base_ref[...].astype(F32) + vec_ref[bias_row : bias_row + 1]
-    for ref in sent_refs:
-        resid = resid + ref[...].astype(F32)
-    out_refs[0][...] = resid
-    gain, shift = vec_ref[gain_row : gain_row + 1], vec_ref[shift_row : shift_row + 1]
-    value = layer_norm(resid, gain, shift)
-    out_refs[1][...] = value
-    out_refs[2][...] = value.astype(BF16)
-
-
-def norm(chain, base, sent, vectors, bias_row, gain_row, shift_row):
-    shape = base.shape
+def norm_kernel(bias_row, line, before, start, base_ref, *refs):
+    sent_refs, vec_ref, mate_refs, (resid_ref, low_ref) = refs[:4], refs[4], refs[5:-2], refs[-2:]
+
+    def normed(resid, gain_row, shift_row):
+        return layer_norm(
+            resid, vec_ref[gain_row : gain_row + 1], vec_ref[shift_row : shift_row + 1]
+        )
+
+    base = base_ref[...].astype(F32)
+    if before is not None:
+        base = normed(base, *before)
+    resid = base + vec_ref[bias_row : bias_row + 1] + sent_refs[0][...]
+    for ref in sent_refs[1:]:
+        resid = resid + ref[start : start + BLOCK].astype(F32)
+    resid_ref[...] = resid
+    at = BLOCK if mate_refs else 0
+    for ref in mate_refs:
+        low_ref[:BLOCK] = ref[...]
+    low_ref[at:] = normed(resid, *line).astype(BF16)
+
+
+def norm(chain, base, sent, vectors, bias_row, line, before=None, start=0, mate=()):
+    rows, width = base.shape
     return call(
         chain,
-        functools.partial(norm_kernel, bias_row, gain_row, shift_row, True),
+        functools.partial(norm_kernel, bias_row, line, before, start),
         "layer_norm",
-        [base, *sent, vectors],
+        [base, *sent, vectors, *mate],
         [
-            jax.ShapeDtypeStruct(shape, F32),
-            jax.ShapeDtypeStruct(shape, F32),
-            jax.ShapeDtypeStruct(shape, BF16),
+            jax.ShapeDtypeStruct((rows, width), F32),
+            jax.ShapeDtypeStruct((rows * (1 + len(mate)), width), BF16),
         ],
     )
 
 
-def norm_back_kernel(gain_row, count, *refs):
-    grad_refs, (resid_ref, vec_ref), out_refs = refs[:count], refs[count : count + 2], refs[count + 2 :]
-    grad = grad_refs[0][...].astype(F32)
-    for ref in grad_refs[1:]:
-        grad = grad + ref[...].astype(F32)
+def norm_back_kernel(gain_row, count, start, *refs):
+    grad_refs, (resid_ref, vec_ref), refs = refs[:count], refs[count : count + 2], refs[count + 2 :]
+    mate_refs, out_refs = refs[:-3], refs[-3:]
+    grad = None
+    for ref in grad_refs:
+        first = start if ref.shape[0] > BLOCK else 0
+        part = ref[first : first + BLOCK].astype(F32)
+        grad = part if grad is None else grad + part
     resid = resid_ref[...]
     center = resid - jnp.mean(resid, axis=-1, keepdims=True)
     scale = lax.rsqrt(jnp.mean(center * center, axis=-1, keepdims=True) + EPSILON)
@@ -387,25 +420,44 @@
     value = (weighted - first - unit * second) * scale
     low = value.astype(BF16)
     out_refs[0][...] = value
-    out_refs[1][...] = low
+    for ref in mate_refs:
+        out_refs[1][:BLOCK] = ref[...]
+    out_refs[1][BLOCK if mate_refs else 0 :] = low
     out_refs[2][...] = jnp.zeros_like(out_refs[2])
     for row, terms in enumerate((both, grad, low.astype(F32))):
         out_refs[2][row : row + 1] = jnp.sum(terms, axis=0, keepdims=True)
 
 
-def norm_back(chain, grads, resid, vectors, gain_row):
-    shape = resid.shape
+def norm_back(chain, grads, resid, vectors, gain_row, start=0, mate=()):
+    rows, width = resid.shape
     return call(
         chain,
-        functools.partial(norm_back_kernel, gain_row, len(grads)),
+        functools.partial(norm_back_kernel, gain_row, len(grads), start),
         "layer_norm_back",
-        [*grads, resid, vectors],
+        [*grads, resid, vectors, *mate],
         [
-            jax.ShapeDtypeStruct(shape, F32),
-            jax.ShapeDtypeStruct(shape, BF16),
-            jax.ShapeDtypeStruct((8, shape[1]), F32),
+            jax.ShapeDtypeStruct((rows, width), F32),
+            jax.ShapeDtypeStruct((rows * (1 + len(mate)), width), BF16),
+            jax.ShapeDtypeStruct((8, width), F32),
         ],
     )
+
+
+def both_totals_kernel(*refs):
+    for at, base_ref, own_ref in ((0, refs[0], refs[1]), (BLOCK, refs[2], refs[3])):
+        total = base_ref[...] + own_ref[...]
+        for ref in refs[4:7]:
+            total = total + ref[at : at + BLOCK].astype(F32)
+        refs[8][at : at + BLOCK] = total.astype(BF16)
+    refs[8][2 * BLOCK :] = refs[7][...]
+
+
+def both_totals(chain, parts):
+    shape = (3 * BLOCK, parts[0].shape[1])
+    (out,) = call(
+        chain, both_totals_kernel, "sum_both", list(parts), [jax.ShapeDtypeStruct(shape, BF16)]
+    )
+    return out
 
 
 def total_kernel(*refs):
@@ -416,9 +468,8 @@
 
 
 def rounded_total(chain, parts):
-    (out,) = call(
-        chain, total_kernel, "sum_parts", list(parts), [jax.ShapeDtypeStruct(parts[0].shape, BF16)]
-    )
+    outs = [jax.ShapeDtypeStruct(parts[0].shape, BF16)]
+    (out,) = call(chain, total_kernel, "sum_parts", list(parts), outs)
     return out
 
 
@@ -426,8 +477,10 @@
     return 0.5 + 0.5 * lax.erf(values * (0.5**0.5))
 
 
-def ffn_fwd_kernel(layer, y0, y1, y2, y3, up_ref, bias_ref, down_ref, *out_refs):
+def ffn_fwd_kernel(layer, y0, y1, y2, y3, up_ref, bias_ref, down_ref, *refs):
+    mate_refs, rows_ref, out_refs = refs[:-5], refs[-5], refs[-4:]
     rows = joined((y0, y1, y2, y3))
+    rows_ref[...] = rows
     hidden = up_ref.shape[1]
     total = None
     for cols in (slice(0, hidden // 2), slice(hidden // 2, hidden)):
@@ -436,30 +489,34 @@
         part = matmul(act, down_ref[cols])
         total = part if total is None else total + part
     spread(total, out_refs)
-
-
-def ffn_forward(chain, layer, pieces, up, biases, down):
-    return call(
+    for ref, out_ref in zip(mate_refs, out_refs[1:], strict=False):
+        out_ref[BLOCK:] = ref[...]
+
+
+def ffn_forward(chain, layer, pieces, up, biases, down, mates=()):
+    rows, *spreads = call(
         chain,
         functools.partial(ffn_fwd_kernel, layer),
         "ffn_forward",
-        [*pieces, up, biases, down],
-        spread_shapes(down.shape[1]),
+        [*pieces, up, biases, down, *mates],
+        [jax.ShapeDtypeStruct((4 * BLOCK, up.shape[0]), BF16)]
+        + spread_shapes(down.shape[1], 2 if mates else 1),
         flops=16 * BLOCK * up.size,
         trans=4 * BLOCK * up.shape[1],
     )
+    return rows, spreads
 
 
 def ffn_bwd_kernel(layer, split, *refs):
-    rows, low = joined(refs[:4]), joined(refs[4:8])
-    up_ref, bias_ref, down_ref = refs[8:11]
-    out_refs = refs[11:15]
+    rows, low = refs[0][...], joined(refs[1:5])
+    up_ref, bias_ref, down_ref = refs[5:8]
+    out_refs, refs = refs[8:12], refs[12:]
     up_all, down_all, bias_all = refs[-3:]
     if split:
-        bias_refs, up_refs, down_refs = refs[15:17], refs[17:19], refs[19:21]
+        bias_refs, up_refs, down_refs = refs[:2], refs[2:4], refs[4:6]
         bias_all[...] = jnp.zeros_like(bias_all)
     else:
-        bias_refs, up_refs, down_refs = refs[15:16], refs[16:17], refs[17:18]
+        bias_refs, up_refs, down_refs = refs[:1], refs[1:2], refs[2:3]
     hidden = up_ref.shape[1]
     total = None
     for c, cols in enumerate((slice(0, hidden // 2), slice(hidden // 2, hidden))):
@@ -489,7 +546,7 @@
         put_halves(bias_all, 0, bias_refs)
 
 
-def ffn_backward(chain, layer, split, pieces, low, up, biases, down, up_view, down_view):
+def ffn_backward(chain, layer, split, rows, low, up, biases, down, up_view, down_view):
     hidden = up.shape[1]
     bias_view = (2, 4, 8, BLOCK) if split else (1, hidden)
     outs = spread_shapes(down.shape[1]) + split_shapes(split, bias_view, 0)
@@ -499,7 +556,7 @@
         chain,
         functools.partial(ffn_bwd_kernel, layer, split),
         "ffn_backward",
-        [*pieces, *low, up, biases, down],
+        [rows, *low, up, biases, down],
         outs,
         scratch=[up_view, down_view, bias_view] if split else [tiny] * 3,
         flops=48 * BLOCK * up.size,
@@ -540,8 +597,9 @@
 def shares_kernel(keep_ref, got_ref, keep_out, got_out, *out_refs):
     group = lax.axis_index("z")
     cols, wide = keep_ref.shape[-1], out_refs[0].shape[-1]
-    for k, ref in enumerate(out_refs):
-        z = group ^ k
+    targets = (out_refs[0], out_refs[1], out_refs[2].at[0], out_refs[2].at[1])
+    for ref, shift in zip(targets, (0, 2, 1, 3), strict=True):
+        z = group ^ shift
         ref[:4, :, :cols] = (keep_ref[z] + got_ref[z].astype(F32)).astype(ref.dtype)
         ref[:4, :, cols:] = jnp.zeros((4, ref.shape[1], wide - cols), ref.dtype)
         ref[4] = (keep_out[z] + got_out[z].astype(F32)).astype(ref.dtype)
@@ -554,7 +612,7 @@
         shares_kernel,
         "group_shares",
         [*heads, *out],
-        [jax.ShapeDtypeStruct(shape, F32)] + [jax.ShapeDtypeStruct(shape, BF16)] * 3,
+        [jax.ShapeDtypeStruct(shape, F32)] * 2 + [jax.ShapeDtypeStruct((2, *shape), BF16)],
     )
 
 
@@ -583,34 +641,22 @@
     out_ref[...] = total.T[:8]
 
 
-def join_layer_kernel(heads_out, part_ref, up_ref, heads_ref, line_ref):
-    hidden = part_ref.shape[-1] - heads_out - BLOCK
-    join_up(part_ref, 0, up_ref)
-    join_heads(part_ref, hidden, heads_ref)
-    join_lines(part_ref, hidden + heads_out, line_ref)
-
-
-def join_layer(chain, parts, heads_out):
-    _, rows, _ = parts.shape
-    return call(
-        chain,
-        functools.partial(join_layer_kernel, heads_out),
-        "join_gradients",
-        [parts],
-        [
-            jax.ShapeDtypeStruct((rows, 128 * rows), F32),
-            jax.ShapeDtypeStruct((3, rows, 32 * rows), F32),
-            jax.ShapeDtypeStruct((8, rows), F32),
-        ],
-    )
-
-
-def join_last_kernel(heads_out, part_ref, cross_ref, self_ref, heads_ref, *refs):
-    line_ref = refs[-1]
-    join_heads(part_ref, 0, heads_ref)
-    join_lines(part_ref, heads_out, line_ref)
-    lines = {"e": line_ref, "s": self_ref, "c": cross_ref}
-    for ref, picks in zip(refs[:-1], LINES, strict=True):
+def join_last_kernel(heads_out, part_ref, *refs):
+    enc_up_ref, self_ref, enc_ref, dec_up_ref, cross_ref = refs[:5]
+    lines = dict(zip("sec", refs[-3:], strict=True))
+    hidden = enc_up_ref.shape[1] // 4
+    wide = part_ref.shape[-1] - 2 * (hidden + heads_out + BLOCK)
+    join_up(part_ref, 0, enc_up_ref)
+    join_heads(part_ref, hidden, self_ref)
+    join_lines(part_ref, hidden + heads_out, lines["s"])
+    start = hidden + heads_out + BLOCK
+    join_heads(part_ref, start, enc_ref)
+    join_lines(part_ref, start + heads_out, lines["e"])
+    start += wide
+    join_up(part_ref, start, dec_up_ref)
+    join_heads(part_ref, start + hidden, cross_ref)
+    join_lines(part_ref, start + hidden + heads_out, lines["c"])
+    for ref, picks in zip(refs[5:-3], LINES, strict=True):
         for row, (name, line) in enumerate(picks):
             ref[row : row + 1] = lines[name][line : line + 1]
 
@@ -628,17 +674,20 @@
 )
 
 
-def join_last(chain, parts, cross_lines, self_lines, heads_out):
+def join_last(chain, parts, heads_out):
     _, rows, _ = parts.shape
-    return call(
+    heads = jax.ShapeDtypeStruct((3, rows, 32 * rows), F32)
+    up = jax.ShapeDtypeStruct((rows, 128 * rows), F32)
+    results = call(
         chain,
         functools.partial(join_last_kernel, heads_out),
         "join_gradients",
-        [parts, cross_lines, self_lines],
-        [jax.ShapeDtypeStruct((3, rows, 32 * rows), F32)]
+        [parts],
+        [up, heads, heads, up, heads]
         + [jax.ShapeDtypeStruct((len(picks), rows), F32) for picks in LINES],
-        scratch=[(8, rows)],
-    )
+        scratch=[(8, rows)] * 3,
+    )
+    return results[:5], results[5:]
 
 
 def place_kernel(plan, turned, mine_ref, other_ref, *out_refs):
@@ -671,7 +720,8 @@
             for entry, shape in zip(plan, shapes, strict=True)
         ],
     )
-    return [out.reshape(-1, out.shape[-1]) for out in outs]
+    outs = [out.reshape(-1, out.shape[-1]) for out in outs]
+    return outs
 
 
 def place_first_kernel(
@@ -680,11 +730,11 @@
     group, core = lax.axis_index("z"), lax.axis_index("core")
     part = 2 * lax.axis_index("y") + lax.axis_index("x")
     for piece_ref, c in ((mine_ref, core), (other_ref, 1 - core)):
-        for k in range(4):
+        for k, shift in enumerate((0, 2, 1, 3)):
             for p in range(4):
-                w_ref[group ^ k, p, c] = piece_ref[k, p, :, :cols]
-                all_ref[group ^ k, p, c] = piece_ref[k, p, :, cols:].astype(F32)
-            out_w_ref[group ^ k, c] = piece_ref[k, 4]
+                w_ref[group ^ shift, p, c] = piece_ref[k, p, :, :cols]
+                all_ref[group ^ shift, p, c] = piece_ref[k, p, :, cols:].astype(F32)
+            out_w_ref[group ^ shift, c] = piece_ref[k, 4]
     rows = all_ref.shape[3]
     rows_ff = 4 * rows
     for z in range(4):
@@ -772,7 +822,7 @@
                         group, within = row * self.subs + block // 8, block % 8
                         core, part = within // 4, within % 4
                         moves.append(
-                            (self.index(z, y, x, c), self.index(group, part // 2, part % 2, core))
+                            (self.index(z, y, x, c), self.index(group, part % 2, part // 2, core))
                         )
         return moves
 
@@ -825,7 +875,8 @@
     split = groups == 4
     ids = jnp.concatenate([src_seg, tgt_seg]).astype(BF16)
     ids = jnp.pad(ids[None], ((0, 7), (0, width - 2 * BLOCK)))
-    packed = lax.ppermute(jnp.concatenate([src, ids], axis=0), AXES, lay.token_moves())
+    packed = jnp.concatenate([src, ids, tgt, out_grad], axis=0)
+    packed = lax.ppermute(packed, AXES, lay.token_moves())
 
     def heads_split(qkv):
         parts = qkv.reshape(3, rows, 4, quarter)
@@ -878,29 +929,27 @@
             axis=0,
         )
         extra = jnp.broadcast_to(extra[None], (4, rows, wide))
-        pieces = plane_turn(
-            jnp.concatenate(
-                [
-                    heads_split(enc_qkv),
-                    extra,
-                    heads_split(self_qkv),
-                    heads_split(cross_qkv),
-                    up_split(enc_up),
-                    up_split(dec_up),
-                ],
-                axis=2,
-            )
+        first = plane_turn(jnp.concatenate([heads_split(enc_qkv), extra], axis=2))
+        rest = jnp.concatenate(
+            [heads_split(self_qkv), heads_split(cross_qkv), up_split(enc_up), up_split(dec_up)],
+            axis=2,
         )
+        first, rest = tie(first, rest)
+        rest = plane_turn(rest).reshape(4 * rows, -1)
         outs = out_turn(jnp.concatenate([enc_out_w, self_out, cross_out], axis=0))
-        pieces, packed = tie(pieces, packed)
-        first = jnp.concatenate([pieces[:, :, :width], outs[None, :rows]], axis=0)
-        first = jnp.stack([first] + [z_swap(first, k) for k in (1, 2, 3)])
-        rest = pieces[:, :, width:].reshape(4 * rows, -1)
+        turned, outs = outs[:rows], outs[rows:]
+        first, packed = tie(first, packed)
+        first = jnp.concatenate([first, turned[None]], axis=0)
+        far = z_swap(first, 2)
+        blocks = plane_gather(packed[: BLOCK + 8])
+        far, blocks, rest = tie(far, blocks, rest)
+        first = jnp.stack([first, far])
+        first = jnp.concatenate([first, z_swap(first, 1)], axis=0)
         narrow = ((0, 0), (0, width - heads_out))
         w_self = jnp.pad(rest[:, :heads_out], narrow)
         w_cross = jnp.pad(rest[:, heads_out : 2 * heads_out], narrow)
         up = rest[:, 2 * heads_out : 2 * heads_out + hidden]
-        one = jnp.concatenate([up, enc_down, outs[rows:], w_self], axis=0)
+        one = jnp.concatenate([up, enc_down, outs, w_self], axis=0)
         one = lax.all_gather(one, "z", axis=0)
         up = rest[:, 2 * heads_out + hidden :]
         two = jnp.concatenate([up, dec_down, w_cross], axis=0)
@@ -909,8 +958,10 @@
         ffn_shapes = [(rows, hidden), (rows_ff, width)]
         row = 4 * rows + rows_ff
 
-    src = packed[:BLOCK]
-    blocks = [packed] + [plane_swap(packed, k) for k in (1, 2, 3)]
+    start = BLOCK + 8
+    src, tgt, out_grad = packed[:BLOCK], packed[start : start + BLOCK], packed[start + BLOCK :]
+    if not split:
+        blocks = plane_gather(packed[:start])
     src_rows = [block[:BLOCK] for block in blocks]
     doc = jnp.concatenate([block[BLOCK : BLOCK + 1] for block in blocks], axis=0)
     doc = doc[:, : 2 * BLOCK].astype(F32).reshape(4, 2, BLOCK)
@@ -966,14 +1017,12 @@
         return own, core_swap(other)
 
     enc_form, self_form, cross_form = (0, 0, False), (1, 1, True), (1, 0, False)
-    q_enc, kv_enc = project(chain, "qk", 0, src_rows, w_enc, mine)
+    q_enc, kv_enc, src_rows = project(chain, 0, src_rows, w_enc, mine)
     kv_enc = with_others(kv_enc)
-    kv_enc, tgt = tie(kv_enc, tgt)
-    tgt = lax.ppermute(tgt, AXES, lay.token_moves())
-    o_enc, lse_enc, sent = attn_forward(chain, enc_form, count, q_enc, kv_enc, wo_enc)
+    enc_saved, sent = attn_forward(chain, enc_form, count, q_enc, kv_enc, wo_enc)
+    tgt_rows = plane_gather(tgt)
     sent = plane_send(sent)
-    sent, tgt = tie(sent, tgt)
-    r_enc1, e1, e1_low = norm(chain, src, sent, vectors, 2, 11, 16)
+    r_enc1, e1_low = norm(chain, src, sent, vectors, 2, (11, 16))
     e1_rows = plane_gather(e1_low)
     if split:
         e1_rows, one = tie(e1_rows, one)
@@ -985,19 +1034,20 @@
             one,
             core_swap(one),
         )
-    e1_rows, tgt = tie(e1_rows, tgt)
-    tgt_rows = plane_gather(tgt)
-    sent = plane_send(ffn_forward(chain, 0, e1_rows, w_up_enc, ups, w_down_enc))
-    q_self, kv_self = project(chain, "qk", 3, tgt_rows, w_self, mine)
+    q_self, kv_self, tgt_rows = project(chain, 3, tgt_rows, w_self, mine)
     kv_self = with_others(kv_self)
-    o_self, lse_self, self_sent = attn_forward(chain, self_form, count, q_self, kv_self, wo_self)
-    r_enc2, encoded, encoded_low = norm(chain, e1, sent, vectors, 9, 12, 17)
-    self_sent = plane_send(self_sent)
-    encoded_rows = plane_gather(encoded_low)
-    r_dec1, t1, t1_low = norm(chain, tgt, self_sent, vectors, 5, 13, 18)
-    t1_rows = plane_gather(t1_low)
+    self_saved, mates = attn_forward(chain, self_form, count, q_self, kv_self, wo_self)
+    e1_rows, sent = ffn_forward(chain, 0, e1_rows, w_up_enc, ups, w_down_enc, mates[1:])
+    sent = plane_send(sent)
+    r_enc2, encoded_low = norm(chain, r_enc1, sent, vectors, 9, (12, 17), (11, 16))
+    sent = [mates[0], *sent[1:]]
+    r_dec1, both_low = norm(
+        chain, tgt, sent, vectors, 5, (13, 18), start=BLOCK, mate=(encoded_low,)
+    )
     if split:
-        encoded_rows, two = tie(encoded_rows, two)
+        both_low, two = tie(both_low, two)
+    both_rows = plane_gather(both_low)
+    if split:
         w_up_dec, w_down_dec, w_cross = place(
             chain,
             ffn_plan + [("rows", row, 0)],
@@ -1006,17 +1056,15 @@
             two,
             core_swap(two),
         )
-    (kv_cross,) = project(chain, "k", 6, encoded_rows, w_cross, mine)
+    q_cross, kv_cross, both_rows = project(chain, 6, both_rows, w_cross, mine, q_start=BLOCK)
     kv_cross = with_others(kv_cross)
-    (q_cross,) = project(chain, "q", 6, t1_rows, w_cross, mine)
-    q_cross, out_grad = tie(q_cross, out_grad)
-    out_grad = lax.ppermute(out_grad, AXES, lay.token_moves())
-    o_cross, lse_cross, sent = attn_forward(chain, cross_form, count, q_cross, kv_cross, wo_cross)
-    r_dec2, t2, t2_low = norm(chain, t1, plane_send(sent), vectors, 8, 14, 19)
+    cross_saved, sent = attn_forward(chain, cross_form, count, q_cross, kv_cross, wo_cross)
+    sent = plane_send(sent)
+    r_dec2, t2_low = norm(chain, r_dec1, sent, vectors, 8, (14, 19), (13, 18))
     t2_rows = plane_gather(t2_low)
-    sent = plane_send(ffn_forward(chain, 1, t2_rows, w_up_dec, ups, w_down_dec))
-    sent, out_grad = tie(sent, out_grad)
-    r_dec3, _, t3_low = norm(chain, t2, sent, vectors, 10, 15, 20)
+    t2_rows, sent = ffn_forward(chain, 1, t2_rows, w_up_dec, ups, w_down_dec)
+    sent = plane_send(sent)
+    r_dec3, t3_low = norm(chain, r_dec2, sent, vectors, 10, (15, 20), (14, 19))
 
     heads_view = row_view + (heads_out + BLOCK,)
     up_view = row_view + (hidden,)
@@ -1055,6 +1103,9 @@
     def z_reduce(grad):
         return lax.psum_scatter(grad, "z", scatter_dimension=0, tiled=False)
 
+    def home(values):
+        return lax.ppermute(values, AXES, lay.back_moves())
+
     def ffn_sends(bias, up, down):
         sends = [core_send(up, "rows"), core_send(down, "down")]
         if split:
@@ -1074,23 +1125,12 @@
     low2_rows = plane_gather(low2)
     dec_ffn = z_reduce(stacked(*sends))
     dq, dkv, g_wo_cross = attn_backward(
-        chain,
-        cross_form,
+        chain, cross_form, split, count, cross_saved, low2_rows, out_view
+    )
+    spreads, g_bias_cross, g_cross = project_back(
+        chain,
         split,
-        count,
-        q_cross,
-        kv_cross,
-        low2_rows,
-        wo_cross,
-        o_cross,
-        lse_cross,
-        out_view,
-    )
-    spreads, g_bias_cross, g_cross = project_back(
-        chain,
-        True,
-        split,
-        t1_rows + encoded_rows,
+        both_rows,
         w_cross,
         dq,
         *own_part(dkv),
@@ -1098,56 +1138,34 @@
         [sums2, sums3],
         ((0, 2, 2), (1, 2, 3), (1, 0, 4), (1, 1, 5), (0, 0, 6), (0, 1, 7)),
     )
-    sent = plane_send(spreads[4:])
+    sent = plane_send(spreads[1:])
     sends = [core_send(g_cross, "rows"), core_send(g_wo_cross, "out")]
     sent, sends = tie(sent, sends)
 
     d_e2, low_e2, sums_e2 = norm_back(chain, sent, r_enc2, vectors, 12)
-    low_e2_rows = plane_gather(low_e2)
-    d_t1_sent = plane_send(spreads[:4])
+    d_r1, both_low, sums1 = norm_back(
+        chain, [d_r2, spreads[0], *sent[1:]], r_dec1, vectors, 13, start=BLOCK, mate=(low_e2,)
+    )
+    both_grads = plane_gather(both_low)
     cross = z_reduce(stacked(*sends))
+    both_grads, dec_ffn = tie(both_grads, dec_ffn)
     spreads, *grads = ffn_backward(
-        chain, 0, split, e1_rows, low_e2_rows, w_up_enc, ups, w_down_enc, up_view, down_view
+        chain, 0, split, e1_rows, both_grads, w_up_enc, ups, w_down_enc, up_view, down_view
     )
     upb_enc = grads[0]
     sent = plane_send(spreads)
-    d_r1, low1, sums1 = norm_back(chain, [d_r2, *d_t1_sent], r_dec1, vectors, 13)
     sends = ffn_sends(*grads)
-    sent, sends = tie(sent, sends)
-    low1_rows = plane_gather(low1)
+    dq_self, dkv_self, g_wo_self = attn_backward(
+        chain, self_form, split, count, self_saved, both_grads, out_view, start=BLOCK
+    )
+    enc_ffn = stacked(*sends)
+    sent, enc_ffn, dq_self = tie(sent, enc_ffn, dq_self)
+    enc_ffn = z_reduce(enc_ffn)
     d_r1e, low_e1, sums_e1 = norm_back(chain, [d_e2, *sent], r_enc1, vectors, 11)
 
     low_e1_rows = plane_gather(low_e1)
-    enc_ffn = z_reduce(stacked(*sends))
-    dq_self, dkv_self, g_wo_self = attn_backward(
-        chain,
-        self_form,
-        split,
-        count,
-        q_self,
-        kv_self,
-        low1_rows,
-        wo_self,
-        o_self,
-        lse_self,
-        out_view,
-    )
-    dq_enc, dkv_enc, g_wo_enc = attn_backward(
-        chain,
-        enc_form,
-        split,
-        count,
-        q_enc,
-        kv_enc,
-        low_e1_rows,
-        wo_enc,
-        o_enc,
-        lse_enc,
-        out_view,
-    )
     spreads_self, g_bias_self, g_self = project_back(
         chain,
-        False,
         split,
         tgt_rows,
         w_self,
@@ -1157,9 +1175,14 @@
         [sums1, sums_e2],
         ((0, 2, 2), (1, 2, 3), (0, 0, 4), (0, 1, 5), (1, 0, 6), (1, 1, 7)),
     )
+    self_sends = [core_send(g_self, "rows"), core_send(g_wo_self, "out")]
+    low_e1_rows, self_sends, cross = tie(low_e1_rows, self_sends, cross)
+    own_self = z_reduce(stacked(*self_sends))
+    dq_enc, dkv_enc, g_wo_enc = attn_backward(
+        chain, enc_form, split, count, enc_saved, low_e1_rows, out_view
+    )
     spreads, g_bias_enc, g_enc = project_back(
         chain,
-        False,
         split,
         src_rows,
         w_enc,
@@ -1168,41 +1191,35 @@
         heads_view,
         [sums_e1],
         ((0, 2, 2), (0, 0, 4), (0, 1, 5)),
+        mates=spreads_self[1:],
     )
     g_enc, g_wo_enc = core_send(g_enc, "rows"), core_send(g_wo_enc, "out")
+    g_enc, enc_ffn = tie(g_enc, enc_ffn)
     sent = plane_send(spreads)
-    self_sent = plane_send(spreads_self)
-    self_sends = [core_send(g_self, "rows"), core_send(g_wo_self, "out")]
 
     if split:
-        parts = shares(chain, g_enc, g_wo_enc, width)
-        parts = [parts[0]] + [z_swap(parts[k], k) for k in (1, 2, 3)]
-        own_self = z_reduce(stacked(*self_sends))
-        src_low = rounded_total(chain, [d_r1e, *sent])
-        tgt_low = rounded_total(chain, [d_r1, *self_sent])
-        dec_parts = jnp.concatenate(
+        own_sum, far_sum, near = shares(chain, g_enc, g_wo_enc, width)
+        near = z_swap(near, 1)
+        near, dec_ffn, cross, enc_ffn = tie(near, dec_ffn, cross, enc_ffn)
+        far_sum = z_swap(rounded_total(chain, [far_sum, near[1]]), 2)
+        homes = both_totals(chain, [d_r1e, sent[0], d_r1, spreads_self[0], *sent[1:], t3_low])
+        last = rounded_total(chain, [own_sum, near[0], far_sum])
+        parts = jnp.concatenate(
             [
+                enc_ffn[: 4 * rows].reshape(4, rows, hidden),
+                own_self[: 4 * rows, : heads_out + BLOCK].reshape(4, rows, heads_out + BLOCK),
+                last[:4],
                 dec_ffn[: 4 * rows].reshape(4, rows, hidden),
                 cross[: 4 * rows, : heads_out + BLOCK].reshape(4, rows, heads_out + BLOCK),
             ],
             axis=2,
         )
-        g_dec_up, g_cross_qkv, cross_lines = join_layer(chain, plane_turn(dec_parts), heads_out)
-        enc_parts = jnp.concatenate(
-            [
-                enc_ffn[: 4 * rows].reshape(4, rows, hidden),
-                own_self[: 4 * rows, : heads_out + BLOCK].reshape(4, rows, heads_out + BLOCK),
-            ],
-            axis=2,
-        )
-        last = rounded_total(chain, parts)
-        g_enc_up, g_self_qkv, self_lines = join_layer(chain, plane_turn(enc_parts), heads_out)
+        parts = plane_turn(parts)
         outs = jnp.concatenate([last[4], own_self[4 * rows :], cross[4 * rows :]], axis=0)
         outs = lax.ppermute(outs, ("z", "y", "x"), [(b, a) for a, b in lay.turn_moves()])
         outs = outs.astype(F32)
-        g_enc_qkv, *small = join_last(
-            chain, plane_turn(last[:4]), cross_lines, self_lines, heads_out
-        )
+        grads, small = join_last(chain, parts, heads_out)
+        g_enc_up, g_self_qkv, g_enc_qkv, g_dec_up, g_cross_qkv = grads
         small = [x[0] if x.shape[0] == 1 else x for x in small]
         tail = 4 * rows + rows_ff
         g_upb_enc, g_upb_dec = (x[tail, :rows_ff].astype(F32) for x in (enc_ffn, dec_ffn))
@@ -1219,9 +1236,7 @@
             parts = parts.reshape(4, rows, 2, groups, rows_ff).transpose(1, 3, 0, 2, 4)
             return parts.reshape(rows, -1).astype(F32)
 
-        src_low = plane_total([d_r1e + sent[0], *sent[1:]]).astype(BF16)
-        tgt_low = plane_total([d_r1 + self_sent[0], *self_sent[1:]]).astype(BF16)
-        own_self = z_reduce(stacked(*self_sends))
+        homes = both_totals(chain, [d_r1e, sent[0], d_r1, spreads_self[0], *sent[1:], t3_low])
         last = z_reduce(stacked(g_enc, g_wo_enc))
         g_dec_up, g_enc_up = up_join(dec_ffn[: 4 * rows]), up_join(enc_ffn[: 4 * rows])
         g_enc_down, g_dec_down = (x[4 * rows :].astype(F32) for x in (enc_ffn, dec_ffn))
@@ -1266,15 +1281,13 @@
         ]
     g_enc_out, g_self_out, g_cross_out = outs[:rows], outs[rows : 2 * rows], outs[2 * rows :]
 
-    def home(values):
-        return lax.ppermute(values, AXES, lay.back_moves())
-
+    homes = home(homes)
     bias_enc, down_enc, gains_enc, shifts_enc = small[:4]
     bias_self, bias_cross, down_dec, gains_dec, shifts_dec = small[4:]
     return (
-        home(t3_low)[None],
-        home(src_low).astype(F32)[None],
-        home(tgt_low).astype(F32)[None],
+        homes[None, 2 * BLOCK :],
+        homes[None, :BLOCK].astype(F32),
+        homes[None, BLOCK : 2 * BLOCK].astype(F32),
         g_enc_qkv,
         g_enc_out,
         bias_enc,

time: 535 us -> 495 us (0.925)
  starting transfers between devices: 159 us -> 98.1 us
  waiting for transfers between devices: 185 us -> 213 us
  Pallas kernels: 101 us -> 80.9 us
  local copies, waits for them, and re-layouts: 57.4 us -> 70.1 us
    ppermute x66 -> x51, starting transfers between devices: 96.2 us -> 67.5 us  [plane_swap(): return lax.ppermute(values, PLANE, [(i, i ^ shift) for i in range(4)])]
    pallas_call x41 -> x38, Pallas kernels: 101 us -> 80.9 us  [call(): pl.pallas_call(body, out_shape=(*outs, jax.ShapeDtypeStruct((8, BLOCK), F...]
    all_to_all x4 -> x3, waiting for transfers between devices: 17.5 us -> 31.1 us  [plane_turn(): lax.all_to_all(values, PLANE, split_axis=0, concat_axis=0, tiled=True)]
    unnamed x293 -> x274, local copies, waits for them, and re-layouts: 47.1 us -> 59.9 us
    ppermute x22, starting transfers between devices: 16 us -> 3.57 us  [core_swap(): return lax.ppermute(values, 'core', [(0, 1), (1, 0)])]
    ppermute x22, waiting for transfers between devices: 4.58 us -> 16.3 us  [core_swap(): return lax.ppermute(values, 'core', [(0, 1), (1, 0)])]
    ppermute x6 -> x4, starting transfers between devices: 13.4 us -> 4.15 us  [z_swap(): return lax.ppermute(values, 'z', [(z, z ^ shift) for z in range(groups)])]
    all_to_all x4 -> x3, starting transfers between devices: 25.6 us -> 17.7 us  [plane_turn(): lax.all_to_all(values, PLANE, split_axis=0, concat_axis=0, tiled=True)]
  transfers between devices with their start and end apart: 112 -> 90, of which waited for: 50 -> 49; matrix products, arithmetic and copies ran while one was open for 3% -> 4% of each run, Pallas kernels for 13% -> 13%
where the time goes in v3:
time: 495 us; the launch traced here: 490 us
  waiting for transfers between devices  213 us (43%)
  starting transfers between devices  98.1 us (20%)
  Pallas kernels  80.9 us (16%)
  local copies, waits for them, and re-layouts  70.1 us (14%)
  between operations  15.8 us (3%)
  other arithmetic  12.2 us (2%)
    ppermute x51, waiting for transfers between devices, plane_swap(): return lax.ppermute(values, PLANE, [(i, i ^ shift) for i in range(4)])  139 us
    pallas_call x38, Pallas kernels, call(): pl.pallas_call(body, out_shape=(*outs, jax.ShapeDtypeStruct((8, BLOCK), F...  80.9 us
    ppermute x51, starting transfers between devices, plane_swap(): return lax.ppermute(values, PLANE, [(i, i ^ shift) for i in range(4)])  67.5 us
    unnamed x274, local copies, waits for them, and re-layouts  59.9 us
    all_to_all x3, waiting for transfers between devices, plane_turn(): lax.all_to_all(values, PLANE, split_axis=0, concat_axis=0, tiled=True)  31.1 us
    ppermute x4, waiting for transfers between devices, z_swap(): return lax.ppermute(values, 'z', [(z, z ^ shift) for z in range(groups)])  21.8 us
    all_to_all x3, starting transfers between devices, plane_turn(): lax.all_to_all(values, PLANE, split_axis=0, concat_axis=0, tiled=True)  17.7 us
    ppermute x22, waiting for transfers between devices, core_swap(): return lax.ppermute(values, 'core', [(0, 1), (1, 0)])  16.3 us
  transfers between devices with their start and end apart: 90, of which 49 were waited for; matrix products, arithmetic and copies ran while one was open for 4% of the time, Pallas kernels for 13%

profile of v3, /device:TPU:0, one launch (start us, length us, event | category | flops | bytes accessed | tf_op | source)
XLA Modules:
  0.0 490.0 jit_solution(17385939358885966710)
XLA Ops:
  12.4 9.1 %all-to-all-start = ((bf16[4,24,768]{2,1,0:T(8,128)(2,1)}), bf16[4,24,768]{2,1,0:T(8,128)(2,1)S(1)}, u32[]{:S(2)}, u32[]{:S(2)}) async-start(bf16[4,24,768]{2,1,0:T(8,128)(2,1)} %pad_maximum_fusion.5), calls=%async_computation | async-start | bytes 294912 | tf_op jit(solution)/shard_map/all_to_all | solution.py:902
  25.1 10.7 %all-to-all-done = bf16[4,24,768]{2,1,0:T(8,128)(2,1)S(1)} async-done(((bf16[4,24,768]{2,1,0:T(8,128)(2,1)}), bf16[4,24,768]{2,1,0:T(8,128)(2,1)S(1)}, u32[]{:S(2)}, u32[]{:S(2)}) %all-to-all-start) | async-done | bytes 147488 | tf_op jit(solution)/shard_map/all_to_all | solution.py:902
  43.8 6.5 %collective-permute-start.4 = (bf16[136,768]{1,0:T(8,128)(2,1)S(1)}, bf16[136,768]{1,0:T(8,128)(2,1)S(1)}, u32[]{:S(2)}, u32[]{:S(2)}) collective-permute-start(bf16[136,768]{1,0:T(8,128)(2,1)S(1)} %slice.123), channel_id=1, source_target_pairs={{0,4},{2,6},{4,0},{6,2},{1,5},{3,7},{5,1},{7,3},{8,12},{10,14},{12... | collective-permute-start | bytes 626696 | tf_op jit(solution)/shard_map/ppermute | solution.py:775
  51.8 10.3 %collective-permute-done.2 = bf16[5,24,768]{2,1,0:T(8,128)(2,1)S(1)} collective-permute-done((bf16[5,24,768]{2,1,0:T(8,128)(2,1)S(1)}, bf16[5,24,768]{2,1,0:T(8,128)(2,1)S(1)}, u32[]{:S(2)}, u32[]{:S(2)}) %collective-permute-start.2) | collective-permute-done | bytes 184352 | tf_op jit(solution)/shard_map/ppermute | solution.py:780
  64.0 7.6 %collective-permute-done.10 = bf16[2,5,24,768]{3,2,1,0:T(8,128)(2,1)S(1)} collective-permute-done((bf16[2,5,24,768]{3,2,1,0:T(8,128)(2,1)S(1)}, bf16[2,5,24,768]{3,2,1,0:T(8,128)(2,1)S(1)}, u32[]{:S(2)}, u32[]{:S(2)}) %collective-permute-start.10) | collective-permute-done | bytes 368672 | tf_op jit(solution)/shard_map/ppermute | solution.py:780
  78.0 6.5 %attn_forward.3 = (bf16[512,1152]{1,0:T(8,128)(2,1)S(1)}, f32[8,512]{1,0:T(8,128)S(1)}, f32[128,768]{1,0:T(8,128)S(1)}, bf16[128,768]{1,0:T(8,128)(2,1)S(1)}, bf...) custom-call(s32[8,128]{1,0:T(8,128)S(1)} %add_convert_fusion.refs_0_, ...), custom_call_target="tpu_custom_call" | custom-call | flops 805306368 | bytes 3461120 | tf_op jit(solution)/shard_map/attn_forward/pallas_call | solution.py:120
  102.3 5.3 %collective-permute-done.18.refs_3_ = bf16[128,768]{1,0:T(8,128)(2,1)S(1)} collective-permute-done((bf16[128,768]{1,0:T(8,128)(2,1)S(1)}, bf16[128,768]{1,0:T(8,128)(2,1)S(1)}, u32[]{:S(2)}, u32[]{:S(2)}) %collective-permute-start.18) | collective-permute-done | bytes 196640 | tf_op jit(solution)/shard_map/ppermute | solution.py:775
  130.4 6.5 %attn_forward.4 = (bf16[512,1152]{1,0:T(8,128)(2,1)S(1)}, f32[8,512]{1,0:T(8,128)S(1)}, f32[128,768]{1,0:T(8,128)S(1)}, bf16[128,768]{1,0:T(8,128)(2,1)S(1)}, bf...) custom-call(s32[8,128]{1,0:T(8,128)S(1)} %add_convert_fusion.refs_0_, ...), custom_call_target="tpu_custom_call" | custom-call | flops 805306368 | bytes 3461120 | tf_op jit(solution)/shard_map/attn_forward/pallas_call | solution.py:120
  145.7 8.5 %collective-permute-done.21.refs_2_ = bf16[256,768]{1,0:T(8,128)(2,1)S(1)} collective-permute-done((bf16[256,768]{1,0:T(8,128)(2,1)S(1)}, bf16[256,768]{1,0:T(8,128)(2,1)S(1)}, u32[]{:S(2)}, u32[]{:S(2)}) %collective-permute-start.21) | collective-permute-done | bytes 393248 | tf_op jit(solution)/shard_map/ppermute | solution.py:775
  154.1 8.0 %collective-permute-done.22.refs_3_ = bf16[256,768]{1,0:T(8,128)(2,1)S(1)} collective-permute-done((bf16[256,768]{1,0:T(8,128)(2,1)S(1)}, bf16[256,768]{1,0:T(8,128)(2,1)S(1)}, u32[]{:S(2)}, u32[]{:S(2)}) %collective-permute-start.22) | collective-permute-done | bytes 393248 | tf_op jit(solution)/shard_map/ppermute | solution.py:775
  170.8 7.4 %collective-permute-done.26.refs_3_ = bf16[256,768]{1,0:T(8,128)(2,1)S(1)} collective-permute-done((bf16[256,768]{1,0:T(8,128)(2,1)}, bf16[256,768]{1,0:T(8,128)(2,1)S(1)}, u32[]{:S(2)}, u32[]{:S(2)}) %collective-permute-start.26) | collective-permute-done | bytes 393248 | tf_op jit(solution)/shard_map/ppermute | solution.py:775
  178.3 8.0 %collective-permute-done.25.refs_2_ = bf16[256,768]{1,0:T(8,128)(2,1)S(1)} collective-permute-done((bf16[256,768]{1,0:T(8,128)(2,1)}, bf16[256,768]{1,0:T(8,128)(2,1)S(1)}, u32[]{:S(2)}, u32[]{:S(2)}) %collective-permute-start.25) | collective-permute-done | bytes 393248 | tf_op jit(solution)/shard_map/ppermute | solution.py:775
  191.1 6.8 %attn_forward.5 = (bf16[512,1152]{1,0:T(8,128)(2,1)S(1)}, f32[8,512]{1,0:T(8,128)S(1)}, f32[128,768]{1,0:T(8,128)S(1)}, bf16[128,768]{1,0:T(8,128)(2,1)S(1)}, bf...) custom-call(s32[8,128]{1,0:T(8,128)S(1)} %add_convert_fusion.refs_0_, ...), custom_call_target="tpu_custom_call" | custom-call | flops 805306368 | bytes 3461120 | tf_op jit(solution)/shard_map/attn_forward/pallas_call | solution.py:120
  215.4 5.3 %collective-permute-done.34.refs_3_ = bf16[128,768]{1,0:T(8,128)(2,1)S(1)} collective-permute-done((bf16[128,768]{1,0:T(8,128)(2,1)S(1)}, bf16[128,768]{1,0:T(8,128)(2,1)S(1)}, u32[]{:S(2)}, u32[]{:S(2)}) %collective-permute-start.34) | collective-permute-done | bytes 196640 | tf_op jit(solution)/shard_map/ppermute | solution.py:775
  273.4 5.5 %collective-permute-done.49.refs_7_ = bf16[128,768]{1,0:T(8,128)(2,1)S(1)} collective-permute-done((bf16[128,768]{1,0:T(8,128)(2,1)}, bf16[128,768]{1,0:T(8,128)(2,1)S(1)}, u32[]{:S(2)}, u32[]{:S(2)}) %collective-permute-start.49) | collective-permute-done | bytes 196640 | tf_op jit(solution)/shard_map/ppermute | solution.py:775
  284.5 7.0 %attn_backward.3 = (bf16[512,192]{1,0:T(8,128)(2,1)S(1)}, f32[512,384]{1,0:T(8,128)S(1)}, f32[512,384]{1,0:T(8,128)S(1)}, f32[4,24,768]{2,1,0:T(8,128)S(1)}, bf1...) custom-call(s32[8,128]{1,0:T(8,128)S(1)} %add_convert_fusion.refs_0_, bf16[512,1152]{1,0:T(8,128)(2,1)S(1)} %copy-done.104, ...), custom_call_target="tpu_custom_call" | custom-call | flops 2013265920 | bytes 4493312 | tf_op jit(solution)/shard_map/attn_backward/pallas_call | solution.py:120
  301.2 7.1 %collective-permute-done.51.refs_1_.refs_2_ = bf16[256,768]{1,0:T(8,128)(2,1)S(1)} collective-permute-done((bf16[256,768]{1,0:T(8,128)(2,1)S(1)}, bf16[256,768]{1,0:T(8,128)(2,1)S(1)}, u32[]{:S(2)}, u32[]{:S(2)}) %collective-permute-start.51) | collective-permute-done | bytes 393248 | tf_op jit(solution)/shard_map/ppermute | solution.py:775
  308.3 8.3 %collective-permute-done.52.refs_2_.refs_3_ = bf16[256,768]{1,0:T(8,128)(2,1)S(1)} collective-permute-done((bf16[256,768]{1,0:T(8,128)(2,1)S(1)}, bf16[256,768]{1,0:T(8,128)(2,1)S(1)}, u32[]{:S(2)}, u32[]{:S(2)}) %collective-permute-start.52) | collective-permute-done | bytes 393248 | tf_op jit(solution)/shard_map/ppermute | solution.py:775
  324.9 9.5 %collective-permute-done.58.refs_4_.refs_7_ = bf16[256,768]{1,0:T(8,128)(2,1)S(1)} collective-permute-done((bf16[256,768]{1,0:T(8,128)(2,1)S(1)}, bf16[256,768]{1,0:T(8,128)(2,1)S(1)}, u32[]{:S(2)}, u32[]{:S(2)}) %collective-permute-start.58) | collective-permute-done | bytes 393248 | tf_op jit(solution)/shard_map/ppermute | solution.py:775
  335.2 5.8 %collective-permute-done.57.refs_3_.refs_6_ = bf16[256,768]{1,0:T(8,128)(2,1)S(1)} collective-permute-done((bf16[256,768]{1,0:T(8,128)(2,1)S(1)}, bf16[256,768]{1,0:T(8,128)(2,1)S(1)}, u32[]{:S(2)}, u32[]{:S(2)}) %collective-permute-start.57) | collective-permute-done | bytes 393248 | tf_op jit(solution)/shard_map/ppermute | solution.py:775
  350.2 5.2 %ffn_backward.3 = (f32[128,768]{1,0:T(8,128)S(1)}, bf16[128,768]{1,0:T(8,128)(2,1)S(1)}, bf16[128,768]{1,0:T(8,128)(2,1)S(1)}, bf16[128,768]{1,0:T(8,128)(2,1)S(...) custom-call(bf16[512,768]{1,0:T(8,128)(2,1)S(1)} %copy-done.98, ...), custom_call_target="tpu_custom_call" | custom-call | flops 3623878656 | bytes 9271296 | tf_op jit(solution)/shard_map/ffn_backward/pallas_call | solution.py:120
  359.9 7.0 %attn_backward.4 = (bf16[512,192]{1,0:T(8,128)(2,1)S(1)}, f32[512,384]{1,0:T(8,128)S(1)}, f32[512,384]{1,0:T(8,128)S(1)}, f32[4,24,768]{2,1,0:T(8,128)S(1)}, bf1...) custom-call(s32[8,128]{1,0:T(8,128)S(1)} %add_convert_fusion.refs_0_, bf16[512,1152]{1,0:T(8,128)(2,1)S(1)} %copy-done.102, ...), custom_call_target="tpu_custom_call" | custom-call | flops 2013265920 | bytes 5279744 | tf_op jit(solution)/shard_map/attn_backward/pallas_call | solution.py:120
  397.6 8.5 %attn_backward.5 = (bf16[512,192]{1,0:T(8,128)(2,1)S(1)}, f32[512,384]{1,0:T(8,128)S(1)}, f32[512,384]{1,0:T(8,128)}, f32[4,24,768]{2,1,0:T(8,128)S(1)}, bf16[4,...) custom-call(s32[8,128]{1,0:T(8,128)S(1)} %add_convert_fusion.refs_0_, bf16[512,1152]{1,0:T(8,128)(2,1)S(1)} %copy-done.100, ...), custom_call_target="tpu_custom_call" | custom-call | flops 2013265920 | bytes 4493312 | tf_op jit(solution)/shard_map/attn_backward/pallas_call | solution.py:120
  461.3 20.4 %all-to-all-done.2.refs_0_ = bf16[4,24,3712]{2,1,0:T(8,128)(2,1)S(1)} async-done(((bf16[4,24,3712]{2,1,0:T(8,128)(2,1)}), bf16[4,24,3712]{2,1,0:T(8,128)(2,1)S(1)}, u32[]{:S(2)}, u32[]{:S(2)}) %all-to-all-start.2) | async-done | bytes 712736 | tf_op jit(solution)/shard_map/all_to_all | solution.py:902
  (539 shorter events, 283.6 us)
Async XLA Ops:
  9.9 30.8 %collective-permute-start = (bf16[392,768]{1,0:T(8,128)(2,1)S(1)}, bf16[392,768]{1,0:T(8,128)(2,1)S(1)}, u32[]{:S(2)}, u32[]{:S(2)}) collective-permute-start(bf16[392,768]{1,0:T(8,128)(2,1)S(1)} %pad_maximum_fusion.1), channel_id=1, source_target_pairs={{0,0},{1,8},{2,16},{3,24},{4,4},{5,12},{6,20},{7,28},{8,2},{9,10},... | collective-permute-start | bytes 1806344 | tf_op jit(solution)/shard_map/ppermute | solution.py:879
  12.4 23.3 %all-to-all-start = ((bf16[4,24,768]{2,1,0:T(8,128)(2,1)}), bf16[4,24,768]{2,1,0:T(8,128)(2,1)S(1)}, u32[]{:S(2)}, u32[]{:S(2)}) async-start(bf16[4,24,768]{2,1,0:T(8,128)(2,1)} %pad_maximum_fusion.5), calls=%async_computation | async-start | bytes 294912 | tf_op jit(solution)/shard_map/all_to_all | solution.py:902
  21.5 19.3 %collective-permute-start.1 = (bf16[72,768]{1,0:T(8,128)(2,1)S(1)}, bf16[72,768]{1,0:T(8,128)(2,1)S(1)}, u32[]{:S(2)}, u32[]{:S(2)}) collective-permute-start(bf16[72,768]{1,0:T(8,128)(2,1)S(1)} %pad_maximum_fusion.6), channel_id=1, source_target_pairs={{0,0},{2,8},{4,16},{6,24},{8,2},{10,10},{12,18},{14,26},{16,4},{18... | collective-permute-start | bytes 331784 | tf_op jit(solution)/shard_map/ppermute | solution.py:905
  40.7 70.6 %all-gather.5.cloned.1.call-start = ((), (), s32[]{:S(2)}) async-start(), calls=%async_computation.11 | async-start | bytes 2580480 | tf_op jit(solution)/shard_map/all_gather | solution.py:953
  40.8 21.3 %collective-permute-start.5 = (bf16[136,768]{1,0:T(8,128)(2,1)S(1)}, bf16[136,768]{1,0:T(8,128)(2,1)S(1)}, u32[]{:S(2)}, u32[]{:S(2)}) collective-permute-start(bf16[136,768]{1,0:T(8,128)(2,1)S(1)} %slice.123), channel_id=1, source_target_pairs={{0,6},{2,4},{4,2},{6,0},{1,7},{3,5},{5,3},{7,1},{8,14},{10,12},{12... | collective-permute-start | bytes 626696 | tf_op jit(solution)/shard_map/ppermute | solution.py:775
  43.8 18.3 %collective-permute-start.4 = (bf16[136,768]{1,0:T(8,128)(2,1)S(1)}, bf16[136,768]{1,0:T(8,128)(2,1)S(1)}, u32[]{:S(2)}, u32[]{:S(2)}) collective-permute-start(bf16[136,768]{1,0:T(8,128)(2,1)S(1)} %slice.123), channel_id=1, source_target_pairs={{0,4},{2,6},{4,0},{6,2},{1,5},{3,7},{5,1},{7,3},{8,12},{10,14},{12... | collective-permute-start | bytes 626696 | tf_op jit(solution)/shard_map/ppermute | solution.py:775
  63.7 101.5 %all-gather.7.cloned.1.call-start = ((), (), s32[]{:S(2)}) async-start(), calls=%async_computation.12 | async-start | bytes 2211840 | tf_op jit(solution)/shard_map/all_gather | solution.py:956
  114.2 228.4 %reduce-scatter.5.cloned.1.call-start = ((), (), s32[]{:S(2)}) async-start(), calls=%async_computation.7 | async-start | bytes 1536000 | tf_op jit(solution)/shard_map/reduce_scatter | solution.py:1104
  142.8 19.3 %collective-permute-start.22 = (bf16[256,768]{1,0:T(8,128)(2,1)S(1)}, bf16[256,768]{1,0:T(8,128)(2,1)S(1)}, u32[]{:S(2)}, u32[]{:S(2)}) collective-permute-start(bf16[256,768]{1,0:T(8,128)(2,1)S(1)} %get-tuple-element.321), channel_id=1, source_target_pairs={{0,4},{2,6},{4,0},{6,2},{1,5},{3,7},{5,1},{7,3},{8,12},{10,14},{12... | collective-permute-start | bytes 1179656 | tf_op jit(solution)/shard_map/ppermute | solution.py:775
  144.2 17.9 %collective-permute-start.23 = (bf16[256,768]{1,0:T(8,128)(2,1)S(1)}, bf16[256,768]{1,0:T(8,128)(2,1)S(1)}, u32[]{:S(2)}, u32[]{:S(2)}) collective-permute-start(bf16[256,768]{1,0:T(8,128)(2,1)S(1)} %get-tuple-element.322), channel_id=1, source_target_pairs={{0,6},{2,4},{4,2},{6,0},{1,7},{3,5},{5,3},{7,1},{8,14},{10,12},{12... | collective-permute-start | bytes 1179656 | tf_op jit(solution)/shard_map/ppermute | solution.py:775
  166.7 19.6 %collective-permute-start.25 = (bf16[256,768]{1,0:T(8,128)(2,1)}, bf16[256,768]{1,0:T(8,128)(2,1)S(1)}, u32[]{:S(2)}, u32[]{:S(2)}) collective-permute-start(bf16[256,768]{1,0:T(8,128)(2,1)} %get-tuple-element.329.refs_0_), channel_id=1, source_target_pairs={{0,4},{2,6},{4,0},{6,2},{1,5},{3,7},{5,1},{7,3},{8,12},{10,14},{12... | collective-permute-start | bytes 1179656 | tf_op jit(solution)/shard_map/ppermute | solution.py:775
  168.1 18.2 %collective-permute-start.24 = (bf16[256,768]{1,0:T(8,128)(2,1)}, bf16[256,768]{1,0:T(8,128)(2,1)S(1)}, u32[]{:S(2)}, u32[]{:S(2)}) collective-permute-start(bf16[256,768]{1,0:T(8,128)(2,1)} %get-tuple-element.329.refs_0_), channel_id=1, source_target_pairs={{0,2},{2,0},{4,6},{6,4},{1,3},{3,1},{5,7},{7,5},{8,10},{10,8},{12,... | collective-permute-start | bytes 1179656 | tf_op jit(solution)/shard_map/ppermute | solution.py:775
  269.8 118.4 %reduce-scatter.7.cloned.1.call-start = ((), (), s32[]{:S(2)}) async-start(), calls=%async_computation.8 | async-start | bytes 921600 | tf_op jit(solution)/shard_map/reduce_scatter | solution.py:1104
  296.1 20.5 %collective-permute-start.54 = (bf16[4,4,24,704]{3,2,1,0:T(8,128)(2,1)S(1)}, bf16[4,4,24,704]{3,2,1,0:T(8,128)(2,1)S(1)}, u32[]{:S(2)}, u32[]{:S(2)}) collective-permute-start(bf16[4,4,24,704]{3,2,1,0:T(8,128)(2,1)S(1)} %get-tuple-element.398), channel_id=1, source_target_pairs={{0,1},{1,0},{2,3},{3,2},{4,5},{5,4},{6,7},{7,6},{8,9},{9,8},{10,11... | collective-permute-start | bytes 1622024 | tf_op jit(solution)/shard_map/ppermute | solution.py:784
  297.1 19.5 %collective-permute-start.52 = (bf16[256,768]{1,0:T(8,128)(2,1)S(1)}, bf16[256,768]{1,0:T(8,128)(2,1)S(1)}, u32[]{:S(2)}, u32[]{:S(2)}) collective-permute-start(bf16[256,768]{1,0:T(8,128)(2,1)S(1)} %get-tuple-element.395), channel_id=1, source_target_pairs={{0,4},{2,6},{4,0},{6,2},{1,5},{3,7},{5,1},{7,3},{8,12},{10,14},{12... | collective-permute-start | bytes 1179656 | tf_op jit(solution)/shard_map/ppermute | solution.py:775
  298.5 18.1 %collective-permute-start.53 = (bf16[256,768]{1,0:T(8,128)(2,1)S(1)}, bf16[256,768]{1,0:T(8,128)(2,1)S(1)}, u32[]{:S(2)}, u32[]{:S(2)}) collective-permute-start(bf16[256,768]{1,0:T(8,128)(2,1)S(1)} %get-tuple-element.396), channel_id=1, source_target_pairs={{0,6},{2,4},{4,2},{6,0},{1,7},{3,5},{5,3},{7,1},{8,14},{10,12},{12... | collective-permute-start | bytes 1179656 | tf_op jit(solution)/shard_map/ppermute | solution.py:775
  320.9 102.1 %reduce-scatter.9.cloned.1.call-start = ((), (), s32[]{:S(2)}) async-start(), calls=%async_computation.9 | async-start | bytes 1536000 | tf_op jit(solution)/shard_map/reduce_scatter | solution.py:1104
  322.8 18.2 %collective-permute-start.57 = (bf16[256,768]{1,0:T(8,128)(2,1)S(1)}, bf16[256,768]{1,0:T(8,128)(2,1)S(1)}, u32[]{:S(2)}, u32[]{:S(2)}) collective-permute-start(bf16[256,768]{1,0:T(8,128)(2,1)S(1)} %copy-done.71), channel_id=1, source_target_pairs={{0,4},{2,6},{4,0},{6,2},{1,5},{3,7},{5,1},{7,3},{8,12},{10,14},{12... | collective-permute-start | bytes 1179656 | tf_op jit(solution)/shard_map/ppermute | solution.py:775
  324.2 17.6 %collective-permute-start.56 = (bf16[256,768]{1,0:T(8,128)(2,1)S(1)}, bf16[256,768]{1,0:T(8,128)(2,1)S(1)}, u32[]{:S(2)}, u32[]{:S(2)}) collective-permute-start(bf16[256,768]{1,0:T(8,128)(2,1)S(1)} %copy-done.71), channel_id=1, source_target_pairs={{0,2},{2,0},{4,6},{6,4},{1,3},{3,1},{5,7},{7,5},{8,10},{10,8},{12,... | collective-permute-start | bytes 1179656 | tf_op jit(solution)/shard_map/ppermute | solution.py:775
  372.6 63.1 %reduce-scatter.11.cloned.1.call-start = ((), (), s32[]{:S(2)}) async-start(), calls=%async_computation.10 | async-start | bytes 921600 | tf_op jit(solution)/shard_map/reduce_scatter | solution.py:1104
  427.8 18.4 %collective-permute-start.72 = (bf16[256,768]{1,0:T(8,128)(2,1)}, bf16[256,768]{1,0:T(8,128)(2,1)S(1)}, u32[]{:S(2)}, u32[]{:S(2)}) collective-permute-start(bf16[256,768]{1,0:T(8,128)(2,1)} %get-tuple-element.484), channel_id=1, source_target_pairs={{0,2},{2,0},{4,6},{6,4},{1,3},{3,1},{5,7},{7,5},{8,10},{10,8},{12,... | collective-permute-start | bytes 1179656 | tf_op jit(solution)/shard_map/ppermute | solution.py:775
  428.7 19.2 %collective-permute-start.73 = (bf16[256,768]{1,0:T(8,128)(2,1)}, bf16[256,768]{1,0:T(8,128)(2,1)S(1)}, u32[]{:S(2)}, u32[]{:S(2)}) collective-permute-start(bf16[256,768]{1,0:T(8,128)(2,1)} %get-tuple-element.485), channel_id=1, source_target_pairs={{0,4},{2,6},{4,0},{6,2},{1,5},{3,7},{5,1},{7,3},{8,12},{10,14},{12... | collective-permute-start | bytes 1179656 | tf_op jit(solution)/shard_map/ppermute | solution.py:775
  429.7 18.3 %collective-permute-start.74 = (bf16[256,768]{1,0:T(8,128)(2,1)}, bf16[256,768]{1,0:T(8,128)(2,1)S(1)}, u32[]{:S(2)}, u32[]{:S(2)}) collective-permute-start(bf16[256,768]{1,0:T(8,128)(2,1)} %get-tuple-element.486), channel_id=1, source_target_pairs={{0,6},{2,4},{4,2},{6,0},{1,7},{3,5},{5,3},{7,1},{8,14},{10,12},{12... | collective-permute-start | bytes 1179656 | tf_op jit(solution)/shard_map/ppermute | solution.py:775
  454.2 27.6 %all-to-all-start.2 = ((bf16[4,24,3712]{2,1,0:T(8,128)(2,1)}), bf16[4,24,3712]{2,1,0:T(8,128)(2,1)S(1)}, u32[]{:S(2)}, u32[]{:S(2)}) async-start(bf16[4,24,3712]{2,1,0:T(8,128)(2,1)} %concatenate.63), calls=%async_computation.6 | async-start | bytes 1425408 | tf_op jit(solution)/shard_map/all_to_all | solution.py:902
  (203 other events, 1259.9 us)
Sparse Core Ops, SparseCore 0:
  63.8 46.0 all-gather.4
  114.3 42.9 all-gather.6
  269.9 32.5 reduce-scatter.4
  321.0 26.1 reduce-scatter.6
  372.7 33.3 reduce-scatter.8
  408.6 27.0 reduce-scatter.10

commit v4 on v3

--- a/solution.py
+++ b/solution.py
@@ -594,6 +594,36 @@
     return out
 
 
+def turned_kernel(count, *refs):
+    group = lax.axis_index("z")
+    outs = refs[2 * count :]
+    targets = (outs[0], outs[1], outs[2].at[0], outs[2].at[1])
+    for target, shift in zip(targets, (0, 2, 1, 3), strict=True):
+        z, row = group ^ shift, 0
+        for keep_ref, got_ref in zip(refs[:count], refs[count : 2 * count], strict=True):
+            total = (keep_ref[z] + got_ref[z].astype(F32)).astype(target.dtype)
+            size, cols = total.shape
+            target[row : row + size, :cols] = total
+            if cols < target.shape[1]:
+                target[row : row + size, cols:] = jnp.zeros(
+                    (size, target.shape[1] - cols), target.dtype
+                )
+            row += size
+
+
+def group_sums(chain, sends, width):
+    keeps = [x[0].reshape(4, -1, x[0].shape[-1]) for x in sends]
+    gots = [x[1].reshape(4, -1, x[1].shape[-1]) for x in sends]
+    shape = (sum(x.shape[1] for x in keeps), width)
+    return call(
+        chain,
+        functools.partial(turned_kernel, len(keeps)),
+        "turn_gradients",
+        [*keeps, *gots],
+        [jax.ShapeDtypeStruct(shape, F32)] * 2 + [jax.ShapeDtypeStruct((2, *shape), BF16)],
+    )
+
+
 def shares_kernel(keep_ref, got_ref, keep_out, got_out, *out_refs):
     group = lax.axis_index("z")
     cols, wide = keep_ref.shape[-1], out_refs[0].shape[-1]
@@ -1123,7 +1153,7 @@
     d_r2, low2, sums2 = norm_back(chain, [d_r3, *sent], r_dec2, vectors, 14)
 
     low2_rows = plane_gather(low2)
-    dec_ffn = z_reduce(stacked(*sends))
+    dec_sends = sends
     dq, dkv, g_wo_cross = attn_backward(
         chain, cross_form, split, count, cross_saved, low2_rows, out_view
     )
@@ -1147,8 +1177,7 @@
         chain, [d_r2, spreads[0], *sent[1:]], r_dec1, vectors, 13, start=BLOCK, mate=(low_e2,)
     )
     both_grads = plane_gather(both_low)
-    cross = z_reduce(stacked(*sends))
-    both_grads, dec_ffn = tie(both_grads, dec_ffn)
+    decoder = z_reduce(stacked(*dec_sends, *sends))
     spreads, *grads = ffn_backward(
         chain, 0, split, e1_rows, both_grads, w_up_enc, ups, w_down_enc, up_view, down_view
     )
@@ -1158,12 +1187,15 @@
     dq_self, dkv_self, g_wo_self = attn_backward(
         chain, self_form, split, count, self_saved, both_grads, out_view, start=BLOCK
     )
-    enc_ffn = stacked(*sends)
-    sent, enc_ffn, dq_self = tie(sent, enc_ffn, dq_self)
-    enc_ffn = z_reduce(enc_ffn)
+    enc_sends = sends
+    if split:
+        enc_own, enc_far, enc_near = group_sums(chain, enc_sends, width)
+        enc_near = z_swap(enc_near, 1)
     d_r1e, low_e1, sums_e1 = norm_back(chain, [d_e2, *sent], r_enc1, vectors, 11)
 
     low_e1_rows = plane_gather(low_e1)
+    if split:
+        enc_far = z_swap(rounded_total(chain, [enc_far, enc_near[1]]), 2)
     spreads_self, g_bias_self, g_self = project_back(
         chain,
         split,
@@ -1176,8 +1208,12 @@
         ((0, 2, 2), (1, 2, 3), (0, 0, 4), (0, 1, 5), (1, 0, 6), (1, 1, 7)),
     )
     self_sends = [core_send(g_self, "rows"), core_send(g_wo_self, "out")]
-    low_e1_rows, self_sends, cross = tie(low_e1_rows, self_sends, cross)
-    own_self = z_reduce(stacked(*self_sends))
+    if split:
+        low_e1_rows, enc_far = tie(low_e1_rows, enc_far)
+    own_self, decoder = tie(stacked(*self_sends), decoder)
+    own_self = z_reduce(own_self)
+    tall = decoder.shape[0] - 5 * rows
+    dec_ffn, cross = decoder[:tall], decoder[tall:]
     dq_enc, dkv_enc, g_wo_enc = attn_backward(
         chain, enc_form, split, count, enc_saved, low_e1_rows, out_view
     )
@@ -1194,13 +1230,14 @@
         mates=spreads_self[1:],
     )
     g_enc, g_wo_enc = core_send(g_enc, "rows"), core_send(g_wo_enc, "out")
-    g_enc, enc_ffn = tie(g_enc, enc_ffn)
     sent = plane_send(spreads)
 
     if split:
         own_sum, far_sum, near = shares(chain, g_enc, g_wo_enc, width)
         near = z_swap(near, 1)
-        near, dec_ffn, cross, enc_ffn = tie(near, dec_ffn, cross, enc_ffn)
+        near, decoder = tie(near, decoder)
+        dec_ffn, cross = decoder[:tall], decoder[tall:]
+        enc_ffn = rounded_total(chain, [enc_own, enc_near[0], enc_far])
         far_sum = z_swap(rounded_total(chain, [far_sum, near[1]]), 2)
         homes = both_totals(chain, [d_r1e, sent[0], d_r1, spreads_self[0], *sent[1:], t3_low])
         last = rounded_total(chain, [own_sum, near[0], far_sum])
@@ -1238,6 +1275,7 @@
 
         homes = both_totals(chain, [d_r1e, sent[0], d_r1, spreads_self[0], *sent[1:], t3_low])
         last = z_reduce(stacked(g_enc, g_wo_enc))
+        enc_ffn = z_reduce(stacked(*enc_sends))
         g_dec_up, g_enc_up = up_join(dec_ffn[: 4 * rows]), up_join(enc_ffn[: 4 * rows])
         g_enc_down, g_dec_down = (x[4 * rows :].astype(F32) for x in (enc_ffn, dec_ffn))
         g_cross_qkv, g_self_qkv, g_enc_qkv = (

time: 495 us -> 482 us (0.974)
  local copies, waits for them, and re-layouts: 70.1 us -> 34.8 us
  waiting for transfers between devices: 213 us -> 238 us
    ppermute x4 -> x6, waiting for transfers between devices: 21.8 us -> 59.5 us  [z_swap(): return lax.ppermute(values, 'z', [(z, z ^ shift) for z in range(groups)])]
    unnamed x274 -> x166, local copies, waits for them, and re-layouts: 59.9 us -> 26.5 us
    all_to_all x3, waiting for transfers between devices: 31.1 us -> 21.4 us  [plane_turn(): lax.all_to_all(values, PLANE, split_axis=0, concat_axis=0, tiled=True)]
    pallas_call x38 -> x39, Pallas kernels: 80.9 us -> 77.5 us  [call(): pl.pallas_call(body, out_shape=(*outs, jax.ShapeDtypeStruct((8, BLOCK), F...]
  transfers between devices with their start and end apart: 90 -> 90, of which waited for: 49 -> 47; matrix products, arithmetic and copies ran while one was open for 4% -> 3% of each run, Pallas kernels for 13% -> 10%
where the time goes in v4:
time: 482 us; the launch traced here: 475 us
  waiting for transfers between devices  238 us (49%)
  starting transfers between devices  98.9 us (21%)
  Pallas kernels  77.5 us (16%)
  local copies, waits for them, and re-layouts  34.8 us (7%)
  between operations  15.6 us (3%)
  other arithmetic  10.5 us (2%)
    ppermute x51, waiting for transfers between devices, plane_swap(): return lax.ppermute(values, PLANE, [(i, i ^ shift) for i in range(4)])  144 us
    pallas_call x39, Pallas kernels, call(): pl.pallas_call(body, out_shape=(*outs, jax.ShapeDtypeStruct((8, BLOCK), F...  77.5 us
    ppermute x51, starting transfers between devices, plane_swap(): return lax.ppermute(values, PLANE, [(i, i ^ shift) for i in range(4)])  67.4 us
    ppermute x6, waiting for transfers between devices, z_swap(): return lax.ppermute(values, 'z', [(z, z ^ shift) for z in range(groups)])  59.5 us
    unnamed x166, local copies, waits for them, and re-layouts  26.5 us
    all_to_all x3, waiting for transfers between devices, plane_turn(): lax.all_to_all(values, PLANE, split_axis=0, concat_axis=0, tiled=True)  21.4 us
    all_to_all x3, starting transfers between devices, plane_turn(): lax.all_to_all(values, PLANE, split_axis=0, concat_axis=0, tiled=True)  19.4 us
    ppermute x22, waiting for transfers between devices, core_swap(): return lax.ppermute(values, 'core', [(0, 1), (1, 0)])  12.9 us
  transfers between devices with their start and end apart: 90, of which 47 were waited for; matrix products, arithmetic and copies ran while one was open for 3% of the time, Pallas kernels for 10%

profile of v4, /device:TPU:0, one launch (start us, length us, event | category | flops | bytes accessed | tf_op | source)
XLA Modules:
  0.0 475.0 jit_solution(3581529643731120501)
XLA Ops:
  12.4 9.1 %all-to-all-start = ((bf16[4,24,768]{2,1,0:T(8,128)(2,1)}), bf16[4,24,768]{2,1,0:T(8,128)(2,1)S(1)}, u32[]{:S(2)}, u32[]{:S(2)}) async-start(bf16[4,24,768]{2,1,0:T(8,128)(2,1)} %pad_maximum_fusion.5), calls=%async_computation | async-start | bytes 294912 | tf_op jit(solution)/shard_map/all_to_all | solution.py:932
  25.0 10.7 %all-to-all-done = bf16[4,24,768]{2,1,0:T(8,128)(2,1)S(1)} async-done(((bf16[4,24,768]{2,1,0:T(8,128)(2,1)}), bf16[4,24,768]{2,1,0:T(8,128)(2,1)S(1)}, u32[]{:S(2)}, u32[]{:S(2)}) %all-to-all-start) | async-done | bytes 147488 | tf_op jit(solution)/shard_map/all_to_all | solution.py:932
  43.8 6.5 %collective-permute-start.4 = (bf16[136,768]{1,0:T(8,128)(2,1)S(1)}, bf16[136,768]{1,0:T(8,128)(2,1)S(1)}, u32[]{:S(2)}, u32[]{:S(2)}) collective-permute-start(bf16[136,768]{1,0:T(8,128)(2,1)S(1)} %slice.136), channel_id=1, source_target_pairs={{0,4},{2,6},{4,0},{6,2},{1,5},{3,7},{5,1},{7,3},{8,12},{10,14},{12... | collective-permute-start | bytes 626696 | tf_op jit(solution)/shard_map/ppermute | solution.py:805
  51.8 10.3 %collective-permute-done.2 = bf16[5,24,768]{2,1,0:T(8,128)(2,1)S(1)} collective-permute-done((bf16[5,24,768]{2,1,0:T(8,128)(2,1)S(1)}, bf16[5,24,768]{2,1,0:T(8,128)(2,1)S(1)}, u32[]{:S(2)}, u32[]{:S(2)}) %collective-permute-start.2) | collective-permute-done | bytes 184352 | tf_op jit(solution)/shard_map/ppermute | solution.py:810
  64.1 7.6 %collective-permute-done.10 = bf16[2,5,24,768]{3,2,1,0:T(8,128)(2,1)S(1)} collective-permute-done((bf16[2,5,24,768]{3,2,1,0:T(8,128)(2,1)S(1)}, bf16[2,5,24,768]{3,2,1,0:T(8,128)(2,1)S(1)}, u32[]{:S(2)}, u32[]{:S(2)}) %collective-permute-start.10) | collective-permute-done | bytes 368672 | tf_op jit(solution)/shard_map/ppermute | solution.py:810
  78.0 6.5 %attn_forward.3 = (bf16[512,1152]{1,0:T(8,128)(2,1)S(1)}, f32[8,512]{1,0:T(8,128)S(1)}, f32[128,768]{1,0:T(8,128)S(1)}, bf16[128,768]{1,0:T(8,128)(2,1)S(1)}, bf...) custom-call(s32[8,128]{1,0:T(8,128)S(1)} %add_convert_fusion.refs_0_, ...), custom_call_target="tpu_custom_call" | custom-call | flops 805306368 | bytes 3461120 | tf_op jit(solution)/shard_map/attn_forward/pallas_call | solution.py:120
  145.4 8.5 %collective-permute-done.21.refs_2_ = bf16[256,768]{1,0:T(8,128)(2,1)S(1)} collective-permute-done((bf16[256,768]{1,0:T(8,128)(2,1)S(1)}, bf16[256,768]{1,0:T(8,128)(2,1)S(1)}, u32[]{:S(2)}, u32[]{:S(2)}) %collective-permute-start.21) | collective-permute-done | bytes 393248 | tf_op jit(solution)/shard_map/ppermute | solution.py:805
  153.9 7.9 %collective-permute-done.22.refs_3_ = bf16[256,768]{1,0:T(8,128)(2,1)S(1)} collective-permute-done((bf16[256,768]{1,0:T(8,128)(2,1)S(1)}, bf16[256,768]{1,0:T(8,128)(2,1)S(1)}, u32[]{:S(2)}, u32[]{:S(2)}) %collective-permute-start.22) | collective-permute-done | bytes 393248 | tf_op jit(solution)/shard_map/ppermute | solution.py:805
  169.8 7.4 %collective-permute-done.26.refs_3_ = bf16[256,768]{1,0:T(8,128)(2,1)S(1)} collective-permute-done((bf16[256,768]{1,0:T(8,128)(2,1)}, bf16[256,768]{1,0:T(8,128)(2,1)S(1)}, u32[]{:S(2)}, u32[]{:S(2)}) %collective-permute-start.26) | collective-permute-done | bytes 393248 | tf_op jit(solution)/shard_map/ppermute | solution.py:805
  177.3 8.0 %collective-permute-done.25.refs_2_ = bf16[256,768]{1,0:T(8,128)(2,1)S(1)} collective-permute-done((bf16[256,768]{1,0:T(8,128)(2,1)}, bf16[256,768]{1,0:T(8,128)(2,1)S(1)}, u32[]{:S(2)}, u32[]{:S(2)}) %collective-permute-start.25) | collective-permute-done | bytes 393248 | tf_op jit(solution)/shard_map/ppermute | solution.py:805
  187.9 6.8 %attn_forward.5 = (bf16[512,1152]{1,0:T(8,128)(2,1)S(1)}, f32[8,512]{1,0:T(8,128)S(1)}, f32[128,768]{1,0:T(8,128)S(1)}, bf16[128,768]{1,0:T(8,128)(2,1)S(1)}, bf...) custom-call(s32[8,128]{1,0:T(8,128)S(1)} %add_convert_fusion.refs_0_, ...), custom_call_target="tpu_custom_call" | custom-call | flops 805306368 | bytes 3461120 | tf_op jit(solution)/shard_map/attn_forward/pallas_call | solution.py:120
  274.4 7.0 %attn_backward.3 = (bf16[512,192]{1,0:T(8,128)(2,1)S(1)}, f32[512,384]{1,0:T(8,128)S(1)}, f32[512,384]{1,0:T(8,128)S(1)}, f32[4,24,768]{2,1,0:T(8,128)S(1)}, bf1...) custom-call(s32[8,128]{1,0:T(8,128)S(1)} %add_convert_fusion.refs_0_, ...), custom_call_target="tpu_custom_call" | custom-call | flops 2013265920 | bytes 4493312 | tf_op jit(solution)/shard_map/attn_backward/pallas_call | solution.py:120
  291.0 7.1 %collective-permute-done.51.refs_1_.refs_2_ = bf16[256,768]{1,0:T(8,128)(2,1)S(1)} collective-permute-done((bf16[256,768]{1,0:T(8,128)(2,1)S(1)}, bf16[256,768]{1,0:T(8,128)(2,1)S(1)}, u32[]{:S(2)}, u32[]{:S(2)}) %collective-permute-start.51) | collective-permute-done | bytes 393248 | tf_op jit(solution)/shard_map/ppermute | solution.py:805
  298.1 8.4 %collective-permute-done.52.refs_2_.refs_3_ = bf16[256,768]{1,0:T(8,128)(2,1)S(1)} collective-permute-done((bf16[256,768]{1,0:T(8,128)(2,1)S(1)}, bf16[256,768]{1,0:T(8,128)(2,1)S(1)}, u32[]{:S(2)}, u32[]{:S(2)}) %collective-permute-start.52) | collective-permute-done | bytes 393248 | tf_op jit(solution)/shard_map/ppermute | solution.py:805
  313.5 7.8 %collective-permute-done.58.refs_4_.refs_7_ = bf16[256,768]{1,0:T(8,128)(2,1)S(1)} collective-permute-done((bf16[256,768]{1,0:T(8,128)(2,1)}, bf16[256,768]{1,0:T(8,128)(2,1)S(1)}, u32[]{:S(2)}, u32[]{:S(2)}) %collective-permute-start.58) | collective-permute-done | bytes 393248 | tf_op jit(solution)/shard_map/ppermute | solution.py:805
  321.3 6.7 %collective-permute-done.57.refs_3_.refs_6_ = bf16[256,768]{1,0:T(8,128)(2,1)} collective-permute-done((bf16[256,768]{1,0:T(8,128)(2,1)}, bf16[256,768]{1,0:T(8,128)(2,1)}, u32[]{:S(2)}, u32[]{:S(2)}) %collective-permute-start.57) | collective-permute-done | bytes 393248 | tf_op jit(solution)/shard_map/ppermute | solution.py:805
  331.7 6.5 %ffn_backward.3 = (f32[128,768]{1,0:T(8,128)S(1)}, bf16[128,768]{1,0:T(8,128)(2,1)S(1)}, bf16[128,768]{1,0:T(8,128)(2,1)S(1)}, bf16[128,768]{1,0:T(8,128)(2,1)S(...) custom-call(bf16[512,768]{1,0:T(8,128)(2,1)S(1)} %copy-done.51, ...), custom_call_target="tpu_custom_call" | custom-call | flops 3623878656 | bytes 9271296 | tf_op jit(solution)/shard_map/ffn_backward/pallas_call | solution.py:120
  338.8 7.6 %attn_backward.4 = (bf16[512,192]{1,0:T(8,128)(2,1)S(1)}, f32[512,384]{1,0:T(8,128)S(1)}, f32[512,384]{1,0:T(8,128)S(1)}, f32[4,24,768]{2,1,0:T(8,128)S(1)}, bf1...) custom-call(s32[8,128]{1,0:T(8,128)S(1)} %add_convert_fusion.refs_0_, bf16[512,1152]{1,0:T(8,128)(2,1)S(1)} %copy-done.55, ...), custom_call_target="tpu_custom_call" | custom-call | flops 2013265920 | bytes 5279744 | tf_op jit(solution)/shard_map/attn_backward/pallas_call | solution.py:120
  362.8 6.6 %collective-permute-done.68 = bf16[2,200,768]{2,1,0:T(8,128)(2,1)S(1)} collective-permute-done((bf16[2,200,768]{2,1,0:T(8,128)(2,1)S(1)}, bf16[2,200,768]{2,1,0:T(8,128)(2,1)S(1)}, u32[]{:S(2)}, u32[]{:S(2)}) %collective-permute-start.68) | collective-permute-done | bytes 614432 | tf_op jit(solution)/shard_map/ppermute | solution.py:810
  384.7 6.8 %collective-permute-done.69.refs_2_ = bf16[200,768]{1,0:T(8,128)(2,1)S(1)} collective-permute-done((bf16[200,768]{1,0:T(8,128)(2,1)S(1)}, bf16[200,768]{1,0:T(8,128)(2,1)S(1)}, u32[]{:S(2)}, u32[]{:S(2)}) %collective-permute-start.69) | collective-permute-done | bytes 307232 | tf_op jit(solution)/shard_map/ppermute | solution.py:810
  392.6 7.0 %attn_backward.5 = (bf16[512,192]{1,0:T(8,128)(2,1)S(1)}, f32[512,384]{1,0:T(8,128)S(1)}, f32[512,384]{1,0:T(8,128)S(1)}, f32[4,24,768]{2,1,0:T(8,128)S(1)}, bf1...) custom-call(s32[8,128]{1,0:T(8,128)S(1)} %add_convert_fusion.refs_0_, bf16[512,1152]{1,0:T(8,128)(2,1)S(1)} %copy-done.53, ...), custom_call_target="tpu_custom_call" | custom-call | flops 2013265920 | bytes 4493312 | tf_op jit(solution)/shard_map/attn_backward/pallas_call | solution.py:120
  414.1 19.7 %collective-permute-done.79 = bf16[2,5,24,768]{3,2,1,0:T(8,128)(2,1)S(1)} collective-permute-done((bf16[2,5,24,768]{3,2,1,0:T(8,128)(2,1)S(1)}, bf16[2,5,24,768]{3,2,1,0:T(8,128)(2,1)S(1)}, u32[]{:S(2)}, u32[]{:S(2)}) %collective-permute-start.79) | collective-permute-done | bytes 368672 | tf_op jit(solution)/shard_map/ppermute | solution.py:810
  437.0 8.4 %collective-permute-done.81.refs_2_ = bf16[5,24,768]{2,1,0:T(8,128)(2,1)S(1)} collective-permute-done((bf16[5,24,768]{2,1,0:T(8,128)(2,1)S(1)}, bf16[5,24,768]{2,1,0:T(8,128)(2,1)S(1)}, u32[]{:S(2)}, u32[]{:S(2)}) %collective-permute-start.81) | collective-permute-done | bytes 184352 | tf_op jit(solution)/shard_map/ppermute | solution.py:810
  456.1 10.7 %all-to-all-done.2.refs_0_ = bf16[4,24,3712]{2,1,0:T(8,128)(2,1)S(1)} async-done(((bf16[4,24,3712]{2,1,0:T(8,128)(2,1)}), bf16[4,24,3712]{2,1,0:T(8,128)(2,1)S(1)}, u32[]{:S(2)}, u32[]{:S(2)}) %all-to-all-start.2) | async-done | bytes 712736 | tf_op jit(solution)/shard_map/all_to_all | solution.py:932
  (431 shorter events, 259.9 us)
Async XLA Ops:
  9.9 30.8 %collective-permute-start = (bf16[392,768]{1,0:T(8,128)(2,1)S(1)}, bf16[392,768]{1,0:T(8,128)(2,1)S(1)}, u32[]{:S(2)}, u32[]{:S(2)}) collective-permute-start(bf16[392,768]{1,0:T(8,128)(2,1)S(1)} %pad_maximum_fusion.1), channel_id=1, source_target_pairs={{0,0},{1,8},{2,16},{3,24},{4,4},{5,12},{6,20},{7,28},{8,2},{9,10},... | collective-permute-start | bytes 1806344 | tf_op jit(solution)/shard_map/ppermute | solution.py:909
  12.4 23.3 %all-to-all-start = ((bf16[4,24,768]{2,1,0:T(8,128)(2,1)}), bf16[4,24,768]{2,1,0:T(8,128)(2,1)S(1)}, u32[]{:S(2)}, u32[]{:S(2)}) async-start(bf16[4,24,768]{2,1,0:T(8,128)(2,1)} %pad_maximum_fusion.5), calls=%async_computation | async-start | bytes 294912 | tf_op jit(solution)/shard_map/all_to_all | solution.py:932
  21.5 19.3 %collective-permute-start.1 = (bf16[72,768]{1,0:T(8,128)(2,1)S(1)}, bf16[72,768]{1,0:T(8,128)(2,1)S(1)}, u32[]{:S(2)}, u32[]{:S(2)}) collective-permute-start(bf16[72,768]{1,0:T(8,128)(2,1)S(1)} %pad_maximum_fusion.6), channel_id=1, source_target_pairs={{0,0},{2,8},{4,16},{6,24},{8,2},{10,10},{12,18},{14,26},{16,4},{18... | collective-permute-start | bytes 331784 | tf_op jit(solution)/shard_map/ppermute | solution.py:935
  40.7 70.6 %all-gather.5.cloned.1.call-start = ((), (), s32[]{:S(2)}) async-start(), calls=%async_computation.7 | async-start | bytes 2580480 | tf_op jit(solution)/shard_map/all_gather | solution.py:983
  40.8 21.3 %collective-permute-start.5 = (bf16[136,768]{1,0:T(8,128)(2,1)S(1)}, bf16[136,768]{1,0:T(8,128)(2,1)S(1)}, u32[]{:S(2)}, u32[]{:S(2)}) collective-permute-start(bf16[136,768]{1,0:T(8,128)(2,1)S(1)} %slice.136), channel_id=1, source_target_pairs={{0,6},{2,4},{4,2},{6,0},{1,7},{3,5},{5,3},{7,1},{8,14},{10,12},{12... | collective-permute-start | bytes 626696 | tf_op jit(solution)/shard_map/ppermute | solution.py:805
  43.8 18.3 %collective-permute-start.4 = (bf16[136,768]{1,0:T(8,128)(2,1)S(1)}, bf16[136,768]{1,0:T(8,128)(2,1)S(1)}, u32[]{:S(2)}, u32[]{:S(2)}) collective-permute-start(bf16[136,768]{1,0:T(8,128)(2,1)S(1)} %slice.136), channel_id=1, source_target_pairs={{0,4},{2,6},{4,0},{6,2},{1,5},{3,7},{5,1},{7,3},{8,12},{10,14},{12... | collective-permute-start | bytes 626696 | tf_op jit(solution)/shard_map/ppermute | solution.py:805
  63.7 100.5 %all-gather.7.cloned.1.call-start = ((), (), s32[]{:S(2)}) async-start(), calls=%async_computation.8 | async-start | bytes 2211840 | tf_op jit(solution)/shard_map/all_gather | solution.py:986
  114.2 293.7 %reduce-scatter.3.cloned.1.call-start = ((), (), s32[]{:S(2)}) async-start(), calls=%async_computation.5 | async-start | bytes 2457600 | tf_op jit(solution)/shard_map/reduce_scatter | solution.py:1134
  142.6 19.3 %collective-permute-start.22 = (bf16[256,768]{1,0:T(8,128)(2,1)S(1)}, bf16[256,768]{1,0:T(8,128)(2,1)S(1)}, u32[]{:S(2)}, u32[]{:S(2)}) collective-permute-start(bf16[256,768]{1,0:T(8,128)(2,1)S(1)} %get-tuple-element.307), channel_id=1, source_target_pairs={{0,4},{2,6},{4,0},{6,2},{1,5},{3,7},{5,1},{7,3},{8,12},{10,14},{12... | collective-permute-start | bytes 1179656 | tf_op jit(solution)/shard_map/ppermute | solution.py:805
  165.7 19.6 %collective-permute-start.25 = (bf16[256,768]{1,0:T(8,128)(2,1)}, bf16[256,768]{1,0:T(8,128)(2,1)S(1)}, u32[]{:S(2)}, u32[]{:S(2)}) collective-permute-start(bf16[256,768]{1,0:T(8,128)(2,1)} %copy-done.13), channel_id=1, source_target_pairs={{0,4},{2,6},{4,0},{6,2},{1,5},{3,7},{5,1},{7,3},{8,12},{10,14},{12... | collective-permute-start | bytes 1179656 | tf_op jit(solution)/shard_map/ppermute | solution.py:805
  167.1 18.2 %collective-permute-start.24 = (bf16[256,768]{1,0:T(8,128)(2,1)}, bf16[256,768]{1,0:T(8,128)(2,1)S(1)}, u32[]{:S(2)}, u32[]{:S(2)}) collective-permute-start(bf16[256,768]{1,0:T(8,128)(2,1)} %copy-done.13), channel_id=1, source_target_pairs={{0,2},{2,0},{4,6},{6,4},{1,3},{3,1},{5,7},{7,5},{8,10},{10,8},{12,... | collective-permute-start | bytes 1179656 | tf_op jit(solution)/shard_map/ppermute | solution.py:805
  285.9 20.5 %collective-permute-start.54 = (bf16[4,4,24,704]{3,2,1,0:T(8,128)(2,1)S(1)}, bf16[4,4,24,704]{3,2,1,0:T(8,128)(2,1)S(1)}, u32[]{:S(2)}, u32[]{:S(2)}) collective-permute-start(bf16[4,4,24,704]{3,2,1,0:T(8,128)(2,1)S(1)} %get-tuple-element.377), channel_id=1, source_target_pairs={{0,1},{1,0},{2,3},{3,2},{4,5},{5,4},{6,7},{7,6},{8,9},{9,8},{10,11... | collective-permute-start | bytes 1622024 | tf_op jit(solution)/shard_map/ppermute | solution.py:814
  286.9 19.5 %collective-permute-start.52 = (bf16[256,768]{1,0:T(8,128)(2,1)S(1)}, bf16[256,768]{1,0:T(8,128)(2,1)S(1)}, u32[]{:S(2)}, u32[]{:S(2)}) collective-permute-start(bf16[256,768]{1,0:T(8,128)(2,1)S(1)} %get-tuple-element.374), channel_id=1, source_target_pairs={{0,4},{2,6},{4,0},{6,2},{1,5},{3,7},{5,1},{7,3},{8,12},{10,14},{12... | collective-permute-start | bytes 1179656 | tf_op jit(solution)/shard_map/ppermute | solution.py:805
  309.5 18.5 %collective-permute-start.57 = (bf16[256,768]{1,0:T(8,128)(2,1)}, bf16[256,768]{1,0:T(8,128)(2,1)}, u32[]{:S(2)}, u32[]{:S(2)}) collective-permute-start(bf16[256,768]{1,0:T(8,128)(2,1)} %get-tuple-element.392.refs_1_.refs_4_), channel_id=1, source_target_pairs={{0,4},{2,6},{4,0},{6,2},{1,5},{3,7},{5,1},{7,3},{8,12},{10,14},{12... | collective-permute-start | bytes 1179656 | tf_op jit(solution)/shard_map/ppermute | solution.py:805
  313.2 132.3 %reduce-scatter.5.cloned.1.call-start = ((), (), s32[]{:S(2)}) async-start(), calls=%async_computation.6 | async-start | bytes 921600 | tf_op jit(solution)/shard_map/reduce_scatter | solution.py:1134
  347.6 21.8 %collective-permute-start.68 = (bf16[2,200,768]{2,1,0:T(8,128)(2,1)S(1)}, bf16[2,200,768]{2,1,0:T(8,128)(2,1)S(1)}, u32[]{:S(2)}, u32[]{:S(2)}) collective-permute-start(bf16[2,200,768]{2,1,0:T(8,128)(2,1)S(1)} %get-tuple-element.426), channel_id=1, source_target_pairs={{0,8},{8,0},{16,24},{24,16},{1,9},{9,1},{17,25},{25,17},{2,10},{10... | collective-permute-start | bytes 1843208 | tf_op jit(solution)/shard_map/ppermute | solution.py:810
  349.4 20.2 %collective-permute-start.70 = (f32[512,384]{1,0:T(8,128)S(1)}, f32[512,384]{1,0:T(8,128)S(1)}, u32[]{:S(2)}, u32[]{:S(2)}) collective-permute-start(f32[512,384]{1,0:T(8,128)S(1)} %get-tuple-element.436), channel_id=1, source_target_pairs={{0,1},{1,0},{2,3},{3,2},{4,5},{5,4},{6,7},{7,6},{8,9},{9,8},{10,11... | collective-permute-start | bytes 2359304 | tf_op jit(solution)/shard_map/ppermute | solution.py:814
  372.1 19.3 %collective-permute-start.71 = (bf16[4,4,24,704]{3,2,1,0:T(8,128)(2,1)S(1)}, bf16[4,4,24,704]{3,2,1,0:T(8,128)(2,1)S(1)}, u32[]{:S(2)}, u32[]{:S(2)}) collective-permute-start(bf16[4,4,24,704]{3,2,1,0:T(8,128)(2,1)S(1)} %get-tuple-element.442), channel_id=1, source_target_pairs={{0,1},{1,0},{2,3},{3,2},{4,5},{5,4},{6,7},{7,6},{8,9},{9,8},{10,11... | collective-permute-start | bytes 1622024 | tf_op jit(solution)/shard_map/ppermute | solution.py:814
  407.9 26.7 %collective-permute-start.74 = (bf16[256,768]{1,0:T(8,128)(2,1)}, bf16[256,768]{1,0:T(8,128)(2,1)S(1)}, u32[]{:S(2)}, u32[]{:S(2)}) collective-permute-start(bf16[256,768]{1,0:T(8,128)(2,1)} %copy-done.35), channel_id=1, source_target_pairs={{0,2},{2,0},{4,6},{6,4},{1,3},{3,1},{5,7},{7,5},{8,10},{10,8},{12,... | collective-permute-start | bytes 1179656 | tf_op jit(solution)/shard_map/ppermute | solution.py:805
  408.5 26.1 %collective-permute-start.75 = (bf16[256,768]{1,0:T(8,128)(2,1)}, bf16[256,768]{1,0:T(8,128)(2,1)S(1)}, u32[]{:S(2)}, u32[]{:S(2)}) collective-permute-start(bf16[256,768]{1,0:T(8,128)(2,1)} %copy-done.34), channel_id=1, source_target_pairs={{0,4},{2,6},{4,0},{6,2},{1,5},{3,7},{5,1},{7,3},{8,12},{10,14},{12... | collective-permute-start | bytes 1179656 | tf_op jit(solution)/shard_map/ppermute | solution.py:805
  409.1 25.5 %collective-permute-start.76 = (bf16[256,768]{1,0:T(8,128)(2,1)}, bf16[256,768]{1,0:T(8,128)(2,1)S(1)}, u32[]{:S(2)}, u32[]{:S(2)}) collective-permute-start(bf16[256,768]{1,0:T(8,128)(2,1)} %copy-done.33), channel_id=1, source_target_pairs={{0,6},{2,4},{4,2},{6,0},{1,7},{3,5},{5,3},{7,1},{8,14},{10,12},{12... | collective-permute-start | bytes 1179656 | tf_op jit(solution)/shard_map/ppermute | solution.py:805
  412.6 21.2 %collective-permute-start.79 = (bf16[2,5,24,768]{3,2,1,0:T(8,128)(2,1)S(1)}, bf16[2,5,24,768]{3,2,1,0:T(8,128)(2,1)S(1)}, u32[]{:S(2)}, u32[]{:S(2)}) collective-permute-start(bf16[2,5,24,768]{3,2,1,0:T(8,128)(2,1)S(1)} %get-tuple-element.467), channel_id=1, source_target_pairs={{0,8},{8,0},{16,24},{24,16},{1,9},{9,1},{17,25},{25,17},{2,10},{10... | collective-permute-start | bytes 1105928 | tf_op jit(solution)/shard_map/ppermute | solution.py:810
  434.9 19.5 %collective-permute-start.80 = (bf16[384,768]{1,0:T(8,128)(2,1)S(1)}, bf16[384,768]{1,0:T(8,128)(2,1)S(1)}, u32[]{:S(2)}, u32[]{:S(2)}) collective-permute-start(bf16[384,768]{1,0:T(8,128)(2,1)S(1)} %get-tuple-element.477), channel_id=1, source_target_pairs={{0,0},{8,1},{16,2},{24,3},{4,4},{12,5},{20,6},{28,7},{2,8},{10,9},... | collective-permute-start | bytes 1769480 | tf_op jit(solution)/shard_map/ppermute | solution.py:1137
  447.7 19.2 %all-to-all-start.2 = ((bf16[4,24,3712]{2,1,0:T(8,128)(2,1)}), bf16[4,24,3712]{2,1,0:T(8,128)(2,1)S(1)}, u32[]{:S(2)}, u32[]{:S(2)}) async-start(bf16[4,24,3712]{2,1,0:T(8,128)(2,1)} %concatenate.63), calls=%async_computation.4 | async-start | bytes 1425408 | tf_op jit(solution)/shard_map/all_to_all | solution.py:932
  (149 other events, 1231.6 us)
Sparse Core Ops, SparseCore 0:
  63.8 46.0 all-gather.4
  114.3 42.9 all-gather.6
  313.3 46.5 reduce-scatter.2
  408.0 27.5 reduce-scatter.4

commit v5 on v4

--- a/solution.py
+++ b/solution.py
@@ -448,12 +448,11 @@
         total = base_ref[...] + own_ref[...]
         for ref in refs[4:7]:
             total = total + ref[at : at + BLOCK].astype(F32)
-        refs[8][at : at + BLOCK] = total.astype(BF16)
-    refs[8][2 * BLOCK :] = refs[7][...]
+        refs[7][at : at + BLOCK] = total.astype(BF16)
 
 
 def both_totals(chain, parts):
-    shape = (3 * BLOCK, parts[0].shape[1])
+    shape = (2 * BLOCK, parts[0].shape[1])
     (out,) = call(
         chain, both_totals_kernel, "sum_both", list(parts), [jax.ShapeDtypeStruct(shape, BF16)]
     )
@@ -671,22 +670,38 @@
     out_ref[...] = total.T[:8]
 
 
-def join_last_kernel(heads_out, part_ref, *refs):
-    enc_up_ref, self_ref, enc_ref, dec_up_ref, cross_ref = refs[:5]
-    lines = dict(zip("sec", refs[-3:], strict=True))
+def join_layer_kernel(heads_out, part_ref, up_ref, heads_ref, line_ref):
+    hidden = part_ref.shape[-1] - heads_out - BLOCK
+    join_up(part_ref, 0, up_ref)
+    join_heads(part_ref, hidden, heads_ref)
+    join_lines(part_ref, hidden + heads_out, line_ref)
+
+
+def join_layer(chain, parts, heads_out):
+    _, rows, _ = parts.shape
+    return call(
+        chain,
+        functools.partial(join_layer_kernel, heads_out),
+        "join_gradients",
+        [parts],
+        [
+            jax.ShapeDtypeStruct((rows, 128 * rows), F32),
+            jax.ShapeDtypeStruct((3, rows, 32 * rows), F32),
+            jax.ShapeDtypeStruct((8, rows), F32),
+        ],
+    )
+
+
+def join_last_kernel(heads_out, part_ref, cross_ref, enc_up_ref, self_ref, enc_ref, *refs):
+    lines = {"s": refs[-2], "e": refs[-1], "c": cross_ref}
     hidden = enc_up_ref.shape[1] // 4
-    wide = part_ref.shape[-1] - 2 * (hidden + heads_out + BLOCK)
     join_up(part_ref, 0, enc_up_ref)
     join_heads(part_ref, hidden, self_ref)
     join_lines(part_ref, hidden + heads_out, lines["s"])
     start = hidden + heads_out + BLOCK
     join_heads(part_ref, start, enc_ref)
     join_lines(part_ref, start + heads_out, lines["e"])
-    start += wide
-    join_up(part_ref, start, dec_up_ref)
-    join_heads(part_ref, start + hidden, cross_ref)
-    join_lines(part_ref, start + hidden + heads_out, lines["c"])
-    for ref, picks in zip(refs[5:-3], LINES, strict=True):
+    for ref, picks in zip(refs[:-2], LINES, strict=True):
         for row, (name, line) in enumerate(picks):
             ref[row : row + 1] = lines[name][line : line + 1]
 
@@ -704,7 +719,7 @@
 )
 
 
-def join_last(chain, parts, heads_out):
+def join_last(chain, parts, cross_lines, heads_out):
     _, rows, _ = parts.shape
     heads = jax.ShapeDtypeStruct((3, rows, 32 * rows), F32)
     up = jax.ShapeDtypeStruct((rows, 128 * rows), F32)
@@ -712,12 +727,11 @@
         chain,
         functools.partial(join_last_kernel, heads_out),
         "join_gradients",
-        [parts],
-        [up, heads, heads, up, heads]
-        + [jax.ShapeDtypeStruct((len(picks), rows), F32) for picks in LINES],
-        scratch=[(8, rows)] * 3,
-    )
-    return results[:5], results[5:]
+        [parts, cross_lines],
+        [up, heads, heads] + [jax.ShapeDtypeStruct((len(picks), rows), F32) for picks in LINES],
+        scratch=[(8, rows)] * 2,
+    )
+    return results[:3], results[3:]
 
 
 def place_kernel(plan, turned, mine_ref, other_ref, *out_refs):
@@ -1170,7 +1184,8 @@
     )
     sent = plane_send(spreads[1:])
     sends = [core_send(g_cross, "rows"), core_send(g_wo_cross, "out")]
-    sent, sends = tie(sent, sends)
+    decoded = home(t3_low)
+    sent, sends, decoded = tie(sent, sends, decoded)
 
     d_e2, low_e2, sums_e2 = norm_back(chain, sent, r_enc2, vectors, 12)
     d_r1, both_low, sums1 = norm_back(
@@ -1239,15 +1254,21 @@
         dec_ffn, cross = decoder[:tall], decoder[tall:]
         enc_ffn = rounded_total(chain, [enc_own, enc_near[0], enc_far])
         far_sum = z_swap(rounded_total(chain, [far_sum, near[1]]), 2)
-        homes = both_totals(chain, [d_r1e, sent[0], d_r1, spreads_self[0], *sent[1:], t3_low])
+        homes = both_totals(chain, [d_r1e, sent[0], d_r1, spreads_self[0], *sent[1:]])
+        parts = jnp.concatenate(
+            [
+                dec_ffn[: 4 * rows].reshape(4, rows, hidden),
+                cross[: 4 * rows, : heads_out + BLOCK].reshape(4, rows, heads_out + BLOCK),
+            ],
+            axis=2,
+        )
+        g_dec_up, g_cross_qkv, cross_lines = join_layer(chain, plane_turn(parts), heads_out)
         last = rounded_total(chain, [own_sum, near[0], far_sum])
         parts = jnp.concatenate(
             [
                 enc_ffn[: 4 * rows].reshape(4, rows, hidden),
                 own_self[: 4 * rows, : heads_out + BLOCK].reshape(4, rows, heads_out + BLOCK),
                 last[:4],
-                dec_ffn[: 4 * rows].reshape(4, rows, hidden),
-                cross[: 4 * rows, : heads_out + BLOCK].reshape(4, rows, heads_out + BLOCK),
             ],
             axis=2,
         )
@@ -1255,8 +1276,8 @@
         outs = jnp.concatenate([last[4], own_self[4 * rows :], cross[4 * rows :]], axis=0)
         outs = lax.ppermute(outs, ("z", "y", "x"), [(b, a) for a, b in lay.turn_moves()])
         outs = outs.astype(F32)
-        grads, small = join_last(chain, parts, heads_out)
-        g_enc_up, g_self_qkv, g_enc_qkv, g_dec_up, g_cross_qkv = grads
+        grads, small = join_last(chain, parts, cross_lines, heads_out)
+        g_enc_up, g_self_qkv, g_enc_qkv = grads
         small = [x[0] if x.shape[0] == 1 else x for x in small]
         tail = 4 * rows + rows_ff
         g_upb_enc, g_upb_dec = (x[tail, :rows_ff].astype(F32) for x in (enc_ffn, dec_ffn))
@@ -1273,7 +1294,7 @@
             parts = parts.reshape(4, rows, 2, groups, rows_ff).transpose(1, 3, 0, 2, 4)
             return parts.reshape(rows, -1).astype(F32)
 
-        homes = both_totals(chain, [d_r1e, sent[0], d_r1, spreads_self[0], *sent[1:], t3_low])
+        homes = both_totals(chain, [d_r1e, sent[0], d_r1, spreads_self[0], *sent[1:]])
         last = z_reduce(stacked(g_enc, g_wo_enc))
         enc_ffn = z_reduce(stacked(*enc_sends))
         g_dec_up, g_enc_up = up_join(dec_ffn[: 4 * rows]), up_join(enc_ffn[: 4 * rows])
@@ -1323,9 +1344,9 @@
     bias_enc, down_enc, gains_enc, shifts_enc = small[:4]
     bias_self, bias_cross, down_dec, gains_dec, shifts_dec = small[4:]
     return (
-        homes[None, 2 * BLOCK :],
+        decoded[None],
         homes[None, :BLOCK].astype(F32),
-        homes[None, BLOCK : 2 * BLOCK].astype(F32),
+        homes[None, BLOCK:].astype(F32),
         g_enc_qkv,
         g_enc_out,
         bias_enc,

time: 482 us -> 481 us (level)
  waiting for transfers between devices: 238 us -> 215 us
  starting transfers between devices: 98.9 us -> 113 us
    ppermute x22, starting transfers between devices: 3.42 us -> 11.9 us  [core_swap(): return lax.ppermute(values, 'core', [(0, 1), (1, 0)])]
    all_to_all x3 -> x4, waiting for transfers between devices: 21.4 us -> 13.6 us  [plane_turn(): lax.all_to_all(values, PLANE, split_axis=0, concat_axis=0, tiled=True)]
    ppermute x51, waiting for transfers between devices: 144 us -> 136 us  [plane_swap(): return lax.ppermute(values, PLANE, [(i, i ^ shift) for i in range(4)])]
    ppermute x6, waiting for transfers between devices: 59.5 us -> 53 us  [z_swap(): return lax.ppermute(values, 'z', [(z, z ^ shift) for z in range(groups)])]
    pallas_call x39 -> x40, Pallas kernels: 77.5 us -> 80.5 us  [call(): pl.pallas_call(body, out_shape=(*outs, jax.ShapeDtypeStruct((8, BLOCK), F...]
    all_to_all x3 -> x4, starting transfers between devices: 19.4 us -> 21 us  [plane_turn(): lax.all_to_all(values, PLANE, split_axis=0, concat_axis=0, tiled=True)]
    unnamed x166 -> x157, local copies, waits for them, and re-layouts: 26.5 us -> 25.7 us
  transfers between devices with their start and end apart: 90 -> 92, of which waited for: 47 -> 47; matrix products, arithmetic and copies ran while one was open for 3% -> 4% of each run, Pallas kernels for 10% -> 11%
where the time goes in v5:
time: 481 us; the launch traced here: 471 us
  waiting for transfers between devices  215 us (45%)
  starting transfers between devices  113 us (23%)
  Pallas kernels  80.5 us (17%)
  local copies, waits for them, and re-layouts  35.3 us (7%)
  between operations  15.3 us (3%)
  other arithmetic  11.9 us (2%)
    ppermute x51, waiting for transfers between devices, plane_swap(): return lax.ppermute(values, PLANE, [(i, i ^ shift) for i in range(4)])  136 us
    pallas_call x40, Pallas kernels, call(): pl.pallas_call(body, out_shape=(*outs, jax.ShapeDtypeStruct((8, BLOCK), F...  80.5 us
    ppermute x51, starting transfers between devices, plane_swap(): return lax.ppermute(values, PLANE, [(i, i ^ shift) for i in range(4)])  68.6 us
    ppermute x6, waiting for transfers between devices, z_swap(): return lax.ppermute(values, 'z', [(z, z ^ shift) for z in range(groups)])  53 us
    unnamed x157, local copies, waits for them, and re-layouts  25.7 us
    all_to_all x4, starting transfers between devices, plane_turn(): lax.all_to_all(values, PLANE, split_axis=0, concat_axis=0, tiled=True)  21 us
    all_to_all x4, waiting for transfers between devices, plane_turn(): lax.all_to_all(values, PLANE, split_axis=0, concat_axis=0, tiled=True)  13.6 us
    ppermute x22, waiting for transfers between devices, core_swap(): return lax.ppermute(values, 'core', [(0, 1), (1, 0)])  12.4 us
  transfers between devices with their start and end apart: 92, of which 47 were waited for; matrix products, arithmetic and copies ran while one was open for 4% of the time, Pallas kernels for 11%

profile of v5, /device:TPU:0, one launch (start us, length us, event | category | flops | bytes accessed | tf_op | source)
XLA Modules:
  0.0 471.4 jit_solution(10557597937978562916)
XLA Ops:
  12.4 9.1 %all-to-all-start = ((bf16[4,24,768]{2,1,0:T(8,128)(2,1)}), bf16[4,24,768]{2,1,0:T(8,128)(2,1)S(1)}, u32[]{:S(2)}, u32[]{:S(2)}) async-start(bf16[4,24,768]{2,1,0:T(8,128)(2,1)} %pad_maximum_fusion.6), calls=%async_computation | async-start | bytes 294912 | tf_op jit(solution)/shard_map/all_to_all | solution.py:946
  25.0 10.7 %all-to-all-done = bf16[4,24,768]{2,1,0:T(8,128)(2,1)S(1)} async-done(((bf16[4,24,768]{2,1,0:T(8,128)(2,1)}), bf16[4,24,768]{2,1,0:T(8,128)(2,1)S(1)}, u32[]{:S(2)}, u32[]{:S(2)}) %all-to-all-start) | async-done | bytes 147488 | tf_op jit(solution)/shard_map/all_to_all | solution.py:946
  43.8 6.5 %collective-permute-start.4 = (bf16[136,768]{1,0:T(8,128)(2,1)S(1)}, bf16[136,768]{1,0:T(8,128)(2,1)S(1)}, u32[]{:S(2)}, u32[]{:S(2)}) collective-permute-start(bf16[136,768]{1,0:T(8,128)(2,1)S(1)} %slice.133), channel_id=1, source_target_pairs={{0,4},{2,6},{4,0},{6,2},{1,5},{3,7},{5,1},{7,3},{8,12},{10,14},{12... | collective-permute-start | bytes 626696 | tf_op jit(solution)/shard_map/ppermute | solution.py:819
  51.8 10.3 %collective-permute-done.2 = bf16[5,24,768]{2,1,0:T(8,128)(2,1)S(1)} collective-permute-done((bf16[5,24,768]{2,1,0:T(8,128)(2,1)S(1)}, bf16[5,24,768]{2,1,0:T(8,128)(2,1)S(1)}, u32[]{:S(2)}, u32[]{:S(2)}) %collective-permute-start.2) | collective-permute-done | bytes 184352 | tf_op jit(solution)/shard_map/ppermute | solution.py:824
  64.1 7.6 %collective-permute-done.10 = bf16[2,5,24,768]{3,2,1,0:T(8,128)(2,1)S(1)} collective-permute-done((bf16[2,5,24,768]{3,2,1,0:T(8,128)(2,1)S(1)}, bf16[2,5,24,768]{3,2,1,0:T(8,128)(2,1)S(1)}, u32[]{:S(2)}, u32[]{:S(2)}) %collective-permute-start.10) | collective-permute-done | bytes 368672 | tf_op jit(solution)/shard_map/ppermute | solution.py:824
  78.0 6.4 %attn_forward.3 = (bf16[512,1152]{1,0:T(8,128)(2,1)S(1)}, f32[8,512]{1,0:T(8,128)S(1)}, f32[128,768]{1,0:T(8,128)S(1)}, bf16[128,768]{1,0:T(8,128)(2,1)S(1)}, bf...) custom-call(s32[8,128]{1,0:T(8,128)S(1)} %add_convert_fusion.refs_0_, ...), custom_call_target="tpu_custom_call" | custom-call | flops 805306368 | bytes 3461120 | tf_op jit(solution)/shard_map/attn_forward/pallas_call | solution.py:120
  130.4 6.4 %attn_forward.4 = (bf16[512,1152]{1,0:T(8,128)(2,1)S(1)}, f32[8,512]{1,0:T(8,128)S(1)}, f32[128,768]{1,0:T(8,128)S(1)}, bf16[128,768]{1,0:T(8,128)(2,1)S(1)}, bf...) custom-call(s32[8,128]{1,0:T(8,128)S(1)} %add_convert_fusion.refs_0_, ...), custom_call_target="tpu_custom_call" | custom-call | flops 805306368 | bytes 3461120 | tf_op jit(solution)/shard_map/attn_forward/pallas_call | solution.py:120
  145.3 8.5 %collective-permute-done.21.refs_2_ = bf16[256,768]{1,0:T(8,128)(2,1)S(1)} collective-permute-done((bf16[256,768]{1,0:T(8,128)(2,1)S(1)}, bf16[256,768]{1,0:T(8,128)(2,1)S(1)}, u32[]{:S(2)}, u32[]{:S(2)}) %collective-permute-start.21) | collective-permute-done | bytes 393248 | tf_op jit(solution)/shard_map/ppermute | solution.py:819
  153.8 7.9 %collective-permute-done.22.refs_3_ = bf16[256,768]{1,0:T(8,128)(2,1)S(1)} collective-permute-done((bf16[256,768]{1,0:T(8,128)(2,1)S(1)}, bf16[256,768]{1,0:T(8,128)(2,1)S(1)}, u32[]{:S(2)}, u32[]{:S(2)}) %collective-permute-start.22) | collective-permute-done | bytes 393248 | tf_op jit(solution)/shard_map/ppermute | solution.py:819
  169.7 7.4 %collective-permute-done.26.refs_3_ = bf16[256,768]{1,0:T(8,128)(2,1)S(1)} collective-permute-done((bf16[256,768]{1,0:T(8,128)(2,1)}, bf16[256,768]{1,0:T(8,128)(2,1)S(1)}, u32[]{:S(2)}, u32[]{:S(2)}) %collective-permute-start.26) | collective-permute-done | bytes 393248 | tf_op jit(solution)/shard_map/ppermute | solution.py:819
  177.1 8.0 %collective-permute-done.25.refs_2_ = bf16[256,768]{1,0:T(8,128)(2,1)S(1)} collective-permute-done((bf16[256,768]{1,0:T(8,128)(2,1)}, bf16[256,768]{1,0:T(8,128)(2,1)S(1)}, u32[]{:S(2)}, u32[]{:S(2)}) %collective-permute-start.25) | collective-permute-done | bytes 393248 | tf_op jit(solution)/shard_map/ppermute | solution.py:819
  187.8 6.8 %attn_forward.5 = (bf16[512,1152]{1,0:T(8,128)(2,1)S(1)}, f32[8,512]{1,0:T(8,128)S(1)}, f32[128,768]{1,0:T(8,128)S(1)}, bf16[128,768]{1,0:T(8,128)(2,1)S(1)}, bf...) custom-call(s32[8,128]{1,0:T(8,128)S(1)} %add_convert_fusion.refs_0_, ...), custom_call_target="tpu_custom_call" | custom-call | flops 805306368 | bytes 3461120 | tf_op jit(solution)/shard_map/attn_forward/pallas_call | solution.py:120
  274.1 7.0 %attn_backward.3 = (bf16[512,192]{1,0:T(8,128)(2,1)S(1)}, f32[512,384]{1,0:T(8,128)S(1)}, f32[512,384]{1,0:T(8,128)S(1)}, f32[4,24,768]{2,1,0:T(8,128)S(1)}, bf1...) custom-call(s32[8,128]{1,0:T(8,128)S(1)} %add_convert_fusion.refs_0_, ...), custom_call_target="tpu_custom_call" | custom-call | flops 2013265920 | bytes 4493312 | tf_op jit(solution)/shard_map/attn_backward/pallas_call | solution.py:120
  290.1 8.5 %collective-permute-start.55 = (bf16[4,24,768]{2,1,0:T(8,128)(2,1)S(1)}, bf16[4,24,768]{2,1,0:T(8,128)(2,1)S(1)}, u32[]{:S(2)}, u32[]{:S(2)}) collective-permute-start(bf16[4,24,768]{2,1,0:T(8,128)(2,1)S(1)} %get-tuple-element.382), channel_id=1, source_target_pairs={{0,1},{1,0},{2,3},{3,2},{4,5},{5,4},{6,7},{7,6},{8,9},{9,8},{10,11... | collective-permute-start | bytes 442376 | tf_op jit(solution)/shard_map/ppermute | solution.py:828
  299.6 6.5 %collective-permute-done.52.refs_2_.refs_3_ = bf16[256,768]{1,0:T(8,128)(2,1)S(1)} collective-permute-done((bf16[256,768]{1,0:T(8,128)(2,1)S(1)}, bf16[256,768]{1,0:T(8,128)(2,1)S(1)}, u32[]{:S(2)}, u32[]{:S(2)}) %collective-permute-start.52) | collective-permute-done | bytes 393248 | tf_op jit(solution)/shard_map/ppermute | solution.py:819
  316.7 6.7 %collective-permute-done.59.refs_4_.refs_7_ = bf16[256,768]{1,0:T(8,128)(2,1)S(1)} collective-permute-done((bf16[256,768]{1,0:T(8,128)(2,1)}, bf16[256,768]{1,0:T(8,128)(2,1)S(1)}, u32[]{:S(2)}, u32[]{:S(2)}) %collective-permute-start.59) | collective-permute-done | bytes 393248 | tf_op jit(solution)/shard_map/ppermute | solution.py:819
  324.2 6.6 %collective-permute-done.58.refs_3_.refs_6_ = bf16[256,768]{1,0:T(8,128)(2,1)} collective-permute-done((bf16[256,768]{1,0:T(8,128)(2,1)}, bf16[256,768]{1,0:T(8,128)(2,1)}, u32[]{:S(2)}, u32[]{:S(2)}) %collective-permute-start.58) | collective-permute-done | bytes 393248 | tf_op jit(solution)/shard_map/ppermute | solution.py:819
  335.5 6.5 %ffn_backward.3 = (f32[128,768]{1,0:T(8,128)S(1)}, bf16[128,768]{1,0:T(8,128)(2,1)S(1)}, bf16[128,768]{1,0:T(8,128)(2,1)S(1)}, bf16[128,768]{1,0:T(8,128)(2,1)S(...) custom-call(bf16[512,768]{1,0:T(8,128)(2,1)S(1)} %copy-done.43, ...), custom_call_target="tpu_custom_call" | custom-call | flops 3623878656 | bytes 9271296 | tf_op jit(solution)/shard_map/ffn_backward/pallas_call | solution.py:120
  342.6 7.7 %attn_backward.4 = (bf16[512,192]{1,0:T(8,128)(2,1)S(1)}, f32[512,384]{1,0:T(8,128)S(1)}, f32[512,384]{1,0:T(8,128)S(1)}, f32[4,24,768]{2,1,0:T(8,128)S(1)}, bf1...) custom-call(s32[8,128]{1,0:T(8,128)S(1)} %add_convert_fusion.refs_0_, bf16[512,1152]{1,0:T(8,128)(2,1)S(1)} %copy-done.47, ...), custom_call_target="tpu_custom_call" | custom-call | flops 2013265920 | bytes 5279744 | tf_op jit(solution)/shard_map/attn_backward/pallas_call | solution.py:120
  367.1 5.4 %collective-permute-done.69 = bf16[2,200,768]{2,1,0:T(8,128)(2,1)S(1)} collective-permute-done((bf16[2,200,768]{2,1,0:T(8,128)(2,1)S(1)}, bf16[2,200,768]{2,1,0:T(8,128)(2,1)S(1)}, u32[]{:S(2)}, u32[]{:S(2)}) %collective-permute-start.69) | collective-permute-done | bytes 614432 | tf_op jit(solution)/shard_map/ppermute | solution.py:824
  387.6 6.8 %collective-permute-done.70.refs_2_ = bf16[200,768]{1,0:T(8,128)(2,1)S(1)} collective-permute-done((bf16[200,768]{1,0:T(8,128)(2,1)S(1)}, bf16[200,768]{1,0:T(8,128)(2,1)S(1)}, u32[]{:S(2)}, u32[]{:S(2)}) %collective-permute-start.70) | collective-permute-done | bytes 307232 | tf_op jit(solution)/shard_map/ppermute | solution.py:824
  395.5 6.9 %attn_backward.5 = (bf16[512,192]{1,0:T(8,128)(2,1)S(1)}, f32[512,384]{1,0:T(8,128)S(1)}, f32[512,384]{1,0:T(8,128)S(1)}, f32[4,24,768]{2,1,0:T(8,128)S(1)}, bf1...) custom-call(s32[8,128]{1,0:T(8,128)S(1)} %add_convert_fusion.refs_0_, bf16[512,1152]{1,0:T(8,128)(2,1)S(1)} %copy-done.45, ...), custom_call_target="tpu_custom_call" | custom-call | flops 2013265920 | bytes 4493312 | tf_op jit(solution)/shard_map/attn_backward/pallas_call | solution.py:120
  414.3 15.9 %collective-permute-done.80 = bf16[2,5,24,768]{3,2,1,0:T(8,128)(2,1)} collective-permute-done((bf16[2,5,24,768]{3,2,1,0:T(8,128)(2,1)S(1)}, bf16[2,5,24,768]{3,2,1,0:T(8,128)(2,1)}, u32[]{:S(2)}, u32[]{:S(2)}) %collective-permute-start.80) | collective-permute-done | bytes 368672 | tf_op jit(solution)/shard_map/ppermute | solution.py:824
  444.4 7.0 %collective-permute-done.82.refs_2_ = bf16[5,24,768]{2,1,0:T(8,128)(2,1)S(1)} collective-permute-done((bf16[5,24,768]{2,1,0:T(8,128)(2,1)}, bf16[5,24,768]{2,1,0:T(8,128)(2,1)S(1)}, u32[]{:S(2)}, u32[]{:S(2)}) %collective-permute-start.82) | collective-permute-done | bytes 184352 | tf_op jit(solution)/shard_map/ppermute | solution.py:824
  (428 shorter events, 269.0 us)
Async XLA Ops:
  9.9 30.8 %collective-permute-start = (bf16[392,768]{1,0:T(8,128)(2,1)S(1)}, bf16[392,768]{1,0:T(8,128)(2,1)S(1)}, u32[]{:S(2)}, u32[]{:S(2)}) collective-permute-start(bf16[392,768]{1,0:T(8,128)(2,1)S(1)} %pad_maximum_fusion.1), channel_id=1, source_target_pairs={{0,0},{1,8},{2,16},{3,24},{4,4},{5,12},{6,20},{7,28},{8,2},{9,10},... | collective-permute-start | bytes 1806344 | tf_op jit(solution)/shard_map/ppermute | solution.py:923
  12.4 23.3 %all-to-all-start = ((bf16[4,24,768]{2,1,0:T(8,128)(2,1)}), bf16[4,24,768]{2,1,0:T(8,128)(2,1)S(1)}, u32[]{:S(2)}, u32[]{:S(2)}) async-start(bf16[4,24,768]{2,1,0:T(8,128)(2,1)} %pad_maximum_fusion.6), calls=%async_computation | async-start | bytes 294912 | tf_op jit(solution)/shard_map/all_to_all | solution.py:946
  21.4 19.3 %collective-permute-start.1 = (bf16[72,768]{1,0:T(8,128)(2,1)S(1)}, bf16[72,768]{1,0:T(8,128)(2,1)S(1)}, u32[]{:S(2)}, u32[]{:S(2)}) collective-permute-start(bf16[72,768]{1,0:T(8,128)(2,1)S(1)} %pad_maximum_fusion.7), channel_id=1, source_target_pairs={{0,0},{2,8},{4,16},{6,24},{8,2},{10,10},{12,18},{14,26},{16,4},{18... | collective-permute-start | bytes 331784 | tf_op jit(solution)/shard_map/ppermute | solution.py:949
  40.7 70.6 %all-gather.5.cloned.1.call-start = ((), (), s32[]{:S(2)}) async-start(), calls=%async_computation.8 | async-start | bytes 2580480 | tf_op jit(solution)/shard_map/all_gather | solution.py:997
  40.8 21.3 %collective-permute-start.5 = (bf16[136,768]{1,0:T(8,128)(2,1)S(1)}, bf16[136,768]{1,0:T(8,128)(2,1)S(1)}, u32[]{:S(2)}, u32[]{:S(2)}) collective-permute-start(bf16[136,768]{1,0:T(8,128)(2,1)S(1)} %slice.133), channel_id=1, source_target_pairs={{0,6},{2,4},{4,2},{6,0},{1,7},{3,5},{5,3},{7,1},{8,14},{10,12},{12... | collective-permute-start | bytes 626696 | tf_op jit(solution)/shard_map/ppermute | solution.py:819
  43.8 18.3 %collective-permute-start.4 = (bf16[136,768]{1,0:T(8,128)(2,1)S(1)}, bf16[136,768]{1,0:T(8,128)(2,1)S(1)}, u32[]{:S(2)}, u32[]{:S(2)}) collective-permute-start(bf16[136,768]{1,0:T(8,128)(2,1)S(1)} %slice.133), channel_id=1, source_target_pairs={{0,4},{2,6},{4,0},{6,2},{1,5},{3,7},{5,1},{7,3},{8,12},{10,14},{12... | collective-permute-start | bytes 626696 | tf_op jit(solution)/shard_map/ppermute | solution.py:819
  63.7 100.3 %all-gather.7.cloned.1.call-start = ((), (), s32[]{:S(2)}) async-start(), calls=%async_computation.9 | async-start | bytes 2211840 | tf_op jit(solution)/shard_map/all_gather | solution.py:1000
  114.2 298.9 %reduce-scatter.3.cloned.1.call-start = ((), (), s32[]{:S(2)}) async-start(), calls=%async_computation.6 | async-start | bytes 2457600 | tf_op jit(solution)/shard_map/reduce_scatter | solution.py:1148
  142.4 19.3 %collective-permute-start.22 = (bf16[256,768]{1,0:T(8,128)(2,1)S(1)}, bf16[256,768]{1,0:T(8,128)(2,1)S(1)}, u32[]{:S(2)}, u32[]{:S(2)}) collective-permute-start(bf16[256,768]{1,0:T(8,128)(2,1)S(1)} %get-tuple-element.310), channel_id=1, source_target_pairs={{0,4},{2,6},{4,0},{6,2},{1,5},{3,7},{5,1},{7,3},{8,12},{10,14},{12... | collective-permute-start | bytes 1179656 | tf_op jit(solution)/shard_map/ppermute | solution.py:819
  143.8 17.9 %collective-permute-start.23 = (bf16[256,768]{1,0:T(8,128)(2,1)S(1)}, bf16[256,768]{1,0:T(8,128)(2,1)S(1)}, u32[]{:S(2)}, u32[]{:S(2)}) collective-permute-start(bf16[256,768]{1,0:T(8,128)(2,1)S(1)} %get-tuple-element.311), channel_id=1, source_target_pairs={{0,6},{2,4},{4,2},{6,0},{1,7},{3,5},{5,3},{7,1},{8,14},{10,12},{12... | collective-permute-start | bytes 1179656 | tf_op jit(solution)/shard_map/ppermute | solution.py:819
  165.5 19.6 %collective-permute-start.25 = (bf16[256,768]{1,0:T(8,128)(2,1)}, bf16[256,768]{1,0:T(8,128)(2,1)S(1)}, u32[]{:S(2)}, u32[]{:S(2)}) collective-permute-start(bf16[256,768]{1,0:T(8,128)(2,1)} %copy-done.11), channel_id=1, source_target_pairs={{0,4},{2,6},{4,0},{6,2},{1,5},{3,7},{5,1},{7,3},{8,12},{10,14},{12... | collective-permute-start | bytes 1179656 | tf_op jit(solution)/shard_map/ppermute | solution.py:819
  166.9 18.2 %collective-permute-start.24 = (bf16[256,768]{1,0:T(8,128)(2,1)}, bf16[256,768]{1,0:T(8,128)(2,1)S(1)}, u32[]{:S(2)}, u32[]{:S(2)}) collective-permute-start(bf16[256,768]{1,0:T(8,128)(2,1)} %copy-done.11), channel_id=1, source_target_pairs={{0,2},{2,0},{4,6},{6,4},{1,3},{3,1},{5,7},{7,5},{8,10},{10,8},{12,... | collective-permute-start | bytes 1179656 | tf_op jit(solution)/shard_map/ppermute | solution.py:819
  285.7 22.4 %collective-permute-start.54 = (bf16[4,4,24,704]{3,2,1,0:T(8,128)(2,1)S(1)}, bf16[4,4,24,704]{3,2,1,0:T(8,128)(2,1)S(1)}, u32[]{:S(2)}, u32[]{:S(2)}) collective-permute-start(bf16[4,4,24,704]{3,2,1,0:T(8,128)(2,1)S(1)} %get-tuple-element.380), channel_id=1, source_target_pairs={{0,1},{1,0},{2,3},{3,2},{4,5},{5,4},{6,7},{7,6},{8,9},{9,8},{10,11... | collective-permute-start | bytes 1622024 | tf_op jit(solution)/shard_map/ppermute | solution.py:828
  286.6 19.5 %collective-permute-start.52 = (bf16[256,768]{1,0:T(8,128)(2,1)S(1)}, bf16[256,768]{1,0:T(8,128)(2,1)S(1)}, u32[]{:S(2)}, u32[]{:S(2)}) collective-permute-start(bf16[256,768]{1,0:T(8,128)(2,1)S(1)} %get-tuple-element.377), channel_id=1, source_target_pairs={{0,4},{2,6},{4,0},{6,2},{1,5},{3,7},{5,1},{7,3},{8,12},{10,14},{12... | collective-permute-start | bytes 1179656 | tf_op jit(solution)/shard_map/ppermute | solution.py:819
  288.0 20.1 %collective-permute-start.53 = (bf16[256,768]{1,0:T(8,128)(2,1)S(1)}, bf16[256,768]{1,0:T(8,128)(2,1)S(1)}, u32[]{:S(2)}, u32[]{:S(2)}) collective-permute-start(bf16[256,768]{1,0:T(8,128)(2,1)S(1)} %get-tuple-element.378), channel_id=1, source_target_pairs={{0,6},{2,4},{4,2},{6,0},{1,7},{3,5},{5,3},{7,1},{8,14},{10,12},{12... | collective-permute-start | bytes 1179656 | tf_op jit(solution)/shard_map/ppermute | solution.py:819
  313.2 17.6 %collective-permute-start.58 = (bf16[256,768]{1,0:T(8,128)(2,1)}, bf16[256,768]{1,0:T(8,128)(2,1)}, u32[]{:S(2)}, u32[]{:S(2)}) collective-permute-start(bf16[256,768]{1,0:T(8,128)(2,1)} %get-tuple-element.397.refs_1_.refs_4_), channel_id=1, source_target_pairs={{0,4},{2,6},{4,0},{6,2},{1,5},{3,7},{5,1},{7,3},{8,12},{10,14},{12... | collective-permute-start | bytes 1179656 | tf_op jit(solution)/shard_map/ppermute | solution.py:819
  316.3 135.2 %reduce-scatter.5.cloned.1.call-start = ((), (), s32[]{:S(2)}) async-start(), calls=%async_computation.7 | async-start | bytes 921600 | tf_op jit(solution)/shard_map/reduce_scatter | solution.py:1148
  350.6 21.8 %collective-permute-start.69 = (bf16[2,200,768]{2,1,0:T(8,128)(2,1)S(1)}, bf16[2,200,768]{2,1,0:T(8,128)(2,1)S(1)}, u32[]{:S(2)}, u32[]{:S(2)}) collective-permute-start(bf16[2,200,768]{2,1,0:T(8,128)(2,1)S(1)} %get-tuple-element.431), channel_id=1, source_target_pairs={{0,8},{8,0},{16,24},{24,16},{1,9},{9,1},{17,25},{25,17},{2,10},{10... | collective-permute-start | bytes 1843208 | tf_op jit(solution)/shard_map/ppermute | solution.py:824
  354.3 18.2 %collective-permute-start.71 = (f32[512,384]{1,0:T(8,128)S(1)}, f32[512,384]{1,0:T(8,128)S(1)}, u32[]{:S(2)}, u32[]{:S(2)}) collective-permute-start(f32[512,384]{1,0:T(8,128)S(1)} %get-tuple-element.441), channel_id=1, source_target_pairs={{0,1},{1,0},{2,3},{3,2},{4,5},{5,4},{6,7},{7,6},{8,9},{9,8},{10,11... | collective-permute-start | bytes 2359304 | tf_op jit(solution)/shard_map/ppermute | solution.py:828
  375.1 19.3 %collective-permute-start.72 = (bf16[4,4,24,704]{3,2,1,0:T(8,128)(2,1)S(1)}, bf16[4,4,24,704]{3,2,1,0:T(8,128)(2,1)S(1)}, u32[]{:S(2)}, u32[]{:S(2)}) collective-permute-start(bf16[4,4,24,704]{3,2,1,0:T(8,128)(2,1)S(1)} %get-tuple-element.447), channel_id=1, source_target_pairs={{0,1},{1,0},{2,3},{3,2},{4,5},{5,4},{6,7},{7,6},{8,9},{9,8},{10,11... | collective-permute-start | bytes 1622024 | tf_op jit(solution)/shard_map/ppermute | solution.py:828
  408.5 30.1 %collective-permute-start.75 = (bf16[256,768]{1,0:T(8,128)(2,1)}, bf16[256,768]{1,0:T(8,128)(2,1)S(1)}, u32[]{:S(2)}, u32[]{:S(2)}) collective-permute-start(bf16[256,768]{1,0:T(8,128)(2,1)} %get-tuple-element.462), channel_id=1, source_target_pairs={{0,2},{2,0},{4,6},{6,4},{1,3},{3,1},{5,7},{7,5},{8,10},{10,8},{12,... | collective-permute-start | bytes 1179656 | tf_op jit(solution)/shard_map/ppermute | solution.py:819
  409.1 29.5 %collective-permute-start.76 = (bf16[256,768]{1,0:T(8,128)(2,1)}, bf16[256,768]{1,0:T(8,128)(2,1)S(1)}, u32[]{:S(2)}, u32[]{:S(2)}) collective-permute-start(bf16[256,768]{1,0:T(8,128)(2,1)} %get-tuple-element.463), channel_id=1, source_target_pairs={{0,4},{2,6},{4,0},{6,2},{1,5},{3,7},{5,1},{7,3},{8,12},{10,14},{12... | collective-permute-start | bytes 1179656 | tf_op jit(solution)/shard_map/ppermute | solution.py:819
  409.6 29.0 %collective-permute-start.77 = (bf16[256,768]{1,0:T(8,128)(2,1)}, bf16[256,768]{1,0:T(8,128)(2,1)}, u32[]{:S(2)}, u32[]{:S(2)}) collective-permute-start(bf16[256,768]{1,0:T(8,128)(2,1)} %get-tuple-element.464), channel_id=1, source_target_pairs={{0,6},{2,4},{4,2},{6,0},{1,7},{3,5},{5,3},{7,1},{8,14},{10,12},{12... | collective-permute-start | bytes 1179656 | tf_op jit(solution)/shard_map/ppermute | solution.py:819
  440.6 17.8 %collective-permute-start.81 = (bf16[256,768]{1,0:T(8,128)(2,1)}, bf16[256,768]{1,0:T(8,128)(2,1)S(1)}, u32[]{:S(2)}, u32[]{:S(2)}) collective-permute-start(bf16[256,768]{1,0:T(8,128)(2,1)} %get-tuple-element.481), channel_id=1, source_target_pairs={{0,0},{8,1},{16,2},{24,3},{4,4},{12,5},{20,6},{28,7},{2,8},{10,9},... | collective-permute-start | bytes 1179656 | tf_op jit(solution)/shard_map/ppermute | solution.py:1151
  (146 other events, 1182.3 us)
Sparse Core Ops, SparseCore 0:
  63.8 46.0 all-gather.4
  114.3 42.9 all-gather.6
  316.4 44.9 reduce-scatter.2
  413.2 23.5 reduce-scatter.4
